TPU v7x, 256 devices: a whole 4x4x8 slice. The times are simulated.
256 devices in a mesh: src: 8 (over z_hi, y), tile: 32 (over z_lo, x, core).
Axes of the slice: x: 4, y: 4, z: 8 (z_hi: 2, z_lo: 4; z = z_hi * 4 + z_lo), core: 2. Of those that a mesh axis runs over, the one named last changes fastest.
Arguments:
- mask_tiles: bfloat16 [32, 1024, 1024], P('tile'), may hold values from -6 to 6
- slot_pos: int32 [32], replicated, may hold values from 0 to 31, as said below
- src_shift: int32 [16, 2], P('src'), may hold values from -32 to 32
- src_weight: int32 [16], P('src'), may hold values from 1 to 8
- pupil_phase: float32 [128, 128], replicated, may hold values from -3.140625 to 3.140625
- target: bfloat16 [32, 1024, 1024], P('tile'), may hold values from 0 to 1
Outputs:
- resist: float32 [32, 1024, 1024], P('tile', 'src')
- mask_step: float32 [32, 1024, 1024], P('tile', 'src')
Inputs may be any that keep to these rules, and one draw needn't show every extreme that they name: slot_pos is a permutation of the strip positions.
All inputs are finite; a program needn't handle non-finite values.
Results may differ from a plain program's by a relative error of at most 0.0051.
Values may be sent and summed in bfloat16 or wider, within the bound.
No kernel may reach another device: no remote copies, remote signals or barrier semaphores. Data moves between devices by JAX's collectives and lax.ppermute only.
A program may use at most 128 MiB of HBM per device.

v0:
```python
import math

import jax
import jax.numpy as jnp
from jax import lax
from jax.sharding import PartitionSpec as P

TILE_PX = 1024
HALO = 64
FREQ = 128
PUPIL_R = 28
SRC_DEV = 2
EXT_PX = 1152


steepness = 4.0
threshold = 0.6
learn_rate = 8.0


def hdot(left, right):
    return jnp.dot(left, right, precision=lax.Precision.HIGHEST, preferred_element_type=jnp.float32)


def angle_table(positions, frequency, period):
    wrapped = jnp.mod(positions[:, None] * frequency[None, :], period)
    return wrapped.astype(jnp.float32) * (2.0 * math.pi / period)


def pupil_parts(shift_pair, pupil_phase, frequency):
    padded = jnp.pad(pupil_phase, FREQ)
    shift_a = shift_pair[0]
    shift_b = shift_pair[1]
    window = lax.dynamic_slice(padded, (FREQ + shift_a, FREQ + shift_b), (FREQ, FREQ))
    along_bins = frequency + shift_a
    across = frequency + shift_b
    inside = (
        along_bins[:, None] * along_bins[:, None] + across[None, :] * across[None, :]
        <= PUPIL_R * PUPIL_R
    )
    return (jnp.where(inside, jnp.cos(window), 0.0), jnp.where(inside, jnp.sin(window), 0.0))


def rows_grad(spectrum, row_index, is_valid, frequency, col_cos_bt, col_sin_bt):
    angles = angle_table(row_index, frequency, EXT_PX)
    valid_rows = is_valid.astype(jnp.float32)[:, None]
    row_cos = jnp.cos(angles) * valid_rows
    row_sin = jnp.sin(angles) * valid_rows
    back_re = hdot(row_cos, spectrum[0]) - hdot(row_sin, spectrum[1])
    back_im = hdot(row_sin, spectrum[0]) + hdot(row_cos, spectrum[1])
    return hdot(back_re, col_cos_bt) - hdot(back_im, col_sin_bt)


def per_device(mask_tiles, slot_pos, src_shift, src_weight, pupil_phase, target):
    tile_count = lax.axis_size("tile")
    src_count = lax.axis_size("src")
    my_slot = lax.axis_index("tile")
    my_src = lax.axis_index("src")
    row_share = TILE_PX // src_count
    sources_total = SRC_DEV * src_count
    frequency = jnp.arange(FREQ, dtype=jnp.int32) - FREQ // 2
    col_angles = angle_table(jnp.arange(TILE_PX, dtype=jnp.int32), frequency, TILE_PX)
    col_cos = jnp.cos(col_angles)
    col_sin = jnp.sin(col_angles)
    col_cos_b = col_cos.astype(jnp.bfloat16)
    col_sin_b = col_sin.astype(jnp.bfloat16)
    col_both = jnp.concatenate([col_cos_b, col_sin_b], axis=1)
    col_cos_bt = col_cos_b.astype(jnp.float32).T
    col_sin_bt = col_sin_b.astype(jnp.float32).T
    row_angles = angle_table(jnp.arange(EXT_PX, dtype=jnp.int32), frequency, EXT_PX)
    row_cos = jnp.cos(row_angles)
    row_sin = jnp.sin(row_angles)
    scale_factor = 1.0 / (FREQ / 2 * math.sqrt(EXT_PX * TILE_PX))
    slot_ids = jnp.arange(tile_count, dtype=jnp.int32)
    my_position = jnp.sum(jnp.where(slot_ids == my_slot, slot_pos, 0))
    above_slot = jnp.sum(jnp.where(slot_pos == my_position - 1, slot_ids, 0))
    below_slot = jnp.sum(jnp.where(slot_pos == my_position + 1, slot_ids, 0))
    has_above = my_position > 0
    has_below = my_position < tile_count - 1
    own_tile = mask_tiles[0]
    rim_zeros = jnp.zeros((HALO, TILE_PX), jnp.bfloat16)
    rim_pair = jnp.concatenate([own_tile[:HALO], own_tile[TILE_PX - HALO :]], axis=0)[None]
    all_rims = lax.all_gather(rim_pair, "tile", axis=0, tiled=True)
    upper_rim = lax.dynamic_index_in_dim(all_rims, above_slot, 0, keepdims=False)[HALO:]
    lower_rim = lax.dynamic_index_in_dim(all_rims, below_slot, 0, keepdims=False)[:HALO]
    upper_rim = jnp.where(has_above, upper_rim, rim_zeros)
    lower_rim = jnp.where(has_below, lower_rim, rim_zeros)
    tile_patch = jnp.concatenate([upper_rim, own_tile, lower_rim], axis=0)
    half_spec = jnp.dot(tile_patch, col_both, preferred_element_type=jnp.float32)
    half_re = half_spec[:, :FREQ]
    half_im = -half_spec[:, FREQ:]
    spec_re = hdot(row_cos.T, half_re) + hdot(row_sin.T, half_im)
    spec_im = hdot(row_cos.T, half_im) - hdot(row_sin.T, half_re)
    weights = src_weight.astype(jnp.float32) / (4.0 * sources_total)
    pupil_list = []
    stack_list = []
    for source in range(SRC_DEV):
        pupil_re, pupil_im = pupil_parts(src_shift[source], pupil_phase, frequency)
        amp_re = scale_factor * (pupil_re * spec_re - pupil_im * spec_im)
        amp_im = scale_factor * (pupil_re * spec_im + pupil_im * spec_re)
        line_re = (hdot(amp_re, col_cos.T) - hdot(amp_im, col_sin.T)).astype(jnp.bfloat16)
        line_im = (hdot(amp_re, col_sin.T) + hdot(amp_im, col_cos.T)).astype(jnp.bfloat16)
        top_half = jnp.concatenate([line_re, line_im], axis=1)
        low_half = jnp.concatenate([-line_im, line_re], axis=1)
        pupil_list.append((pupil_re, pupil_im))
        stack_list.append(jnp.concatenate([top_half, low_half], axis=0))

    def out_rows(row_count):
        positions = jnp.arange(row_count, dtype=jnp.int32) + HALO
        angles = angle_table(positions, frequency, EXT_PX)
        return jnp.concatenate([jnp.cos(angles), jnp.sin(angles)], axis=1).astype(jnp.bfloat16)

    full_table = out_rows(TILE_PX)
    kept_fields = [
        jnp.dot(full_table, line_stack, preferred_element_type=jnp.float32)
        for line_stack in stack_list
    ]

    def field_rows(source):
        return kept_fields[source]

    total_image = jnp.zeros((row_share * lax.axis_size("src"), TILE_PX), jnp.float32)
    for image_source in range(SRC_DEV):
        fields = field_rows(image_source)
        squared = fields * fields
        total_image = total_image + weights[image_source] * (
            squared[:, :TILE_PX] + squared[:, TILE_PX:]
        )
    intensity = lax.psum_scatter(total_image, "src", scatter_dimension=0, tiled=True)
    my_target = lax.dynamic_slice_in_dim(target[0], my_src * row_share, row_share, 0).astype(
        jnp.float32
    )
    resist_rows = jax.nn.sigmoid(steepness * (intensity - threshold))
    adjoint_mine = (
        2.0 * (resist_rows - my_target) * steepness * resist_rows * (1.0 - resist_rows)
    ).astype(jnp.bfloat16)
    adjoint_piece = lax.all_gather(adjoint_mine, "src", axis=0, tiled=True)
    row_count = adjoint_piece.shape[0]
    row_table = out_rows(row_count)
    adjoint_wide = jnp.concatenate([adjoint_piece, adjoint_piece], axis=1).astype(jnp.float32)
    updated = []
    for fold_source in range(SRC_DEV):
        fields = field_rows(fold_source)
        dfield = (2.0 * weights[fold_source] * adjoint_wide * fields).astype(jnp.bfloat16)
        fold_blocks = lax.dot_general(
            row_table, dfield, (((0,), (0,)), ((), ())), preferred_element_type=jnp.float32
        )
        updated.append(fold_blocks)
    totals = tuple(updated)
    grad_re = jnp.zeros((FREQ, FREQ), jnp.float32)
    grad_im = jnp.zeros((FREQ, FREQ), jnp.float32)
    for source in range(SRC_DEV):
        blocks = totals[source]
        dline_re = blocks[:FREQ, :TILE_PX] + blocks[FREQ:, TILE_PX:]
        dline_im = blocks[:FREQ, TILE_PX:] - blocks[FREQ:, :TILE_PX]
        damp_re = hdot(dline_re, col_cos) + hdot(dline_im, col_sin)
        damp_im = hdot(dline_im, col_cos) - hdot(dline_re, col_sin)
        pupil_re, pupil_im = pupil_list[source]
        grad_re = grad_re + scale_factor * (pupil_re * damp_re + pupil_im * damp_im)
        grad_im = grad_im + scale_factor * (pupil_re * damp_im - pupil_im * damp_re)
    summed = lax.psum(jnp.stack([grad_re, grad_im]), "src")
    all_spectra = lax.all_gather(summed[None], "tile", axis=0, tiled=True)
    above_spec = lax.dynamic_index_in_dim(all_spectra, above_slot, 0, keepdims=False)
    below_spec = lax.dynamic_index_in_dim(all_spectra, below_slot, 0, keepdims=False)
    row_index = my_src * row_share + jnp.arange(row_share, dtype=jnp.int32)
    all_rows = jnp.ones((row_share,), jnp.bool_)
    step_rows = rows_grad(summed, HALO + row_index, all_rows, frequency, col_cos_bt, col_sin_bt)
    step_rows = step_rows + rows_grad(
        above_spec,
        TILE_PX + HALO + row_index,
        (row_index < HALO) & has_above,
        frequency,
        col_cos_bt,
        col_sin_bt,
    )
    step_rows = step_rows + rows_grad(
        below_spec,
        row_index + HALO - TILE_PX,
        (row_index >= TILE_PX - HALO) & has_below,
        frequency,
        col_cos_bt,
        col_sin_bt,
    )
    return (resist_rows[None], (-learn_rate * step_rows)[None])


def solution(mesh):
    return jax.shard_map(
        per_device,
        mesh=mesh,
        in_specs=(P("tile", None, None), P(), P("src", None), P("src"), P(), P("tile", None, None)),
        out_specs=(P("tile", "src", None), P("tile", "src", None)),
        check_vma=False,
    )
```

profile of v0, /device:TPU:1, one launch (start us, length us, event | category | flops | bytes accessed | tf_op | source)
XLA Modules:
  0.0 561.4 jit_solution(6624075375163534336)
XLA Ops:
  7.2 1.0 slice_bitcast_fusion.1
  8.2 0.7 pad_maximum_fusion.4
  8.9 0.0 reduce-scatter.2.cloned.1.call-start
  9.0 1.3 fusion.265
  11.6 1.4 fusion.266
  16.1 1.5 fusion.374
  24.4 1.2 add_multiply_fusion.2
  25.6 1.2 add_multiply_fusion.4
  26.8 0.7 convert_multiply_fusion.2
  27.5 0.7 fusion.375
  28.2 4.6 cosine_convert_fusion
  32.8 51.2 %all-gather.8.cloned.1.call-done = bf16[4096,1024]{1,0:T(8,128)(2,1)} async-done(((bf16[128,1024]{1,0:T(8,128)(2,1)}), bf16[4096,1024]{1,0:T(8,128)(2,1)}) %all-gather.8.cloned.1.call-update) | async-done | bytes 8388624 | tf_op jit(solution)/shard_map/all_gather | solution.py:83
  84.0 1.0 fusion.130
  85.0 2.4 fusion.13
  87.4 3.3 fusion.49
  90.7 3.3 fusion.51
  94.0 3.3 convolution_subtract_fusion.10
  97.3 4.6 add_multiply_fusion.1
  101.9 2.5 fusion.116
  104.4 2.5 fusion.106
  106.9 2.5 fusion.113
  109.4 2.7 fusion.103
  112.1 2.7 fusion.378
  114.8 2.7 fusion.23
  117.5 2.7 fusion.376
  120.2 2.7 fusion.25
  123.0 4.5 fusion.379
  127.5 4.5 fusion.377
  132.0 4.6 fusion.9
  136.7 123.8 %reduce-scatter.2.cloned.1.call-done = f32[128,1024]{1,0:T(8,128)} async-done(((f32[1024,1024]{1,0:T(8,128)}), f32[128,1024]{1,0:T(8,128)}) %reduce-scatter.2.cloned.1.call-update) | async-done | bytes 524304 | tf_op jit(solution)/shard_map/reduce_scatter | solution.py:129
  260.5 2.2 fusion.69
  262.7 0.3 all-reduce.3.cloned.1.call-start
  264.2 71.2 %all-gather.6.cloned.1.call-done = bf16[1024,1024]{1,0:T(8,128)(2,1)} async-done(((bf16[128,1024]{1,0:T(8,128)(2,1)}), bf16[1024,1024]{1,0:T(8,128)(2,1)}) %all-gather.6.cloned.1.call-update) | async-done | bytes 2097168 | tf_op jit(solution)/shard_map/all_gather | solution.py:137
  335.4 5.9 %fusion.6 = f32[256,2048]{1,0:T(8,128)S(1)} fusion(f32[1024,2048]{1,0:T(8,128)} %get-tuple-element.35, f32[]{:T(128)S(6)} %mul.567, bf16[1024,1024]{1,0:T(8,128)(2,1)} %all-gather.6.cloned.1.call-done, bf16[1024,128]{1,0:T(8,128)(2,1)S(1)} %get-tuple-element.19, bf16[1024,128]{1,0:T(8,128)(2,1)S(1)} %get-tuple-element.18), kind=kOutput, calls=%fused_computation.7 | convolution fusion | flops 1089470464 | bytes 13107204 | tf_op jit(solution)/shard_map/dot_general | solution.py:145
  341.3 2.6 fusion.98
  343.9 2.6 fusion.100
  346.5 5.7 %fusion.4 = f32[256,2048]{1,0:T(8,128)S(1)} fusion(f32[1024,2048]{1,0:T(8,128)} %get-tuple-element.31, f32[]{:T(128)S(6)} %mul.578, bf16[1024,1024]{1,0:T(8,128)(2,1)S(1)} %copy-done, bf16[1024,128]{1,0:T(8,128)(2,1)S(1)} %get-tuple-element.19, bf16[1024,128]{1,0:T(8,128)(2,1)S(1)} %get-tuple-element.18), kind=kOutput, calls=%fused_computation.6 | convolution fusion | flops 1089470464 | bytes 13107204 | tf_op jit(solution)/shard_map/dot_general | solution.py:145
  352.2 2.6 fusion.96
  354.7 2.6 fusion.94
  357.3 2.6 convolution_subtract_fusion.9
  359.9 2.6 convolution_add_fusion.5
  362.5 3.0 convolution_subtract_fusion.8
  365.5 3.5 multiply_bitcast_fusion.1
  369.0 0.7 pad_maximum_fusion.5
  369.7 97.7 %all-reduce.3.cloned.1.call-done = f32[2,128,128]{2,1,0:T(8,128)} async-done(((f32[2,128,128]{2,1,0:T(8,128)}), f32[2,128,128]{2,1,0:T(8,128)}) %all-reduce.3.cloned.1.call-update) | async-done | bytes 131088 | tf_op jit(solution)/shard_map/psum | solution.py:161
  467.4 1.4 fusion.148
  468.8 1.4 fusion.146
  470.2 1.4 convolution_add_fusion.4
  471.5 1.4 convolution_subtract_fusion.7
  472.9 2.2 fusion.127
  475.1 2.3 convolution_subtract_fusion.2
  477.4 56.0 %all-gather.10.cloned.1.call-done = f32[64,128,128]{2,1,0:T(8,128)} async-done(((f32[2,128,128]{2,1,0:T(8,128)}), f32[64,128,128]{2,1,0:T(8,128)}) %all-gather.10.cloned.1.call-update) | async-done | bytes 4194320 | tf_op jit(solution)/shard_map/all_gather | solution.py:162
  533.4 1.4 fusion.157
  534.8 1.4 fusion.156
  536.2 1.4 fusion.155
  537.5 1.4 fusion.154
  538.9 1.4 convolution_add_fusion.2
  540.3 1.4 convolution_subtract_fusion.5
  541.6 2.2 fusion.123
  543.9 1.4 convolution_add_fusion.3
  545.2 1.4 convolution_subtract_fusion.6
  546.6 2.4 fusion.125
  549.1 2.3 fusion.22
  551.3 3.2 fusion.21
  (17 shorter events, 0.2 us)
Async XLA Ops:
  7.2 76.8 %all-gather.8.cloned.1.call-start = ((), (), s32[]{:S(2)}) async-start(), calls=%async_computation.4 | async-start | bytes 8650752 | tf_op jit(solution)/shard_map/all_gather | solution.py:83
  8.9 251.5 %reduce-scatter.2.cloned.1.call-start = ((), (), s32[]{:S(2)}) async-start(), calls=%async_computation.1 | async-start | bytes 4718592 | tf_op jit(solution)/shard_map/reduce_scatter | solution.py:129
  87.4 9.9 %copy-start.1 = (f32[128,128]{1,0:T(8,128)S(1)}, f32[128,128]{1,0:T(8,128)}, u32[]{:S(2)}) copy-start(f32[128,128]{1,0:T(8,128)} %param.10) | copy-start | bytes 196612
  136.6 198.8 %all-gather.6.cloned.1.call-start = ((), (), s32[]{:S(2)}) async-start(), calls=%async_computation.2 | async-start | bytes 2359296 | tf_op jit(solution)/shard_map/all_gather | solution.py:137
  262.7 204.7 %all-reduce.3.cloned.1.call-start = ((), (), s32[]{:S(2)}) async-start(), calls=%async_computation.3 | async-start | bytes 262144 | tf_op jit(solution)/shard_map/psum | solution.py:161
  341.3 5.2 copy-start
  369.7 163.8 %all-gather.10.cloned.1.call-start = ((), (), s32[]{:S(2)}) async-start(), calls=%async_computation.5 | async-start | bytes 4325376 | tf_op jit(solution)/shard_map/all_gather | solution.py:162
Sparse Core Ops, SparseCore 0:
  10.4 73.5 all-gather.7
  136.7 123.6 reduce-scatter.1
  263.7 71.7 all-gather.5
  369.8 97.5 all-reduce.2
  469.2 64.1 all-gather.9
where the time goes:
time: 572 us; the launch traced here: 561 us
  waiting for transfers between devices  400 us (70%)
  matrix products  111 us (19%)
  between operations  27 us (5%)
  other arithmetic  19.6 us (3%)
    reduce_scatter x1, waiting for transfers between devices, per_device(): lax.psum_scatter(total_image, 'src', scatter_dimension=0, tiled=True)  124 us
    psum x1, waiting for transfers between devices, per_device(): summed = lax.psum(jnp.stack([grad_re, grad_im]), 'src')  97.7 us
    dot_general x38, matrix products, hdot(): jnp.dot(left, right, precision=lax.Precision.HIGHEST, preferred_element_t...  88.3 us
    all_gather x1, waiting for transfers between devices, per_device(): adjoint_piece = lax.all_gather(adjoint_mine, 'src', axis=0, tiled=True)  71.2 us
    all_gather x1, waiting for transfers between devices, per_device(): all_spectra = lax.all_gather(summed[None], 'tile', axis=0, tiled=True)  56 us
    all_gather x1, waiting for transfers between devices, per_device(): all_rims = lax.all_gather(rim_pair, 'tile', axis=0, tiled=True)  51.2 us
    dot_general x2, matrix products, per_device(): lax.dot_general(row_table, dfield, (((0,), (0,)), ((), ())), preferred_el...  11.6 us
  transfers between devices with their start and end apart: 5, of which 5 were waited for; matrix products, arithmetic and copies ran while one was open for 4% of the time, Pallas kernels for 0%

commit v1 on v0

v1 whole, which is shorter than its diff:
```python
import math
import numpy as np, jax, jax.numpy as jnp
from jax import lax
from jax.sharding import PartitionSpec as P

HI=lax.Precision.HIGHEST
def hdot(a,b): return jnp.dot(a,b,precision=HI,preferred_element_type=jnp.float32)
k=np.arange(64)
def tab(pos,period):
    ang=2*np.pi*((pos[:,None]*k[None])%period)/period
    return np.concatenate([np.cos(ang),np.sin(ang)],1)
TC=tab(np.arange(1024),1024); TR=tab(np.arange(1152),1152)
f=np.arange(128)-64
Ec=np.zeros((128,64)); Es=np.zeros((128,64))
for i,ff in enumerate(f):
    if ff==-64: continue
    Ec[i,abs(ff)]=1; Es[i,abs(ff)]=np.sign(ff)
E=np.concatenate([Ec,Es],1)
ap=np.arange(64)-32
ang=2*np.pi*((np.arange(128)[:,None]*ap[None])%128)/128
Wr,Wi=np.cos(ang),np.sin(ang)
WX=np.concatenate([np.concatenate([Wr.T,Wi.T],1),np.concatenate([-Wi.T,Wr.T],1)],0)
WY=np.concatenate([np.concatenate([Wr,-Wi],1),np.concatenate([Wi,Wr],1)],0)
def interp(pos):
    p=np.arange(-63,64)
    d=pos[:,None]-np.arange(128)[None]
    return np.cos(2*np.pi*d[:,:,None]*p/128).sum(-1)/128
RY=interp((64+np.arange(1024))/9.0); RX=interp(np.arange(1024)/8.0)
disc=(ap[:,None]**2+ap[None]**2<=784)
scale=1.0/(64*math.sqrt(1152*1024))
sg=np.ones((128,128));
Mre=np.zeros((128,128)); Mre[:64,:64]=1; Mre[64:,64:]=-1
Mim=np.zeros((128,128)); Mim[:64,64:]=-1; Mim[64:,:64]=-1
c32=lambda a: jnp.asarray(a,jnp.float32)
def main(M,shifts,weights,phase,target):
    e=c32(E)
    sre=hdot(hdot(e,M*c32(Mre)),e.T); sim=hdot(hdot(e,M*c32(Mim)),e.T)
    ph=phase[32:96,32:96]
    pr=jnp.where(disc,jnp.cos(ph),0)*scale; pi=jnp.where(disc,jnp.sin(ph),0)*scale
    ki=jnp.arange(128)
    U=(ki[None,None,:]==(jnp.arange(64)[None,:,None]+32-shifts[:,0,None,None])).astype(jnp.float32)
    V=(ki[None,None,:]==(jnp.arange(64)[None,:,None]+32-shifts[:,1,None,None])).astype(jnp.float32)
    ein=lambda s,*a: jnp.einsum(s,*a,precision=HI,preferred_element_type=jnp.float32)
    wr=ein('sal,sbl->sab',ein('sak,kl->sal',U,sre),V); wi=ein('sal,sbl->sab',ein('sak,kl->sal',U,sim),V)
    A=jnp.concatenate([pr*wr-pi*wi,pr*wi+pi*wr],2)
    L=ein('sak,kj->saj',A,c32(WX))
    L2=jnp.concatenate([L[:,:,:128],L[:,:,128:]],1)
    g=ein('ik,skj->sij',c32(WY),L2)
    sq=g*g
    Ic=(weights[:,None,None]*(sq[:,:128]+sq[:,128:])).sum(0)
    I=hdot(hdot(c32(RY),Ic),c32(RX).T)
    r=jax.nn.sigmoid(4.0*(I-0.6))
    adj=(2.0*(r-target.astype(jnp.float32))*4.0*r*(1-r)).astype(jnp.bfloat16).astype(jnp.float32)
    Ac=hdot(hdot(c32(RY).T,adj),c32(RX))
    dg=g*(2*weights[:,None,None]*jnp.concatenate([Ac,Ac],0))
    dL2=ein('ik,sij->skj',c32(WY),dg)
    dL=jnp.concatenate([dL2[:,:64],dL2[:,64:]],2)
    dA=ein('saj,kj->sak',dL,c32(WX))
    dr,di=dA[:,:,:64],dA[:,:,64:]
    gr=pr*dr+pi*di; gi=pr*di-pi*dr
    Gr=ein('sak,sal->kl',U,ein('sab,sbl->sal',gr,V)); Gi=ein('sak,sal->kl',U,ein('sab,sbl->sal',gi,V))
    N=hdot(hdot(e.T,Gr),e)*c32(Mre)+hdot(hdot(e.T,Gi),e)*c32(Mim)
    return r,N


def per_device(mask_tiles, slot_pos, src_shift, src_weight, pupil_phase, target):
    tile_count = lax.axis_size("tile")
    src_count = lax.axis_size("src")
    my_slot = lax.axis_index("tile")
    my_src = lax.axis_index("src")
    row_share = 1024 // src_count
    slot_ids = jnp.arange(tile_count, dtype=jnp.int32)
    my_position = jnp.sum(jnp.where(slot_ids == my_slot, slot_pos, 0))
    is_above = slot_pos == my_position - 1
    is_below = slot_pos == my_position + 1
    ints = jnp.concatenate([src_shift, src_weight[:, None]], axis=1)
    step = 1
    while step < src_count:
        other = lax.ppermute(ints, "src", [(i, i ^ step) for i in range(src_count)])
        ints = jnp.concatenate([ints, other], axis=0)
        step *= 2
    weights = ints[:, 2].astype(jnp.float32) / (4.0 * ints.shape[0])
    col_table = jnp.asarray(TC, jnp.float32).astype(jnp.bfloat16)
    row_table = c32(TR)
    half = jnp.dot(mask_tiles[0], col_table, preferred_element_type=jnp.float32)
    rims = half.astype(jnp.bfloat16)
    sent = jnp.where(is_below[:, None, None], rims[None, 960:],
                     jnp.where(is_above[:, None, None], rims[None, :64], jnp.bfloat16(0)))
    got = lax.all_to_all(sent, "tile", 0, 0, tiled=True).astype(jnp.float32)
    upper = jnp.sum(jnp.where(is_above[:, None, None], got, 0.0), axis=0)
    lower = jnp.sum(jnp.where(is_below[:, None, None], got, 0.0), axis=0)
    moments = hdot(row_table.T, jnp.concatenate([upper, half, lower], axis=0))
    resist, folded = main(moments, ints[:, :2], weights, pupil_phase, target[0])
    edge_rows = jnp.where(my_src == 0, row_table[1088:], row_table[:64])
    edge_to = jnp.where(my_src == 0, is_below, is_above)
    edge = hdot(edge_rows, folded).astype(jnp.bfloat16)
    sent = jnp.where(edge_to[:, None, None], edge[None], jnp.bfloat16(0))
    got = lax.all_to_all(sent, "tile", 0, 0, tiled=True).astype(jnp.float32)
    edge_from = jnp.where(my_src == 0, is_above, is_below)
    wanted = (my_src == 0) | (my_src == src_count - 1)
    rim = jnp.sum(jnp.where((edge_from & wanted)[:, None, None], got, 0.0), axis=0)
    empty = jnp.zeros((row_share - 64, 128), jnp.float32)
    rim = jnp.where(my_src == 0, jnp.concatenate([rim, empty], axis=0), jnp.concatenate([empty, rim], axis=0))
    mine = lax.dynamic_slice_in_dim(row_table, 64 + my_src * row_share, row_share, 0)
    back = hdot(mine, folded) + rim
    step_rows = hdot(back, col_table.astype(jnp.float32).T)
    resist_rows = lax.dynamic_slice_in_dim(resist, my_src * row_share, row_share, 0)
    return (resist_rows[None], (-8.0 * step_rows)[None])


def solution(mesh):
    return jax.shard_map(
        per_device,
        mesh=mesh,
        in_specs=(P("tile", None, None), P(), P("src", None), P("src"), P(), P("tile", None, None)),
        out_specs=(P("tile", "src", None), P("tile", "src", None)),
        check_vma=False,
    )
```

time: 572 us -> 95.9 us (0.17); the launches traced: 561 us -> 95.1 us
  waiting for transfers between devices: 400 us -> 21.4 us
  matrix products: 111 us -> 33.5 us
  starting transfers between devices: 0.42 us -> 25.5 us
  between operations: 27 us -> 2.52 us
  other arithmetic: 19.6 us -> 8.76 us
    all_gather x3 -> x0, waiting for transfers between devices: 178 us -> none  [the longest x1 71.2 us: per_device(): adjoint_piece = lax.all_gather(adjoint_mine, 'src', axis=0, tiled=True)]
    reduce_scatter x1 -> x0, waiting for transfers between devices: 124 us -> none  [per_device(): lax.psum_scatter(total_image, 'src', scatter_dimension=0, tiled=True)]
    psum x1 -> x0, waiting for transfers between devices: 97.7 us -> none  [per_device(): summed = lax.psum(jnp.stack([grad_re, grad_im]), 'src')]
    dot_general x43 -> x31, matrix products: 111 us -> 33.5 us  [the longest x18 17.5 us: hdot(): return jnp.dot(a, b, precision=HI, preferred_element_type=jnp.float32)]
    all_to_all x0 -> x2, waiting for transfers between devices: none -> 16.8 us  [per_device(): got = lax.all_to_all(sent, 'tile', 0, 0, tiled=True).astype(jnp.float32)]
    all_to_all x0 -> x2, starting transfers between devices: none -> 16.3 us  [per_device(): got = lax.all_to_all(sent, 'tile', 0, 0, tiled=True).astype(jnp.float32)]
    ppermute x0 -> x3, starting transfers between devices: none -> 9.19 us  [per_device(): other = lax.ppermute(ints, 'src', [(i, i ^ step) for i in range(src_count)])]
  transfers between devices with their start and end apart: 5 -> 5, of which waited for: 5 -> 4; matrix products, arithmetic and copies ran while one was open for 4% -> 10% of each run, Pallas kernels for 0% -> 0%
where the time goes in v1:
time: 95.9 us; the launch traced here: 95.1 us
  matrix products  33.5 us (35%)
  starting transfers between devices  25.5 us (27%)
  waiting for transfers between devices  21.4 us (22%)
  other arithmetic  8.76 us (9%)
  local copies, waits for them, and re-layouts  3.48 us (4%)
  between operations  2.52 us (3%)
    dot_general x18, matrix products, hdot(): return jnp.dot(a, b, precision=HI, preferred_element_type=jnp.float32)  17.5 us
    all_to_all x2, waiting for transfers between devices, per_device(): got = lax.all_to_all(sent, 'tile', 0, 0, tiled=True).astype(jnp.float32)  16.8 us
    all_to_all x2, starting transfers between devices, per_device(): got = lax.all_to_all(sent, 'tile', 0, 0, tiled=True).astype(jnp.float32)  16.3 us
    dot_general x12, matrix products, main(): jnp.einsum(s, *a, precision=HI, preferred_element_type=jnp.float32)  14.2 us
    ppermute x3, starting transfers between devices, per_device(): other = lax.ppermute(ints, 'src', [(i, i ^ step) for i in range(src_count)])  9.19 us
    ppermute x3, waiting for transfers between devices, per_device(): other = lax.ppermute(ints, 'src', [(i, i ^ step) for i in range(src_count)])  4.64 us
  transfers between devices with their start and end apart: 5, of which 4 were waited for; matrix products, arithmetic and copies ran while one was open for 10% of the time, Pallas kernels for 0%

profile of v1, /device:TPU:1, one launch (start us, length us, event | category | flops | bytes accessed | tf_op | source)
XLA Modules:
  0.0 95.1 jit_solution(1210277917956389242)
XLA Ops:
  0.6 0.0 copy-start
  0.7 0.9 copy.43
  1.6 0.7 pad_add_fusion
  2.3 2.1 %collective-permute-start = (s32[2,3]{0,1:T(4,128)S(1)}, s32[2,3]{0,1:T(4,128)S(1)}, u32[]{:S(2)}, u32[]{:S(2)}) collective-permute-start(s32[2,3]{0,1:T(4,128)S(1)} %pad_add_fusion), channel_id=1, source_target_pairs={{0,32},{32,0},{64,96},{96,64},{128,160},{160,128},{192,224},{224,1... | collective-permute-start | bytes 80 | tf_op jit(solution)/shard_map/ppermute | solution.py:79
  4.4 1.3 %fusion.66 = s32[]{:T(128)} fusion(s32[32]{0:T(128)} %param.23, s32[]{:T(128)S(6)} %axis_index.22), kind=kLoop, calls=%fused_computation.104 | loop fusion | flops 95 | bytes 136 | tf_op jit(solution)/shard_map/reduce_sum | solution.py:73
  7.0 1.8 %fusion.5 = f32[128,1024]{1,0:T(8,128)S(1)} fusion(bf16[1024,128]{1,0:T(8,128)(2,1)} %constant.92, bf16[1,1024,1024]{2,1,0:T(8,128)(2,1)S(1)} %copy-done), kind=kOutput, calls=%fused_computation.9 | convolution fusion | flops 268435456 | bytes 2883584 | tf_op jit(solution)/shard_map/dot_general | solution.py:85
  8.8 0.1 fusion.75
  8.9 0.1 copy.44
  9.0 0.1 copy.45
  9.1 1.3 %select_and_fusion = (pred[32]{0:T(512)(128)(4,1)}, pred[32]{0:T(512)(128)(4,1)S(1)}, pred[32]{0:T(512)(128)(4,1)S(1)}) fusion(pred[]{:T(512)S(6)} %or.3, pred[]{:T(512)S(6)} %eq.66, s32[32]{0:T(128)} %param.23, s32[]{:T(128)S(6)} %sub.58, s32[]{:T(128)S(6)} %add.47), kind=kLoop, calls=%fused_computation.101 | loop fusion | flops 128 | bytes 234 | tf_op jit(solution)/shard_map/and | solution.py:101
  10.4 0.9 select_select_fusion
  11.3 9.6 %all-to-all-start = ((bf16[32,64,128]{2,1,0:T(8,128)(2,1)}), bf16[32,64,128]{2,1,0:T(8,128)(2,1)S(1)}, u32[]{:S(2)}, u32[]{:S(2)}) async-start(bf16[32,64,128]{2,1,0:T(8,128)(2,1)} %select_select_fusion), calls=%async_computation | async-start | bytes 1048576 | tf_op jit(solution)/shard_map/all_to_all | solution.py:89
  20.9 0.5 broadcast_select_fusion.1
  21.5 1.0 %select_multiply_fusion.1 = (f32[64,64]{1,0:T(8,128)S(1)}, f32[64,64]{1,0:T(8,128)S(1)}) fusion(pred[64,64]{1,0:T(32,128)(4,1)} %constant.79.clone, f32[128,128]{1,0:T(8,128)} %param.26), kind=kLoop, calls=%fused_computation.93 | loop fusion | flops 16384 | bytes 53248 | tf_op jit(solution)/shard_map/mul | solution.py:39
  22.5 0.1 pad_add_fusion.1
  22.6 2.6 %collective-permute-start.1 = (s32[4,3]{0,1:T(4,128)S(1)}, s32[4,3]{0,1:T(4,128)S(1)}, u32[]{:S(2)}, u32[]{:S(2)}) collective-permute-start(s32[4,3]{0,1:T(4,128)S(1)} %pad_add_fusion.1), channel_id=1, source_target_pairs={{0,64},{32,96},{64,0},{96,32},{128,192},{160,224},{192,128},{224,1... | collective-permute-start | bytes 152 | tf_op jit(solution)/shard_map/ppermute | solution.py:79
  25.2 1.6 %collective-permute-done.1 = s32[4,3]{0,1:T(4,128)S(1)} collective-permute-done((s32[4,3]{0,1:T(4,128)S(1)}, s32[4,3]{0,1:T(4,128)S(1)}, u32[]{:S(2)}, u32[]{:S(2)}) %collective-permute-start.1) | collective-permute-done | bytes 80 | tf_op jit(solution)/shard_map/ppermute | solution.py:79
  26.8 0.1 pad_add_fusion.2
  26.9 4.4 %collective-permute-start.2 = (s32[8,3]{0,1:T(4,128)S(1)}, s32[8,3]{0,1:T(4,128)S(1)}, u32[]{:S(2)}, u32[]{:S(2)}) collective-permute-start(s32[8,3]{0,1:T(4,128)S(1)} %pad_add_fusion.2), channel_id=1, source_target_pairs={{0,128},{32,160},{64,192},{96,224},{128,0},{160,32},{192,64},{224,... | collective-permute-start | bytes 296 | tf_op jit(solution)/shard_map/ppermute | solution.py:79
  31.3 3.0 %collective-permute-done.2 = s32[8,3]{0,1:T(4,128)S(1)} collective-permute-done((s32[8,3]{0,1:T(4,128)S(1)}, s32[8,3]{0,1:T(4,128)S(1)}, u32[]{:S(2)}, u32[]{:S(2)}) %collective-permute-start.2) | collective-permute-done | bytes 128 | tf_op jit(solution)/shard_map/ppermute | solution.py:79
  34.4 0.1 pad_add_fusion.3
  34.4 0.6 multiply_bitcast_fusion
  35.0 0.1 broadcast_subtract_fusion
  35.1 2.3 %all-to-all-done = bf16[32,64,128]{2,1,0:T(8,128)(2,1)S(1)} async-done(((bf16[32,64,128]{2,1,0:T(8,128)(2,1)}), bf16[32,64,128]{2,1,0:T(8,128)(2,1)S(1)}, u32[]{:S(2)}, u32[]{:S(2)}) %all-to-all-start) | async-done | bytes 524320 | tf_op jit(solution)/shard_map/all_to_all | solution.py:89
  37.3 0.9 fusion.14
  38.3 1.0 %fusion.76 = f32[128,128]{1,0:T(8,128)S(1)} fusion(f32[64,128]{1,0:T(8,128)S(1)} %get-tuple-element.3, f32[64,128]{1,0:T(8,128)} %constant.93), kind=kOutput, calls=%fused_computation.121 | convolution fusion | flops 12582912 | bytes 131072 | tf_op jit(solution)/shard_map/dot_general | solution.py:7
  39.4 1.7 %convolution_add_fusion.2 = f32[128,128]{1,0:T(8,128)S(1)} fusion(f32[128,128]{1,0:T(8,128)S(1)} %fusion.76, f32[128,1024]{1,0:T(8,128)S(1)} %fusion.5, f32[1024,128]{1,0:T(8,128)} %constant.94), kind=kOutput, calls=%fused_computation.27 | convolution fusion | flops 201342976 | bytes 1179648 | tf_op jit(solution)/shard_map/dot_general | solution.py:7
  41.0 1.0 %convolution_add_fusion.1 = f32[128,128]{1,0:T(8,128)S(1)} fusion(f32[128,128]{1,0:T(8,128)S(1)} %convolution_add_fusion.2, f32[64,128]{1,0:T(8,128)S(1)} %get-tuple-element.2, f32[64,128]{1,0:T(8,128)} %constant.95), kind=kOutput, calls=%fused_computation.26 | convolution fusion | flops 12599296 | bytes 196608 | tf_op jit(solution)/shard_map/dot_general | solution.py:7
  42.1 0.3 fusion.61
  42.4 0.3 fusion.59
  42.7 0.3 convolution_bitcast_fusion.2
  43.0 0.3 convolution_bitcast_fusion.3
  43.2 0.5 fusion.42
  43.7 0.5 fusion.41
  44.2 0.6 fusion.40
  44.8 0.6 multiply_subtract_fusion
  45.5 1.0 %fusion.27 = f32[16,64,256]{2,1,0:T(8,128)S(1)} fusion(f32[128,256,1]{1,0,2:T(8,128)S(1)} %copy-done.7, f32[16,64,64]{2,1,0:T(8,128)S(1)} %get-tuple-element.8, f32[16,64,64]{2,1,0:T(8,128)S(1)} %get-tuple-element.7), kind=kOutput, calls=%fused_computation.45 | convolution fusion | flops 402784256 | bytes 1703936 | tf_op jit(solution)/shard_map/sak,kj->saj/dot_general | solution.py:43
  46.5 0.1 fusion.74
  46.7 3.2 %bitcast_multiply_fusion.1 = (f32[16,256,128]{1,2,0:T(8,128)S(1)}, f32[16,128,256]{2,1,0:T(8,128)}) fusion(f32[256,128,1]{1,0,2:T(8,128)S(1)} %copy-done.8, f32[16,64,128]{2,1,0:T(8,128)S(1)} %get-tuple-element.12, f32[16,64,128]{2,1,0:T(8,128)S(1)} %get-tuple-element.11), kind=kOutput, calls=%fused_computation.7 | convolution fusion | flops 806092800 | bytes 5373952 | tf_op jit(solution)/shard_map/ik,skj->sij/dot_general | solution.py:43
  49.9 0.2 fusion.16
  50.1 0.6 fusion.77
  50.7 4.6 %add_divide_fusion = f32[1024,1024]{1,0:T(8,128)S(1)} fusion(f32[128,1024]{1,0:T(8,128)S(1)} %fusion.77, f32[1024,128]{1,0:T(8,128)S(1)} %copy-done.6), kind=kOutput, calls=%fused_computation.5 | convolution fusion | flops 1615855616 | bytes 5242880 | tf_op jit(solution)/shard_map/dot_general | solution.py:7
  55.3 2.9 %fusion.8 = f32[1024,128]{1,0:T(8,128)S(1)} fusion(f32[1024,128]{1,0:T(8,128)S(1)} %copy-done.3, f32[1024,1024]{1,0:T(8,128)S(1)} %add_divide_fusion, bf16[1,1024,1024]{2,1,0:T(8,128)(2,1)S(1)} %copy-done.4), kind=kOutput, calls=%fused_computation.12 | convolution fusion | flops 1617952768 | bytes 7340032 | tf_op jit(solution)/shard_map/dot_general | solution.py:7
  58.2 1.0 %fusion.78 = f32[128,128]{1,0:T(8,128)S(1)} fusion(f32[1024,128]{1,0:T(8,128)S(1)} %fusion.8, f32[1024,128]{1,0:T(8,128)S(1)} %copy-done.6), kind=kOutput, calls=%fused_computation.123 | convolution fusion | flops 201326592 | bytes 1114112 | tf_op jit(solution)/shard_map/dot_general | solution.py:7
  59.2 0.1 copy.47
  59.3 4.1 %fusion.10 = f32[16,128,128]{2,1,0:T(8,128)S(1)} fusion(f32[256,128,1]{1,0,2:T(8,128)S(1)} %copy-done.8, f32[16,128,256]{2,1,0:T(8,128)} %get-tuple-element.24, f32[256,128]{0,1:T(8,128)S(1)} %copy.47, f32[16]{0:T(128)S(1)} %copy-done.18), kind=kOutput, calls=%fused_computation.13 | convolution fusion | flops 806354944 | bytes 3407936 | tf_op jit(solution)/shard_map/ik,sij->skj/dot_general | solution.py:43
  63.5 0.1 fusion.73
  63.6 1.0 %fusion.21 = f32[16,64,128]{2,1,0:T(8,128)S(1)} fusion(f32[128,256,1]{1,0,2:T(8,128)S(1)} %copy-done.7, f32[16,64,128]{2,1,0:T(8,128)S(1)} %get-tuple-element.10, f32[16,64,128]{2,1,0:T(8,128)S(1)} %get-tuple-element.9), kind=kOutput, calls=%fused_computation.38 | convolution fusion | flops 402915328 | bytes 1703936 | tf_op jit(solution)/shard_map/saj,kj->sak/dot_general | solution.py:43
  64.6 0.6 fusion.35
  65.2 0.6 fusion.31
  65.8 0.7 convolution_bitcast_fusion.1
  66.6 0.7 convolution_bitcast_fusion
  67.3 0.3 fusion.80
  67.6 0.3 fusion.79
  67.9 0.3 convolution_multiply_fusion.2
  68.2 0.3 fusion.12
  68.5 0.2 convolution_convert_fusion
  68.7 0.9 broadcast_select_fusion
  69.6 6.7 %all-to-all-start.1 = ((bf16[32,64,128]{2,1,0:T(8,128)(2,1)}), bf16[32,64,128]{2,1,0:T(8,128)(2,1)S(1)}, u32[]{:S(2)}, u32[]{:S(2)}) async-start(bf16[32,64,128]{2,1,0:T(8,128)(2,1)} %broadcast_select_fusion), calls=%async_computation.1 | async-start | bytes 1048576 | tf_op jit(solution)/shard_map/all_to_all | solution.py:98
  76.3 1.9 %dynamic-slice_bitcast_fusion = f32[1,128,1024]{2,1,0:T(8,128)} fusion(f32[1024,1024]{1,0:T(8,128)} %copy-done.1, s32[]{:T(128)S(6)} %select_n.73), kind=kLoop, calls=%fused_computation.57 | loop fusion | bytes 1048580 | tf_op jit(solution)/shard_map/broadcast_in_dim | solution.py:108
  78.2 14.5 %all-to-all-done.1 = bf16[32,64,128]{2,1,0:T(8,128)(2,1)S(1)} async-done(((bf16[32,64,128]{2,1,0:T(8,128)(2,1)}), bf16[32,64,128]{2,1,0:T(8,128)(2,1)S(1)}, u32[]{:S(2)}, u32[]{:S(2)}) %all-to-all-start.1) | async-done | bytes 524320 | tf_op jit(solution)/shard_map/all_to_all | solution.py:98
  92.7 0.2 select_reduce_fusion
  92.9 1.0 %convolution_add_fusion = f32[128,128]{1,0:T(8,128)S(1)} fusion(f32[128,128]{1,0:T(8,128)S(1)} %fusion.12, f32[64,128]{1,0:T(8,128)S(1)} %select_reduce_fusion, f32[1152,128]{1,0:T(8,128)} %constant.75.clone, s32[]{:T(128)S(6)} %select_n.74, pred[]{:T(512)S(6)} %eq.66), kind=kOutput, calls=%fused_computation.18 | convolution fusion | flops 25198592 | bytes 229381 | tf_op jit(solution)/shard_map/dot_general | solution.py:7
  93.9 1.2 %fusion.11 = f32[1,128,1024]{2,1,0:T(8,128)} fusion(f32[128,128]{1,0:T(8,128)S(1)} %convolution_add_fusion, bf16[1024,128]{1,0:T(8,128)(2,1)S(1)} %copy-done.5), kind=kOutput, calls=%fused_computation.17 | convolution fusion | flops 201457664 | bytes 851968 | tf_op jit(solution)/shard_map/dot_general | solution.py:7
  (44 shorter events, 0.2 us)
Async XLA Ops:
  0.6 6.4 %copy-start = (bf16[1,1024,1024]{2,1,0:T(8,128)(2,1)S(1)}, bf16[1,1024,1024]{2,1,0:T(8,128)(2,1)}, u32[]{:S(2)}) copy-start(bf16[1,1024,1024]{2,1,0:T(8,128)(2,1)} %param.22) | copy-start | bytes 6291460
  0.6 41.5 %copy-start.2 = (f32[128,128]{1,0:T(8,128)S(1)}, f32[128,128]{1,0:T(8,128)}, u32[]{:S(2)}) copy-start(f32[128,128]{1,0:T(8,128)} %constant.76.clone) | copy-start | bytes 196612
  0.7 41.4 %copy-start.10 = (f32[128,128]{1,0:T(8,128)S(1)}, f32[128,128]{1,0:T(8,128)}, u32[]{:S(2)}) copy-start(f32[128,128]{1,0:T(8,128)} %constant.77.clone) | copy-start | bytes 196612
  0.7 41.7 %copy-start.9 = (f32[128,128]{1,0:T(8,128)S(1)}, f32[128,128]{1,0:T(8,128)}, u32[]{:S(2)}) copy-start(f32[128,128]{1,0:T(8,128)} %constant.78.clone) | copy-start | bytes 196612
  0.7 21.8 %copy-start.13 = (s32[2]{0:T(128)S(1)}, s32[2]{0:T(128)}, u32[]{:S(2)}) copy-start(s32[2]{0:T(128)} %param.25) | copy-start | bytes 28
  2.3 20.2 %collective-permute-start = (s32[2,3]{0,1:T(4,128)S(1)}, s32[2,3]{0,1:T(4,128)S(1)}, u32[]{:S(2)}, u32[]{:S(2)}) collective-permute-start(s32[2,3]{0,1:T(4,128)S(1)} %pad_add_fusion), channel_id=1, source_target_pairs={{0,32},{32,0},{64,96},{96,64},{128,160},{160,128},{192,224},{224,1... | collective-permute-start | bytes 80 | tf_op jit(solution)/shard_map/ppermute | solution.py:79
  10.4 10.6 %copy-start.14 = (pred[32]{0:T(512)(128)(4,1)}, pred[32]{0:T(512)(128)(4,1)S(1)}, u32[]{:S(2)}) copy-start(pred[32]{0:T(512)(128)(4,1)S(1)} %get-tuple-element.5) | copy-start | bytes 100
  10.4 10.6 %copy-start.15 = (pred[32]{0:T(512)(128)(4,1)}, pred[32]{0:T(512)(128)(4,1)S(1)}, u32[]{:S(2)}) copy-start(pred[32]{0:T(512)(128)(4,1)S(1)} %get-tuple-element.6) | copy-start | bytes 100
  11.3 34.1 %copy-start.7 = (f32[128,256,1]{1,0,2:T(8,128)S(1)}, f32[128,256,1]{1,0,2:T(8,128)}, u32[]{:S(2)}) copy-start(f32[128,256,1]{1,0,2:T(8,128)} %constant.98) | copy-start | bytes 393220
  11.3 26.0 %all-to-all-start = ((bf16[32,64,128]{2,1,0:T(8,128)(2,1)}), bf16[32,64,128]{2,1,0:T(8,128)(2,1)S(1)}, u32[]{:S(2)}, u32[]{:S(2)}) async-start(bf16[32,64,128]{2,1,0:T(8,128)(2,1)} %select_select_fusion), calls=%async_computation | async-start | bytes 1048576 | tf_op jit(solution)/shard_map/all_to_all | solution.py:89
  22.6 4.3 %collective-permute-start.1 = (s32[4,3]{0,1:T(4,128)S(1)}, s32[4,3]{0,1:T(4,128)S(1)}, u32[]{:S(2)}, u32[]{:S(2)}) collective-permute-start(s32[4,3]{0,1:T(4,128)S(1)} %pad_add_fusion.1), channel_id=1, source_target_pairs={{0,64},{32,96},{64,0},{96,32},{128,192},{160,224},{192,128},{224,1... | collective-permute-start | bytes 152 | tf_op jit(solution)/shard_map/ppermute | solution.py:79
  26.9 7.4 %collective-permute-start.2 = (s32[8,3]{0,1:T(4,128)S(1)}, s32[8,3]{0,1:T(4,128)S(1)}, u32[]{:S(2)}, u32[]{:S(2)}) collective-permute-start(s32[8,3]{0,1:T(4,128)S(1)} %pad_add_fusion.2), channel_id=1, source_target_pairs={{0,128},{32,160},{64,192},{96,224},{128,0},{160,32},{192,64},{224,... | collective-permute-start | bytes 296 | tf_op jit(solution)/shard_map/ppermute | solution.py:79
  43.7 2.9 %copy-start.8 = (f32[256,128,1]{1,0,2:T(8,128)S(1)}, f32[256,128,1]{1,0,2:T(8,128)}, u32[]{:S(2)}) copy-start(f32[256,128,1]{1,0,2:T(8,128)} %constant.99) | copy-start | bytes 393220
  46.5 3.4 %copy-start.19 = (f32[16]{0:T(128)S(1)}, f32[16]{0:T(128)}, u32[]{:S(2)}) copy-start(f32[16]{0:T(128)} %get-tuple-element.18) | copy-start | bytes 196
  46.6 3.4 %copy-start.3 = (f32[1024,128]{1,0:T(8,128)S(1)}, f32[1024,128]{1,0:T(8,128)}, u32[]{:S(2)}) copy-start(f32[1024,128]{1,0:T(8,128)} %constant.82.clone) | copy-start | bytes 1572868
  46.6 4.0 %copy-start.6 = (f32[1024,128]{1,0:T(8,128)S(1)}, f32[1024,128]{1,0:T(8,128)}, u32[]{:S(2)}) copy-start(f32[1024,128]{1,0:T(8,128)} %constant.83.clone) | copy-start | bytes 1572868
  50.7 4.6 %copy-start.4 = (bf16[1,1024,1024]{2,1,0:T(8,128)(2,1)S(1)}, bf16[1,1024,1024]{2,1,0:T(8,128)(2,1)}, u32[]{:S(2)}) copy-start(bf16[1,1024,1024]{2,1,0:T(8,128)(2,1)} %param.27) | copy-start | bytes 6291460
  55.3 3.9 %copy-start.1 = (f32[1024,1024]{1,0:T(8,128)}, f32[1024,1024]{1,0:T(8,128)S(1)}, u32[]{:S(2)}) copy-start(f32[1024,1024]{1,0:T(8,128)S(1)} %add_divide_fusion) | copy-start | bytes 12582916
  55.3 4.0 %copy-start.18 = (f32[16]{0:T(128)S(1)}, f32[16]{0:T(128)}, u32[]{:S(2)}) copy-start(f32[16]{0:T(128)} %get-tuple-element.17) | copy-start | bytes 196
  63.5 5.0 %copy-start.11 = (f32[64,128]{1,0:T(8,128)S(1)}, f32[64,128]{1,0:T(8,128)}, u32[]{:S(2)}) copy-start(f32[64,128]{1,0:T(8,128)} %constant.93) | copy-start | bytes 98308
  63.5 5.0 %copy-start.12 = (f32[64,128]{1,0:T(8,128)S(1)}, f32[64,128]{1,0:T(8,128)}, u32[]{:S(2)}) copy-start(f32[64,128]{1,0:T(8,128)} %constant.95) | copy-start | bytes 98308
  63.5 5.2 %copy-start.16 = (pred[32]{0:T(512)(128)(4,1)S(1)}, pred[32]{0:T(512)(128)(4,1)}, u32[]{:S(2)}) copy-start(pred[32]{0:T(512)(128)(4,1)} %broadcast_select_fusion.1) | copy-start | bytes 100
  63.6 29.1 %copy-start.17 = (pred[32]{0:T(512)(128)(4,1)S(1)}, pred[32]{0:T(512)(128)(4,1)}, u32[]{:S(2)}) copy-start(pred[32]{0:T(512)(128)(4,1)} %get-tuple-element.4) | copy-start | bytes 100
  64.6 29.4 %copy-start.5 = (bf16[1024,128]{1,0:T(8,128)(2,1)S(1)}, bf16[1024,128]{1,0:T(8,128)(2,1)}, u32[]{:S(2)}) copy-start(bf16[1024,128]{1,0:T(8,128)(2,1)} %constant.92) | copy-start | bytes 786436
  69.6 23.1 %all-to-all-start.1 = ((bf16[32,64,128]{2,1,0:T(8,128)(2,1)}), bf16[32,64,128]{2,1,0:T(8,128)(2,1)S(1)}, u32[]{:S(2)}, u32[]{:S(2)}) async-start(bf16[32,64,128]{2,1,0:T(8,128)(2,1)} %broadcast_select_fusion), calls=%async_computation.1 | async-start | bytes 1048576 | tf_op jit(solution)/shard_map/all_to_all | solution.py:98

commit v2 on v1

v2 whole, which is shorter than its diff:
```python
import math

import jax
import jax.numpy as jnp
import ml_dtypes
import numpy as np
from jax import lax
from jax.experimental import pallas as pl
from jax.experimental.pallas import tpu as pltpu
from jax.sharding import PartitionSpec as P

TILE_PX = 1024
HALO = 64
EXT_PX = 1152
FREQ = 128
GRID = 128
SOURCES = 16
PUPIL_R = 28
ROWS = 128
STEEPNESS = 4.0
THRESHOLD = 0.6
LEARN_RATE = 8.0
SCALE = 1.0 / (FREQ / 2 * math.sqrt(EXT_PX * TILE_PX))
INTERPRET = False
BF16 = ml_dtypes.bfloat16


def split(table):
    high = table.astype(BF16)
    return high, (table - high.astype(np.float64)).astype(BF16)


def half_table(count, period):
    angle = 2 * np.pi * ((np.arange(count)[:, None] * np.arange(64)[None]) % period) / period
    return np.concatenate([np.cos(angle), np.sin(angle)], axis=1)


def full_table(count, period):
    freq = np.arange(FREQ) - FREQ // 2
    angle = 2 * np.pi * ((np.arange(count)[:, None] * freq[None]) % period) / period
    keep = (freq > -64)[None]
    return np.concatenate([np.cos(angle) * keep, np.sin(angle) * keep], axis=1)


def unfold_tables():
    even = np.zeros((FREQ, 64))
    odd = np.zeros((FREQ, 64))
    for row, freq in enumerate(range(-64, 64)):
        if freq > -64:
            even[row, abs(freq)] = 1
            odd[row, abs(freq)] = np.sign(freq)
    return even, odd


def coarse_table():
    angle = 2 * np.pi * ((np.arange(GRID)[:, None] * (np.arange(64) - 32)[None]) % GRID) / GRID
    return np.cos(angle), np.sin(angle)


def interpolation(positions):
    apart = positions[:, None] - np.arange(GRID)[None]
    return np.cos(2 * np.pi * apart[:, :, None] * np.arange(-63, 64) / GRID).sum(axis=-1) / GRID


COL = half_table(TILE_PX, TILE_PX).astype(BF16)
ROW = full_table(EXT_PX, EXT_PX)
EVEN, ODD = unfold_tables()
COS_W, SIN_W = coarse_table()
ROW_F32 = ROW.astype(np.float32)
RIM_HL = np.concatenate(split(np.concatenate([ROW[:HALO], ROW[EXT_PX - HALO :]], axis=0).T), axis=1)
UNFOLD = np.stack(
    [
        np.concatenate([np.concatenate([EVEN, -ODD], axis=1).T] * 2, axis=0),
        np.concatenate([np.concatenate([-EVEN, -ODD], axis=1).T] * 2, axis=0),
        np.concatenate([np.concatenate([EVEN, ODD], axis=1)] * 2, axis=0),
    ]
).astype(BF16)
LEFT_H, LEFT_L = split(np.concatenate([COS_W, SIN_W], axis=0))
LEFT = np.concatenate([LEFT_H, LEFT_H, LEFT_L], axis=1)
RIGHT_H, RIGHT_L = split(
    np.concatenate(
        [np.concatenate([COS_W.T, SIN_W.T], axis=1), np.concatenate([-SIN_W.T, COS_W.T], axis=1)], axis=0
    )
)
RIGHT = np.concatenate([RIGHT_H, RIGHT_L], axis=0)
RIGHT_T = np.concatenate([RIGHT_H.T, RIGHT_L.T], axis=1)
LEFT_T = np.concatenate(split(np.concatenate([COS_W.T, SIN_W.T], axis=0)), axis=0)
GRID_Y = np.concatenate(split(interpolation((HALO + np.arange(TILE_PX)) / 9.0)), axis=1)
GRID_YT = np.concatenate(split(interpolation((HALO + np.arange(TILE_PX)) / 9.0).T), axis=0)
GRID_X = np.concatenate(split(interpolation(np.arange(TILE_PX) / 8.0)), axis=1)
DISC = (np.arange(64)[:, None] - 32) ** 2 + (np.arange(64)[None] - 32) ** 2 <= PUPIL_R * PUPIL_R


def dot(left, right):
    return jnp.dot(left, right, preferred_element_type=jnp.float32)


def dot_t(left, right):
    return lax.dot_general(left, right, (((1,), (1,)), ((), ())), preferred_element_type=jnp.float32)


def halves(value):
    high = value.astype(jnp.bfloat16)
    return high, (value - high.astype(jnp.float32)).astype(jnp.bfloat16)


def low_lanes(shape):
    return lax.broadcasted_iota(jnp.int32, shape, 1) < 64


def rims_kernel(where_ref, tile_ref, col_ref, sent_ref, rows_ref, sems):
    copies = [
        pltpu.make_async_copy(tile_ref.at[pl.ds(start, HALO)], rows_ref.at[pl.ds(place, HALO)], sems.at[number])
        for number, (start, place) in enumerate(((0, 0), (TILE_PX - HALO, HALO)))
    ]
    for copy in copies:
        copy.start()
    sent_ref[...] = jnp.zeros(sent_ref.shape, jnp.bfloat16)
    for copy in copies:
        copy.wait()
    rims = dot(rows_ref[...], col_ref[...]).astype(jnp.bfloat16)

    @pl.when(where_ref[2] > 0)
    def _():
        sent_ref[where_ref[0]] = rims[:HALO]

    @pl.when(where_ref[3] > 0)
    def _():
        sent_ref[where_ref[1]] = rims[HALO:]


def make_rims(where, tile, col):
    return pl.pallas_call(
        rims_kernel,
        out_shape=jax.ShapeDtypeStruct((32, HALO, 128), jnp.bfloat16),
        in_specs=[
            pl.BlockSpec(memory_space=pltpu.SMEM),
            pl.BlockSpec(memory_space=pl.ANY),
            pl.BlockSpec(memory_space=pltpu.VMEM),
        ],
        out_specs=pl.BlockSpec(memory_space=pltpu.VMEM),
        scratch_shapes=[pltpu.VMEM((2 * HALO, TILE_PX), jnp.bfloat16), pltpu.SemaphoreType.DMA((2,))],
        interpret=INTERPRET,
        name="rims",
    )(where, tile, col)


def fields_kernel(
    where_ref, ints_ref, up_ref, down_ref, own_ref, pupil_ref, rim_ref, unfold_ref, left_ref, right_ref, right_t_ref,
    left_t_ref, grid_y_ref, grid_yt_ref, grid_x_ref, edge_ref, mine_a_ref, mine_b_ref, target_hbm,
    resist_hbm, back_ref, sent_ref,
    target_ref, resist_ref, spec_ref, field_ref, fold_ref, grad_ref, sems,
):
    fetch = pltpu.make_async_copy(target_hbm, target_ref, sems.at[0])
    fetch.start()
    low = low_lanes((128, 128))
    low_w = low_lanes((64, 128))
    up = jnp.where(where_ref[2] > 0, up_ref[0].astype(jnp.float32), 0.0)
    down = jnp.where(where_ref[3] > 0, down_ref[0].astype(jnp.float32), 0.0)
    rims = jnp.concatenate([up, down], axis=0).astype(jnp.bfloat16)
    half = own_ref[...] + dot(rim_ref[...], jnp.concatenate([rims, rims], axis=0))
    by_cos, by_sin = half[:FREQ], half[FREQ:]
    spec_ref[0] = dot(jnp.concatenate(halves(jnp.where(low, by_cos, by_sin)), axis=1), unfold_ref[0])
    spec_ref[1] = dot(jnp.concatenate(halves(jnp.where(low, by_sin, by_cos)), axis=1), unfold_ref[1])
    coarse = jnp.zeros((GRID, GRID), jnp.float32)
    for source in range(SOURCES):
        shift_a = ints_ref[source, 0]
        shift_b = ints_ref[source, 1]
        rows = pl.ds(32 - shift_a, 64)
        spec_re = spec_ref[0, rows, :]
        spec_im = spec_ref[1, rows, :]
        near = lax.rem(96 + shift_b, 128)
        far = 32 + shift_b
        window = jnp.where(low_w, pltpu.roll(spec_re, near, 1), pltpu.roll(spec_im, far, 1))
        amp = pupil_ref[0] * window + pupil_ref[1] * pltpu.roll(window, 64, 1)
        amp_h, amp_l = halves(amp)
        both = dot(left_ref[...], jnp.concatenate([amp_h, amp_l, amp_h], axis=0))
        swapped = pltpu.roll(both[GRID:], 64, 1)
        line = both[:GRID] + jnp.where(low, -swapped, swapped)
        line_h, line_l = halves(line)
        field = dot(jnp.concatenate([line_h, line_h], axis=1), right_ref[...]) + dot(line_l, right_ref[:128])
        field_ref[source] = field
        weight = ints_ref[source, 2].astype(jnp.float32) * (1.0 / (4.0 * SOURCES))
        squared = field * field
        coarse = coarse + weight * (squared[:, :GRID] + squared[:, GRID:])
    coarse_h, coarse_l = halves(coarse)
    coarse_hh = jnp.concatenate([coarse_h, coarse_h], axis=0)
    fetch.wait()
    chunk = 256
    for place in range(TILE_PX // chunk):
        rows = pl.ds(place * chunk, chunk)
        rows_y = dot(grid_y_ref[rows, :], coarse_hh) + dot(grid_y_ref[rows, :GRID], coarse_l)
        rows_h, rows_l = halves(rows_y)
        intensity = dot_t(jnp.concatenate([rows_h, rows_h], axis=1), grid_x_ref[...]) + dot_t(
            rows_l, grid_x_ref[:, :GRID]
        )
        resist = jax.nn.sigmoid(STEEPNESS * (intensity - THRESHOLD))
        resist_ref[rows, :] = resist
        wanted = target_ref[rows, :].astype(jnp.float32)
        adjoint = ((2.0 * STEEPNESS) * (resist - wanted) * resist * (1.0 - resist)).astype(jnp.bfloat16)
        folded = dot(adjoint, grid_x_ref[...])
        fold_ref[rows, :] = jnp.concatenate(halves(folded[:, :GRID] + folded[:, GRID:]), axis=1)
    my_src = where_ref[4]
    keep = pltpu.make_async_copy(resist_ref.at[pl.ds(my_src * ROWS, ROWS)], resist_hbm, sems.at[1])
    keep.start()
    adjoint4 = dot(grid_yt_ref[...], fold_ref[...])
    adjoint2 = adjoint4[:GRID] + adjoint4[GRID:]
    coarse_adjoint = 2.0 * (adjoint2[:, :GRID] + adjoint2[:, GRID:])
    grad_ref[...] = jnp.zeros(grad_ref.shape, jnp.float32)
    for source in range(SOURCES):
        shift_a = ints_ref[source, 0]
        shift_b = ints_ref[source, 1]
        weight = ints_ref[source, 2].astype(jnp.float32) * (1.0 / (4.0 * SOURCES))
        weighted = weight * coarse_adjoint
        dfield_h, dfield_l = halves(field_ref[source] * jnp.concatenate([weighted, weighted], axis=1))
        dline2 = dot(dfield_h, right_t_ref[...])
        dline = dline2[:, :128] + dline2[:, 128:] + dot(dfield_l, right_t_ref[:, :128])
        damp4 = dot(left_t_ref[...], jnp.concatenate(halves(dline), axis=1))
        damp2 = damp4[:128] + damp4[128:]
        damp1 = damp2[:, :128] + damp2[:, 128:]
        swapped = pltpu.roll(damp1[64:], 64, 1)
        damp = damp1[:64] + jnp.where(low_w, swapped, -swapped)
        grad = pupil_ref[0] * damp - pupil_ref[1] * pltpu.roll(damp, 64, 1)
        rows = pl.ds(32 - shift_a, 64)
        grad_ref[0, rows, :] += pltpu.roll(jnp.where(low_w, grad, 0.0), 32 - shift_b, 1)
        grad_ref[1, rows, :] += pltpu.roll(jnp.where(low_w, 0.0, grad), lax.rem(96 - shift_b, 128), 1)
    grads = jnp.concatenate([grad_ref[0], grad_ref[1]], axis=0)
    folded = dot(jnp.concatenate(halves(grads), axis=1), unfold_ref[2])
    fold_re, fold_im = folded[:FREQ], folded[FREQ:]
    packed = jnp.concatenate(
        [jnp.where(low, fold_re, -fold_im), jnp.where(low, -fold_im, -fold_re)], axis=0
    )
    tables = jnp.concatenate([edge_ref[...], mine_a_ref[...], mine_b_ref[...]], axis=0)
    back = jnp.dot(tables, packed, precision=lax.Precision.HIGHEST, preferred_element_type=jnp.float32)
    sent_ref[...] = jnp.zeros(sent_ref.shape, jnp.bfloat16)

    @pl.when(where_ref[6] > 0)
    def _():
        sent_ref[where_ref[5]] = back[:HALO].astype(jnp.bfloat16)

    back_ref[...] = back[HALO:]
    keep.wait()


def make_fields(where, ints, got, own, pupil, target):
    whole = pl.BlockSpec(memory_space=pltpu.VMEM)
    const = lambda table: jnp.asarray(table)
    grid_spec = pltpu.PrefetchScalarGridSpec(
        num_scalar_prefetch=2,
        grid=(1,),
        in_specs=[
            pl.BlockSpec((1, HALO, 128), lambda i, where, ints: (where[0], 0, 0)),
            pl.BlockSpec((1, HALO, 128), lambda i, where, ints: (where[1], 0, 0)),
        ]
        + [whole] * 11
        + [
            pl.BlockSpec((HALO, 2 * FREQ), lambda i, where, ints: (where[7], 0)),
            pl.BlockSpec((HALO, 2 * FREQ), lambda i, where, ints: (1 + 2 * where[4], 0)),
            pl.BlockSpec((HALO, 2 * FREQ), lambda i, where, ints: (2 + 2 * where[4], 0)),
            pl.BlockSpec(memory_space=pl.ANY),
        ],
        out_specs=[pl.BlockSpec(memory_space=pl.ANY), whole, whole],
        scratch_shapes=[
            pltpu.VMEM((TILE_PX, TILE_PX), jnp.bfloat16),
            pltpu.VMEM((TILE_PX, TILE_PX), jnp.float32),
            pltpu.VMEM((2, FREQ, FREQ), jnp.float32),
            pltpu.VMEM((SOURCES, GRID, 2 * GRID), jnp.float32),
            pltpu.VMEM((TILE_PX, 2 * GRID), jnp.bfloat16),
            pltpu.VMEM((2, FREQ, FREQ), jnp.float32),
            pltpu.SemaphoreType.DMA((2,)),
        ],
    )
    row_table = const(ROW_F32)
    return pl.pallas_call(
        fields_kernel,
        out_shape=(
            jax.ShapeDtypeStruct((ROWS, TILE_PX), jnp.float32),
            jax.ShapeDtypeStruct((ROWS, 128), jnp.float32),
            jax.ShapeDtypeStruct((32, HALO, 128), jnp.bfloat16),
        ),
        grid_spec=grid_spec,
        compiler_params=pltpu.CompilerParams(vmem_limit_bytes=48 * 1024 * 1024),
        interpret=INTERPRET,
        name="fields",
    )(
        where, ints, got, got, own, pupil, const(RIM_HL), const(UNFOLD), const(LEFT), const(RIGHT), const(RIGHT_T),
        const(LEFT_T), const(GRID_Y), const(GRID_YT), const(GRID_X), row_table, row_table, row_table, target,
    )


def steps_kernel(where_ref, got_ref, back_ref, col_ref, out_ref):
    rim = got_ref[0].astype(jnp.float32)
    top = jnp.where(where_ref[9] > 0, rim, 0.0)
    bottom = jnp.where(where_ref[10] > 0, rim, 0.0)
    back = -LEARN_RATE * (back_ref[...] + jnp.concatenate([top, bottom], axis=0))
    high, low = halves(back)
    out_ref[...] = dot_t(high, col_ref[...]) + dot_t(low, col_ref[...])


def make_steps(where, got, back, col):
    whole = pl.BlockSpec(memory_space=pltpu.VMEM)
    grid_spec = pltpu.PrefetchScalarGridSpec(
        num_scalar_prefetch=1,
        grid=(1,),
        in_specs=[pl.BlockSpec((1, HALO, 128), lambda i, where: (where[8], 0, 0)), whole, whole],
        out_specs=whole,
    )
    return pl.pallas_call(
        steps_kernel,
        out_shape=jax.ShapeDtypeStruct((ROWS, TILE_PX), jnp.float32),
        grid_spec=grid_spec,
        interpret=INTERPRET,
        name="steps",
    )(where, got, back, col)


def places(slot_pos, my_slot, my_src, src_count):
    slot_ids = jnp.arange(slot_pos.shape[0], dtype=jnp.int32)
    my_position = jnp.sum(jnp.where(slot_ids == my_slot, slot_pos, 0))
    above = jnp.sum(jnp.where(slot_pos == my_position - 1, slot_ids, 0))
    below = jnp.sum(jnp.where(slot_pos == my_position + 1, slot_ids, 0))
    has_above = my_position > 0
    has_below = my_position < slot_pos.shape[0] - 1
    first = my_src == 0
    last = my_src == src_count - 1
    return jnp.stack(
        [
            above,
            below,
            has_above.astype(jnp.int32),
            has_below.astype(jnp.int32),
            my_src,
            jnp.where(first, below, above),
            jnp.where(first, has_below, has_above).astype(jnp.int32),
            jnp.where(first, (EXT_PX - HALO) // HALO, 0),
            jnp.where(first, above, below),
            (first & has_above).astype(jnp.int32),
            (last & has_below).astype(jnp.int32),
        ]
    ).astype(jnp.int32)


def pupil_tables(pupil_phase):
    window = pupil_phase[32:96, 32:96]
    real = jnp.where(DISC, jnp.cos(window), 0.0) * SCALE
    imag = jnp.where(DISC, jnp.sin(window), 0.0) * SCALE
    return jnp.stack([jnp.concatenate([real, real], axis=1), jnp.concatenate([-imag, imag], axis=1)])


def own_half(tile, col):
    half = jnp.dot(tile, col, preferred_element_type=jnp.float32)
    rows = jnp.asarray(ROW_F32[HALO : HALO + TILE_PX])
    return lax.dot_general(
        rows, half, (((0,), (0,)), ((), ())), precision=lax.Precision.HIGHEST, preferred_element_type=jnp.float32
    )


def per_device(mask_tiles, slot_pos, src_shift, src_weight, pupil_phase, target):
    src_count = lax.axis_size("src")
    where = places(slot_pos, lax.axis_index("tile"), lax.axis_index("src"), src_count)
    ints = jnp.concatenate([src_shift, src_weight[:, None]], axis=1)
    step = 1
    while step < src_count:
        other = lax.ppermute(ints, "src", [(i, i ^ step) for i in range(src_count)])
        ints = jnp.concatenate([ints, other], axis=0)
        step *= 2
    col = jnp.asarray(COL)
    tile = mask_tiles[0]
    got = lax.all_to_all(make_rims(where, tile, col), "tile", 0, 0, tiled=True)
    resist, back, sent = make_fields(where, ints, got, own_half(tile, col), pupil_tables(pupil_phase), target[0])
    got = lax.all_to_all(sent, "tile", 0, 0, tiled=True)
    return (resist[None], make_steps(where, got, back, col)[None])


def solution(mesh):
    return jax.shard_map(
        per_device,
        mesh=mesh,
        in_specs=(P("tile", None, None), P(), P("src", None), P("src"), P(), P("tile", None, None)),
        out_specs=(P("tile", "src", None), P("tile", "src", None)),
        check_vma=False,
    )
```

time: 95.9 us -> 86.9 us (0.906)
  matrix products: 33.5 us -> 4.47 us
  blocking collectives: 0 us -> 25.5 us
  waiting for transfers between devices: 21.4 us -> 3.95 us
  Pallas kernels: 0 us -> 16.3 us
  starting transfers between devices: 25.5 us -> 18.8 us
  other arithmetic: 8.76 us -> 3.77 us
  local copies, waits for them, and re-layouts: 3.48 us -> 7.44 us
  between operations: 2.52 us -> 6.07 us
    dot_general x31 -> x2, matrix products: 33.5 us -> 4.47 us  [the longest x1 2.64 us: own_half(): half = jnp.dot(tile, col, preferred_element_type=jnp.float32)]
    all_to_all x0 -> x1, blocking collectives: none -> 25.5 us  [per_device(): got = lax.all_to_all(sent, 'tile', 0, 0, tiled=True)]
    pallas_call x0 -> x3, Pallas kernels: none -> 16.3 us  [the longest x1 10.5 us: make_fields(): pl.pallas_call(fields_kernel, out_shape=(jax.ShapeDtypeStruct((ROWS, TILE...]
    all_to_all x2 -> x1, waiting for transfers between devices: 16.8 us -> 0.71 us  [per_device(): got = lax.all_to_all(make_rims(where, tile, col), 'tile', 0, 0, tiled=True)]
    all_to_all x2 -> x1, starting transfers between devices: 16.3 us -> 9.48 us  [per_device(): got = lax.all_to_all(make_rims(where, tile, col), 'tile', 0, 0, tiled=True)]
    unnamed x41 -> x33, local copies, waits for them, and re-layouts: 1.04 us -> 5.4 us
    select_n x3 -> x0, other arithmetic: 2.37 us -> none  [the longest x1 0.93 us: per_device(): jnp.where(is_below[:, None, None], rims[None, 960:], jnp.where(is_above[:...]
    another operation x0 -> x1, local copies, waits for them, and re-layouts: none -> 1.95 us  [places(): jnp.stack([above, below, has_above.astype(jnp.int32), has_below.astype(jn...]
  transfers between devices with their start and end apart: 5 -> 4, of which waited for: 4 -> 3; matrix products, arithmetic and copies ran while one was open for 10% -> 11% of each run, Pallas kernels for 0% -> 3%
where the time goes in v2:
time: 86.9 us; the launch traced here: 86.3 us
  blocking collectives  25.5 us (29%)
  starting transfers between devices  18.8 us (22%)
  Pallas kernels  16.3 us (19%)
  local copies, waits for them, and re-layouts  7.44 us (9%)
  between operations  6.07 us (7%)
  matrix products  4.47 us (5%)
  waiting for transfers between devices  3.95 us (5%)
  other arithmetic  3.77 us (4%)
    all_to_all x1, blocking collectives, per_device(): got = lax.all_to_all(sent, 'tile', 0, 0, tiled=True)  25.5 us
    pallas_call x1, Pallas kernels, make_fields(): pl.pallas_call(fields_kernel, out_shape=(jax.ShapeDtypeStruct((ROWS, TILE...  10.5 us
    all_to_all x1, starting transfers between devices, per_device(): got = lax.all_to_all(make_rims(where, tile, col), 'tile', 0, 0, tiled=True)  9.48 us
    ppermute x3, starting transfers between devices, per_device(): other = lax.ppermute(ints, 'src', [(i, i ^ step) for i in range(src_count)])  9.31 us
    unnamed x33, local copies, waits for them, and re-layouts  5.4 us
    ppermute x3, waiting for transfers between devices, per_device(): other = lax.ppermute(ints, 'src', [(i, i ^ step) for i in range(src_count)])  3.25 us
    pallas_call x1, Pallas kernels, make_rims(): pl.pallas_call(rims_kernel, out_shape=jax.ShapeDtypeStruct((32, HALO, 128...  2.96 us
    pallas_call x1, Pallas kernels, make_steps(): pl.pallas_call(steps_kernel, out_shape=jax.ShapeDtypeStruct((ROWS, TILE_P...  2.76 us
  transfers between devices with their start and end apart: 4, of which 3 were waited for; matrix products, arithmetic and copies ran while one was open for 11% of the time, Pallas kernels for 3%

profile of v2, /device:TPU:1, one launch (start us, length us, event | category | flops | bytes accessed | tf_op | source)
XLA Modules:
  0.0 86.3 jit_solution(4359849977145435877)
XLA Ops:
  0.6 0.0 copy-start.14
  0.6 0.0 copy-start.13
  0.7 0.8 copy.22
  1.5 0.7 pad_add_fusion
  2.1 2.1 %collective-permute-start = (s32[2,3]{0,1:T(4,128)S(1)}, s32[2,3]{0,1:T(4,128)S(1)}, u32[]{:S(2)}, u32[]{:S(2)}) collective-permute-start(s32[2,3]{0,1:T(4,128)S(1)} %pad_add_fusion), channel_id=1, source_target_pairs={{0,32},{32,0},{64,96},{96,64},{128,160},{160,128},{192,224},{224,1... | collective-permute-start | bytes 80 | tf_op jit(solution)/shard_map/ppermute | solution.py:364
  4.2 1.3 %fusion = s32[]{:T(128)} fusion(s32[32]{0:T(128)} %param.20, s32[]{:T(128)S(6)} %axis_index.22), kind=kLoop, calls=%fused_computation.12 | loop fusion | flops 95 | bytes 136 | tf_op jit(solution)/shard_map/reduce_sum | solution.py:319
  8.1 1.3 %fusion.2 = (s32[]{:T(128)}, s32[]{:T(128)}) fusion(s32[32]{0:T(128)} %param.20, s32[]{:T(128)S(6)} %add.4, s32[]{:T(128)S(6)} %sub.3), kind=kLoop, calls=%fused_computation.14 | loop fusion | flops 190 | bytes 144 | tf_op jit(solution)/shard_map/reduce_sum | solution.py:321
  12.0 2.0 %stack.76.where_ref = s32[11]{0:T(128)} concatenate(s32[1]{0:T(128)} %bitcast, s32[1]{0:T(128)} %bitcast.1, s32[1]{0:T(128)} %bitcast.2, s32[1]{0:T(128)} %bitcast.3, s32[1]{0:T(128)} %bitcast.4, s32[1]{0:T(128)} %bitcast.5, s32[1]{0:T(128)} %bitcast.6, s32[1]{0:T(128)} %bitcast.7, s32[1]{0:T(128)} %bitcast.8, s32[1]{0:T(128)} %bitcast.9, s32[1]{0:T(128)} %bitcast.10), dimensions={0} | concatenate | bytes 88 | tf_op jit(solution)/shard_map/stack | solution.py:326
  14.0 3.0 %rims.1 = bf16[32,64,128]{2,1,0:T(8,128)(2,1)} custom-call(s32[11]{0:T(128)} %stack.76.where_ref, bf16[1024,1024]{1,0:T(8,128)(2,1)} %bitcast.25, bf16[1024,128]{1,0:T(8,128)(2,1)} %constant.51.clone.col_ref), custom_call_target="tpu_custom_call" | custom-call | tf_op jit(solution)/shard_map/rims/pallas_call | solution.py:133
  17.0 9.5 %all-to-all-start = ((bf16[32,64,128]{2,1,0:T(8,128)(2,1)}), bf16[32,64,128]{2,1,0:T(8,128)(2,1)S(1)}, u32[]{:S(2)}, u32[]{:S(2)}) async-start(bf16[32,64,128]{2,1,0:T(8,128)(2,1)} %rims.1), calls=%async_computation | async-start | bytes 1048576 | tf_op jit(solution)/shard_map/all_to_all | solution.py:369
  26.4 0.0 copy-done.14
  26.5 0.0 copy-done.13
  26.5 0.0 copy-start.12
  26.5 0.2 select_multiply_fusion.1
  26.7 0.1 maximum_bitcast_fusion
  26.8 0.0 copy-start.15
  26.8 0.0 copy-start
  26.8 0.0 copy-start.1
  26.8 0.0 copy-start.2
  26.8 0.0 copy-start.3
  26.8 0.0 copy-start.9
  26.9 0.0 copy-start.11
  26.9 2.6 %fusion.3 = f32[128,1024]{1,0:T(8,128)S(1)} fusion(bf16[1024,128]{1,0:T(8,128)(2,1)} %constant.51.clone.col_ref, bf16[1,1024,1024]{2,1,0:T(8,128)(2,1)} %param.19), kind=kOutput, calls=%fused_computation.15 | convolution fusion | flops 268435456 | bytes 2883584 | tf_op jit(solution)/shard_map/dot_general | solution.py:351
  29.5 0.0 copy-done.12
  29.5 1.8 %fusion.6.own_ref = f32[256,128]{1,0:T(8,128)S(1)} fusion(f32[1024,256]{1,0:T(8,128)S(1)} %copy-done.12, f32[128,1024]{1,0:T(8,128)S(1)} %fusion.3), kind=kOutput, calls=%fused_computation.18 | convolution fusion | flops 402653184 | bytes 1703936 | tf_op jit(solution)/shard_map/dot_general | solution.py:353
  31.4 0.0 collective-permute-done
  31.4 0.0 copy-done.15
  31.4 0.1 pad_add_fusion.1
  31.5 2.6 %collective-permute-start.1 = (s32[4,3]{0,1:T(4,128)S(1)}, s32[4,3]{0,1:T(4,128)S(1)}, u32[]{:S(2)}, u32[]{:S(2)}) collective-permute-start(s32[4,3]{0,1:T(4,128)S(1)} %pad_add_fusion.1), channel_id=1, source_target_pairs={{0,64},{32,96},{64,0},{96,32},{128,192},{160,224},{192,128},{224,1... | collective-permute-start | bytes 152 | tf_op jit(solution)/shard_map/ppermute | solution.py:364
  34.1 1.3 %collective-permute-done.1 = s32[4,3]{0,1:T(4,128)S(1)} collective-permute-done((s32[4,3]{0,1:T(4,128)S(1)}, s32[4,3]{0,1:T(4,128)S(1)}, u32[]{:S(2)}, u32[]{:S(2)}) %collective-permute-start.1) | collective-permute-done | bytes 80 | tf_op jit(solution)/shard_map/ppermute | solution.py:364
  35.4 0.1 pad_add_fusion.2
  35.5 4.5 %collective-permute-start.2 = (s32[8,3]{0,1:T(4,128)S(1)}, s32[8,3]{0,1:T(4,128)S(1)}, u32[]{:S(2)}, u32[]{:S(2)}) collective-permute-start(s32[8,3]{0,1:T(4,128)S(1)} %pad_add_fusion.2), channel_id=1, source_target_pairs={{0,128},{32,160},{64,192},{96,224},{128,0},{160,32},{192,64},{224,... | collective-permute-start | bytes 296 | tf_op jit(solution)/shard_map/ppermute | solution.py:364
  40.0 1.9 %collective-permute-done.2 = s32[8,3]{0,1:T(4,128)S(1)} collective-permute-done((s32[8,3]{0,1:T(4,128)S(1)}, s32[8,3]{0,1:T(4,128)S(1)}, u32[]{:S(2)}, u32[]{:S(2)}) %collective-permute-start.2) | collective-permute-done | bytes 128 | tf_op jit(solution)/shard_map/ppermute | solution.py:364
  42.0 0.1 pad_add_fusion.3
  42.1 0.1 copy.23.ints_ref
  42.1 0.7 all-to-all-done.up_ref.down_ref
  42.8 0.0 copy-done
  42.9 0.0 copy-done.1
  42.9 0.0 copy-done.2
  42.9 0.0 copy-done.3
  42.9 0.0 copy-done.9
  42.9 0.0 copy-done.11
  42.9 0.0 copy-start.4
  42.9 0.9 %copy-done.4 = bf16[3,256,128]{2,1,0:T(8,128)(2,1)S(1)} copy-done((bf16[3,256,128]{2,1,0:T(8,128)(2,1)S(1)}, bf16[3,256,128]{2,1,0:T(8,128)(2,1)}, u32[]{:S(2)}) %copy-start.4) | copy-done | bytes 196632
  43.8 0.0 copy-start.5
  43.8 0.9 %copy-done.5 = bf16[256,256]{1,0:T(8,128)(2,1)S(1)} copy-done((bf16[256,256]{1,0:T(8,128)(2,1)S(1)}, bf16[256,256]{1,0:T(8,128)(2,1)}, u32[]{:S(2)}) %copy-start.5) | copy-done | bytes 131096
  44.7 0.0 copy-start.6
  44.7 0.9 %copy-done.6 = bf16[256,256]{1,0:T(8,128)(2,1)S(1)} copy-done((bf16[256,256]{1,0:T(8,128)(2,1)S(1)}, bf16[256,256]{1,0:T(8,128)(2,1)}, u32[]{:S(2)}) %copy-start.6) | copy-done | bytes 131096
  45.6 0.0 copy-start.7
  45.6 0.9 %copy-done.7 = bf16[256,192]{1,0:T(8,128)(2,1)S(1)} copy-done((bf16[256,192]{1,0:T(8,128)(2,1)S(1)}, bf16[256,192]{1,0:T(8,128)(2,1)}, u32[]{:S(2)}) %copy-start.7) | copy-done | bytes 98328
  46.5 0.0 copy-start.8
  46.5 0.9 %copy-done.8 = bf16[256,256]{1,0:T(8,128)(2,1)S(1)} copy-done((bf16[256,256]{1,0:T(8,128)(2,1)S(1)}, bf16[256,256]{1,0:T(8,128)(2,1)}, u32[]{:S(2)}) %copy-start.8) | copy-done | bytes 131096
  47.4 10.5 %fields.1 = (f32[128,1024]{1,0:T(8,128)}, f32[128,128]{1,0:T(8,128)S(1)}, bf16[32,64,128]{2,1,0:T(8,128)(2,1)S(1)}) custom-call(s32[11]{0:T(128)S(1)} %copy-done.11, s32[16,3]{1,0:T(8,128)S(1)} %copy.23.ints_ref, bf16[32,64,128]{2,1,0:T(8,128)(2,1)S(1)} %all-to-all-done.up_ref.down_ref, bf16[32,64,128]{2,1,0:T(8,128)(2,1)S(1)} %all-to-all-done.up_ref.down_ref, ...), custom_call_target="tpu_custom_call" | custom-call | tf_op jit(solution)/shard_map/fields/pallas_call | solution.py:274
  58.0 0.0 copy-start.10
  58.0 25.5 %all_to_all.10.got_ref = bf16[32,64,128]{2,1,0:T(8,128)(2,1)} all-to-all(bf16[32,64,128]{2,1,0:T(8,128)(2,1)S(1)} %get-tuple-element.6), channel_id=1, replica_groups=mesh['src'=8,'tile'=32] {'tile'}, dimensions={0} | all-to-all | bytes 1048576 | tf_op jit(solution)/shard_map/all_to_all | solution.py:371
  83.5 0.0 copy-done.10
  83.5 2.8 %steps.1 = f32[128,1024]{1,0:T(8,128)} custom-call(s32[11]{0:T(128)} %stack.76.where_ref, bf16[32,64,128]{2,1,0:T(8,128)(2,1)} %all_to_all.10.got_ref, f32[128,128]{1,0:T(8,128)} %copy-done.10, bf16[1024,128]{1,0:T(8,128)(2,1)} %constant.51.clone.col_ref), custom_call_target="tpu_custom_call" | custom-call | tf_op jit(solution)/shard_map/steps/pallas_call | solution.py:308
  (1 shorter events, 0.0 us)
Async XLA Ops:
  0.6 25.8 %copy-start.14 = (pred[64,64]{1,0:T(32,128)(4,1)S(1)}, pred[64,64]{1,0:T(32,128)(4,1)}, u32[]{:S(2)}) copy-start(pred[64,64]{1,0:T(32,128)(4,1)} %constant.53.clone) | copy-start | bytes 12292
  0.6 25.8 %copy-start.13 = (f32[128,128]{1,0:T(8,128)S(1)}, f32[128,128]{1,0:T(8,128)}, u32[]{:S(2)}) copy-start(f32[128,128]{1,0:T(8,128)} %param.23) | copy-start | bytes 196612
  2.1 29.3 %collective-permute-start = (s32[2,3]{0,1:T(4,128)S(1)}, s32[2,3]{0,1:T(4,128)S(1)}, u32[]{:S(2)}, u32[]{:S(2)}) collective-permute-start(s32[2,3]{0,1:T(4,128)S(1)} %pad_add_fusion), channel_id=1, source_target_pairs={{0,32},{32,0},{64,96},{96,64},{128,160},{160,128},{192,224},{224,1... | collective-permute-start | bytes 80 | tf_op jit(solution)/shard_map/ppermute | solution.py:364
  17.0 25.9 %all-to-all-start = ((bf16[32,64,128]{2,1,0:T(8,128)(2,1)}), bf16[32,64,128]{2,1,0:T(8,128)(2,1)S(1)}, u32[]{:S(2)}, u32[]{:S(2)}) async-start(bf16[32,64,128]{2,1,0:T(8,128)(2,1)} %rims.1), calls=%async_computation | async-start | bytes 1048576 | tf_op jit(solution)/shard_map/all_to_all | solution.py:369
  26.5 3.1 %copy-start.12 = (f32[1024,256]{1,0:T(8,128)S(1)}, f32[1024,256]{1,0:T(8,128)}, u32[]{:S(2)}) copy-start(f32[1024,256]{1,0:T(8,128)} %constant.52.clone) | copy-start | bytes 3145732
  26.8 4.6 %copy-start.15 = (s32[2]{0:T(128)S(1)}, s32[2]{0:T(128)}, u32[]{:S(2)}) copy-start(s32[2]{0:T(128)} %param.22) | copy-start | bytes 28
  26.8 16.1 %copy-start = (f32[1152,256]{1,0:T(8,128)S(1)}, f32[1152,256]{1,0:T(8,128)}, u32[]{:S(2)}) copy-start(f32[1152,256]{1,0:T(8,128)} %constant.54.clone.edge_ref.mine_a_ref.mine_b_ref) | copy-start | bytes 3538948
  26.8 16.0 %copy-start.1 = (bf16[1024,256]{1,0:T(8,128)(2,1)S(1)}, bf16[1024,256]{1,0:T(8,128)(2,1)}, u32[]{:S(2)}) copy-start(bf16[1024,256]{1,0:T(8,128)(2,1)} %constant.63.clone.grid_x_ref) | copy-start | bytes 1572868
  26.8 16.0 %copy-start.2 = (bf16[256,1024]{1,0:T(8,128)(2,1)S(1)}, bf16[256,1024]{1,0:T(8,128)(2,1)}, u32[]{:S(2)}) copy-start(bf16[256,1024]{1,0:T(8,128)(2,1)} %constant.62.clone.grid_yt_ref) | copy-start | bytes 1572868
  26.8 16.0 %copy-start.3 = (bf16[1024,256]{1,0:T(8,128)(2,1)S(1)}, bf16[1024,256]{1,0:T(8,128)(2,1)}, u32[]{:S(2)}) copy-start(bf16[1024,256]{1,0:T(8,128)(2,1)} %constant.61.clone.grid_y_ref) | copy-start | bytes 1572868
  26.8 16.0 %copy-start.9 = (bf16[256,128]{1,0:T(8,128)(2,1)S(1)}, bf16[256,128]{1,0:T(8,128)(2,1)}, u32[]{:S(2)}) copy-start(bf16[256,128]{1,0:T(8,128)(2,1)} %constant.60.clone.left_t_ref) | copy-start | bytes 196612
  26.9 16.0 %copy-start.11 = (s32[11]{0:T(128)S(1)}, s32[11]{0:T(128)}, u32[]{:S(2)}) copy-start(s32[11]{0:T(128)} %stack.76.where_ref) | copy-start | bytes 136
  31.5 4.0 %collective-permute-start.1 = (s32[4,3]{0,1:T(4,128)S(1)}, s32[4,3]{0,1:T(4,128)S(1)}, u32[]{:S(2)}, u32[]{:S(2)}) collective-permute-start(s32[4,3]{0,1:T(4,128)S(1)} %pad_add_fusion.1), channel_id=1, source_target_pairs={{0,64},{32,96},{64,0},{96,32},{128,192},{160,224},{192,128},{224,1... | collective-permute-start | bytes 152 | tf_op jit(solution)/shard_map/ppermute | solution.py:364
  35.5 6.5 %collective-permute-start.2 = (s32[8,3]{0,1:T(4,128)S(1)}, s32[8,3]{0,1:T(4,128)S(1)}, u32[]{:S(2)}, u32[]{:S(2)}) collective-permute-start(s32[8,3]{0,1:T(4,128)S(1)} %pad_add_fusion.2), channel_id=1, source_target_pairs={{0,128},{32,160},{64,192},{96,224},{128,0},{160,32},{192,64},{224,... | collective-permute-start | bytes 296 | tf_op jit(solution)/shard_map/ppermute | solution.py:364
  42.9 0.9 %copy-start.4 = (bf16[3,256,128]{2,1,0:T(8,128)(2,1)S(1)}, bf16[3,256,128]{2,1,0:T(8,128)(2,1)}, u32[]{:S(2)}) copy-start(bf16[3,256,128]{2,1,0:T(8,128)(2,1)} %constant.56.clone.unfold_ref) | copy-start | bytes 589828
  43.8 0.9 %copy-start.5 = (bf16[256,256]{1,0:T(8,128)(2,1)S(1)}, bf16[256,256]{1,0:T(8,128)(2,1)}, u32[]{:S(2)}) copy-start(bf16[256,256]{1,0:T(8,128)(2,1)} %constant.59.clone.right_t_ref) | copy-start | bytes 393220
  44.7 0.9 %copy-start.6 = (bf16[256,256]{1,0:T(8,128)(2,1)S(1)}, bf16[256,256]{1,0:T(8,128)(2,1)}, u32[]{:S(2)}) copy-start(bf16[256,256]{1,0:T(8,128)(2,1)} %constant.58.clone.right_ref) | copy-start | bytes 393220
  45.6 0.9 %copy-start.7 = (bf16[256,192]{1,0:T(8,128)(2,1)S(1)}, bf16[256,192]{1,0:T(8,128)(2,1)}, u32[]{:S(2)}) copy-start(bf16[256,192]{1,0:T(8,128)(2,1)} %constant.57.clone.left_ref) | copy-start | bytes 294916
  46.5 0.9 %copy-start.8 = (bf16[256,256]{1,0:T(8,128)(2,1)S(1)}, bf16[256,256]{1,0:T(8,128)(2,1)}, u32[]{:S(2)}) copy-start(bf16[256,256]{1,0:T(8,128)(2,1)} %constant.55.clone.rim_ref) | copy-start | bytes 393220
  58.0 25.6 %copy-start.10 = (f32[128,128]{1,0:T(8,128)}, f32[128,128]{1,0:T(8,128)S(1)}, u32[]{:S(2)}) copy-start(f32[128,128]{1,0:T(8,128)S(1)} %get-tuple-element.7.back_ref) | copy-start | bytes 196612

commit v3 on v2

v3 whole, which is shorter than its diff:
```python
import math

import jax
import jax.numpy as jnp
import ml_dtypes
import numpy as np
from jax import lax
from jax.experimental import pallas as pl
from jax.experimental.pallas import tpu as pltpu
from jax.sharding import PartitionSpec as P

TILE_PX = 1024
HALO = 64
EXT_PX = 1152
FREQ = 128
GRID = 128
SOURCES = 16
TILES = 32
SRC_DEVICES = 8
PUPIL_R = 28
ROWS = 128
STEEPNESS = 4.0
THRESHOLD = 0.6
LEARN_RATE = 8.0
SCALE = 1.0 / (FREQ / 2 * math.sqrt(EXT_PX * TILE_PX))
INTERPRET = False
BF16 = ml_dtypes.bfloat16


def split(table):
    high = table.astype(BF16)
    return high, (table - high.astype(np.float64)).astype(BF16)


def half_table(count, period):
    angle = 2 * np.pi * ((np.arange(count)[:, None] * np.arange(64)[None]) % period) / period
    return np.concatenate([np.cos(angle), np.sin(angle)], axis=1)


def unfold_tables():
    even = np.zeros((FREQ, 64))
    odd = np.zeros((FREQ, 64))
    for row, freq in enumerate(range(-64, 64)):
        if freq > -64:
            even[row, abs(freq)] = 1
            odd[row, abs(freq)] = np.sign(freq)
    return even, odd


def coarse_table():
    angle = 2 * np.pi * ((np.arange(GRID)[:, None] * (np.arange(64) - 32)[None]) % GRID) / GRID
    return np.cos(angle), np.sin(angle)


def interpolation(positions):
    apart = positions[:, None] - np.arange(GRID)[None]
    return np.cos(2 * np.pi * apart[:, :, None] * np.arange(-63, 64) / GRID).sum(axis=-1) / GRID


COL = half_table(TILE_PX, TILE_PX).astype(BF16)
ROW = half_table(EXT_PX, EXT_PX)
EVEN, ODD = unfold_tables()
COS_W, SIN_W = coarse_table()
ROW_F32 = ROW.astype(np.float32)
ZERO = np.zeros((FREQ, 64))
UNFOLD = np.concatenate(
    [np.concatenate([EVEN, ZERO], axis=1), np.concatenate([ZERO, ODD], axis=1)], axis=0
)
LEFT_H, LEFT_L = split(np.concatenate([COS_W, SIN_W], axis=0))
RIGHT = np.concatenate(
    split(
        np.concatenate(
            [np.concatenate([COS_W.T, SIN_W.T], axis=1), np.concatenate([-SIN_W.T, COS_W.T], axis=1)], axis=0
        )
    ),
    axis=0,
)
LEFT_T = np.concatenate(split(np.concatenate([COS_W.T, SIN_W.T], axis=0)), axis=0)
RIM = np.concatenate(split(np.concatenate([ROW[:HALO], ROW[EXT_PX - HALO :]], axis=0).T), axis=1)
LANES = np.concatenate([EVEN, ODD], axis=1)
SMALL = np.concatenate(
    [
        UNFOLD.astype(BF16),
        np.concatenate([LEFT_H, LEFT_H, LEFT_L, np.zeros_like(LEFT_L)], axis=1),
        RIGHT,
        LEFT_T,
        np.concatenate([RIM, UNFOLD.T.astype(BF16)], axis=0),
        np.concatenate([LANES, np.zeros_like(LANES)], axis=0).astype(BF16),
    ],
    axis=1,
)
ROWS_Y = (HALO + np.arange(TILE_PX)) / 9.0
GRIDS = np.concatenate(split(interpolation(ROWS_Y)) + split(interpolation(np.arange(TILE_PX) / 8.0)), axis=1)
GRID_YT = np.concatenate(split(interpolation(ROWS_Y).T), axis=0)
DISC = (np.arange(64)[:, None] - 32) ** 2 + (np.arange(64)[None] - 32) ** 2 <= PUPIL_R * PUPIL_R


def dot(left, right):
    return jnp.dot(left, right, preferred_element_type=jnp.float32)


def dot_t(left, right):
    return lax.dot_general(left, right, (((1,), (1,)), ((), ())), preferred_element_type=jnp.float32)


def halves(value):
    high = value.astype(jnp.bfloat16)
    return high, (value - high.astype(jnp.float32)).astype(jnp.bfloat16)


def low_lanes(shape):
    return lax.broadcasted_iota(jnp.int32, shape, 1) < 64


def places(slot_ref):
    my_slot = lax.axis_index("tile")
    my_position = slot_ref[my_slot]
    above = jnp.int32(-1)
    below = jnp.int32(-1)
    for slot in range(TILES):
        position = slot_ref[slot]
        above = jnp.where(position == my_position - 1, slot, above)
        below = jnp.where(position == my_position + 1, slot, below)
    return my_slot, lax.axis_index("src"), above, below


def rims_kernel(slot_ref, tile_ref, col_ref, sent_ref, rows_ref, sems):
    copies = [
        pltpu.make_async_copy(tile_ref.at[pl.ds(start, HALO)], rows_ref.at[pl.ds(place, HALO)], sems.at[number])
        for number, (start, place) in enumerate(((0, 0), (TILE_PX - HALO, HALO)))
    ]
    for copy in copies:
        copy.start()
    my_slot, my_src, above, below = places(slot_ref)
    sent_ref[...] = jnp.zeros(sent_ref.shape, jnp.bfloat16)
    for copy in copies:
        copy.wait()
    rims = dot(rows_ref[...], col_ref[...]).astype(jnp.bfloat16)

    @pl.when(above >= 0)
    def _():
        sent_ref[above] = rims[:HALO]

    @pl.when(below >= 0)
    def _():
        sent_ref[below] = rims[HALO:]


SCALARS = pl.BlockSpec(memory_space=pltpu.SMEM)
WHOLE = pl.BlockSpec(memory_space=pltpu.VMEM)
LEFT_THERE = pl.BlockSpec(memory_space=pl.ANY)


def make_rims(slot_pos, tile, col):
    return pl.pallas_call(
        rims_kernel,
        out_shape=jax.ShapeDtypeStruct((TILES, HALO, 128), jnp.bfloat16),
        in_specs=[SCALARS, LEFT_THERE, WHOLE],
        out_specs=WHOLE,
        scratch_shapes=[pltpu.VMEM((2 * HALO, TILE_PX), jnp.bfloat16), pltpu.SemaphoreType.DMA((2,))],
        interpret=INTERPRET,
        name="rims",
    )(slot_pos, tile, col)


def fields_kernel(
    slot_ref, ints_ref, got_ref, own_ref, pupil_ref, small_ref, grids_ref, grid_yt_ref, row_ref, target_hbm,
    resist_hbm, back_ref, sent_ref,
    target_ref, resist_ref, spec_ref, field_ref, fold_ref, grad_ref, sems,
):
    fetch = pltpu.make_async_copy(target_hbm, target_ref, sems.at[0])
    fetch.start()
    my_slot, my_src, above, below = places(slot_ref)
    unfold = small_ref[:, 0:128]
    left = small_ref[:, 128:320]
    right = small_ref[:, 384:640]
    left_t = small_ref[:, 640:768]
    rim_table = small_ref[:128, 768:1024]
    unfold_t = small_ref[128:, 768:1024]
    lanes = small_ref[:128, 1024:1152]
    lanes2 = jnp.concatenate([lanes, lanes], axis=1)
    low = low_lanes((128, 128))
    low_w = low_lanes((64, 128))
    up = jnp.where(above >= 0, got_ref[jnp.maximum(above, 0)].astype(jnp.float32), 0.0)
    down = jnp.where(below >= 0, got_ref[jnp.maximum(below, 0)].astype(jnp.float32), 0.0)
    rims = jnp.concatenate([up, down], axis=0).astype(jnp.bfloat16)
    moments = own_ref[...] + dot(rim_table, jnp.concatenate([rims, rims], axis=0))
    half = dot(jnp.concatenate([unfold, unfold], axis=1), jnp.concatenate(halves(moments), axis=0))
    by_cos, by_sin = half[:FREQ], half[FREQ:]
    spec_ref[0] = dot_t(jnp.concatenate(halves(jnp.where(low, by_cos, -by_sin)), axis=1), lanes2)
    spec_ref[1] = dot_t(jnp.concatenate(halves(jnp.where(low, -by_sin, -by_cos)), axis=1), lanes2)
    coarse = jnp.zeros((GRID, GRID), jnp.float32)
    for source in range(SOURCES):
        shift_a = ints_ref[source, 0]
        shift_b = ints_ref[source, 1]
        rows = pl.ds(32 - shift_a, 64)
        spec_re = spec_ref[0, rows, :]
        spec_im = spec_ref[1, rows, :]
        near = lax.rem(96 + shift_b, 128)
        far = 32 + shift_b
        window = jnp.where(low_w, pltpu.roll(spec_re, near, 1), pltpu.roll(spec_im, far, 1))
        amp = pupil_ref[0] * window + pupil_ref[1] * pltpu.roll(window, 64, 1)
        amp_h, amp_l = halves(amp)
        both = dot(left, jnp.concatenate([amp_h, amp_l, amp_h], axis=0))
        swapped = pltpu.roll(both[GRID:], 64, 1)
        line = both[:GRID] + jnp.where(low, -swapped, swapped)
        line_h, line_l = halves(line)
        field = dot(jnp.concatenate([line_h, line_h], axis=1), right) + dot(line_l, right[:128])
        field_ref[source] = field
        weight = ints_ref[source, 2].astype(jnp.float32) * (1.0 / (4.0 * SOURCES))
        squared = field * field
        coarse = coarse + weight * (squared[:, :GRID] + squared[:, GRID:])
    coarse_h, coarse_l = halves(coarse)
    coarse_hh = jnp.concatenate([coarse_h, coarse_h], axis=0)
    grid_x = grids_ref[:, 256:512]
    fetch.wait()
    chunk = 256
    for place in range(TILE_PX // chunk):
        rows = pl.ds(place * chunk, chunk)
        rows_y = dot(grids_ref[rows, 0:256], coarse_hh) + dot(grids_ref[rows, 0:128], coarse_l)
        rows_h, rows_l = halves(rows_y)
        intensity = dot_t(jnp.concatenate([rows_h, rows_h], axis=1), grid_x) + dot_t(rows_l, grid_x[:, :GRID])
        resist = jax.nn.sigmoid(STEEPNESS * (intensity - THRESHOLD))
        resist_ref[rows, :] = resist
        wanted = target_ref[rows, :].astype(jnp.float32)
        adjoint = ((2.0 * STEEPNESS) * (resist - wanted) * resist * (1.0 - resist)).astype(jnp.bfloat16)
        folded = dot(adjoint, grid_x)
        fold_ref[rows, :] = jnp.concatenate(halves(folded[:, :GRID] + folded[:, GRID:]), axis=1)
    mine = pl.multiple_of(my_src * ROWS, ROWS)
    keep = pltpu.make_async_copy(resist_ref.at[pl.ds(mine, ROWS)], resist_hbm, sems.at[1])
    keep.start()
    adjoint4 = dot(grid_yt_ref[...], fold_ref[...])
    adjoint2 = adjoint4[:GRID] + adjoint4[GRID:]
    coarse_adjoint = 2.0 * (adjoint2[:, :GRID] + adjoint2[:, GRID:])
    grad_ref[...] = jnp.zeros(grad_ref.shape, jnp.float32)
    for source in range(SOURCES):
        shift_a = ints_ref[source, 0]
        shift_b = ints_ref[source, 1]
        weight = ints_ref[source, 2].astype(jnp.float32) * (1.0 / (4.0 * SOURCES))
        weighted = weight * coarse_adjoint
        dfield_h, dfield_l = halves(field_ref[source] * jnp.concatenate([weighted, weighted], axis=1))
        dline2 = dot_t(dfield_h, right)
        dline = dline2[:, :128] + dline2[:, 128:] + dot_t(dfield_l, right[:128])
        damp4 = dot(left_t, jnp.concatenate(halves(dline), axis=1))
        damp2 = damp4[:128] + damp4[128:]
        damp1 = damp2[:, :128] + damp2[:, 128:]
        swapped = pltpu.roll(damp1[64:], 64, 1)
        damp = damp1[:64] + jnp.where(low_w, swapped, -swapped)
        grad = pupil_ref[0] * damp - pupil_ref[1] * pltpu.roll(damp, 64, 1)
        rows = pl.ds(32 - shift_a, 64)
        grad_ref[0, rows, :] += pltpu.roll(jnp.where(low_w, grad, 0.0), 32 - shift_b, 1)
        grad_ref[1, rows, :] += pltpu.roll(jnp.where(low_w, 0.0, grad), lax.rem(96 - shift_b, 128), 1)
    grads = jnp.concatenate([grad_ref[0], grad_ref[1]], axis=0)
    folded = dot(jnp.concatenate(halves(grads), axis=1), jnp.concatenate([lanes, lanes], axis=0))
    fold_re, fold_im = folded[:FREQ], folded[FREQ:]
    packed = jnp.concatenate(
        [jnp.where(low, fold_re, -fold_im), jnp.where(low, -fold_im, -fold_re)], axis=0
    )
    packed = dot(jnp.concatenate([unfold_t, unfold_t], axis=1), jnp.concatenate(halves(packed), axis=0))
    first = my_src == 0
    edge_rows = row_ref[pl.ds(pl.multiple_of(jnp.where(first, EXT_PX - HALO, 0), HALO), HALO), :]
    mine_rows = row_ref[pl.ds(pl.multiple_of(HALO + my_src * ROWS, HALO), ROWS), :]
    tables = jnp.concatenate([edge_rows, mine_rows], axis=0)
    back = jnp.dot(tables, packed, precision=lax.Precision.HIGHEST, preferred_element_type=jnp.float32)
    sent_ref[...] = jnp.zeros(sent_ref.shape, jnp.bfloat16)
    goes_to = jnp.where(first, below, above)

    @pl.when(goes_to >= 0)
    def _():
        sent_ref[goes_to // 2] = back[:HALO].astype(jnp.bfloat16)

    back_ref[...] = back[HALO:]
    keep.wait()


def make_fields(slot_pos, ints, got, own, pupil, row_table, target):
    return pl.pallas_call(
        fields_kernel,
        out_shape=(
            jax.ShapeDtypeStruct((ROWS, TILE_PX), jnp.float32),
            jax.ShapeDtypeStruct((ROWS, 128), jnp.float32),
            jax.ShapeDtypeStruct((TILES // 2, HALO, 128), jnp.bfloat16),
        ),
        in_specs=[SCALARS, SCALARS] + [WHOLE] * 7 + [LEFT_THERE],
        out_specs=[LEFT_THERE, WHOLE, WHOLE],
        scratch_shapes=[
            pltpu.VMEM((TILE_PX, TILE_PX), jnp.bfloat16),
            pltpu.VMEM((TILE_PX, TILE_PX), jnp.float32),
            pltpu.VMEM((2, FREQ, FREQ), jnp.float32),
            pltpu.VMEM((SOURCES, GRID, 2 * GRID), jnp.float32),
            pltpu.VMEM((TILE_PX, 2 * GRID), jnp.bfloat16),
            pltpu.VMEM((2, FREQ, FREQ), jnp.float32),
            pltpu.SemaphoreType.DMA((2,)),
        ],
        compiler_params=pltpu.CompilerParams(vmem_limit_bytes=48 * 1024 * 1024),
        interpret=INTERPRET,
        name="fields",
    )(
        slot_pos, ints, got, own, pupil, jnp.asarray(SMALL), jnp.asarray(GRIDS), jnp.asarray(GRID_YT), row_table, target
    )


def steps_kernel(slot_ref, got_ref, other_ref, back_ref, col_ref, out_ref):
    my_slot, my_src, above, below = places(slot_ref)
    first = my_src == 0
    last = my_src == SRC_DEVICES - 1
    comes_from = jnp.where(first, above, below)
    place = jnp.maximum(comes_from, 0) // 2
    same_core = lax.rem(jnp.maximum(comes_from, 0), 2) == lax.rem(my_slot, 2)
    rim = jnp.where(same_core, got_ref[place].astype(jnp.float32), other_ref[place].astype(jnp.float32))
    top = jnp.where(first & (above >= 0), rim, 0.0)
    bottom = jnp.where(last & (below >= 0), rim, 0.0)
    back = -LEARN_RATE * (back_ref[...] + jnp.concatenate([top, bottom], axis=0))
    high, low = halves(back)
    out_ref[...] = dot_t(high, col_ref[...]) + dot_t(low, col_ref[...])


def make_steps(slot_pos, got, other, back, col):
    return pl.pallas_call(
        steps_kernel,
        out_shape=jax.ShapeDtypeStruct((ROWS, TILE_PX), jnp.float32),
        in_specs=[SCALARS] + [WHOLE] * 4,
        out_specs=WHOLE,
        interpret=INTERPRET,
        name="steps",
    )(slot_pos, got, other, back, col)


def pupil_tables(pupil_phase):
    window = pupil_phase[32:96, 32:96]
    real = jnp.where(DISC, jnp.cos(window), 0.0) * SCALE
    imag = jnp.where(DISC, jnp.sin(window), 0.0) * SCALE
    return jnp.stack([jnp.concatenate([real, real], axis=1), jnp.concatenate([-imag, imag], axis=1)])


def own_moments(tile, col, row_table):
    half = jnp.dot(tile, col, preferred_element_type=jnp.float32)
    rows = row_table[HALO : HALO + TILE_PX]
    return lax.dot_general(
        rows, half, (((0,), (0,)), ((), ())), precision=lax.Precision.HIGHEST, preferred_element_type=jnp.float32
    )


def all_sources(src_shift, src_weight):
    ints = jnp.concatenate([src_shift, src_weight[:, None]], axis=1)
    swap = lambda value, mask: lax.ppermute(value, "src", [(i, i ^ mask) for i in range(SRC_DEVICES)])
    near = jnp.concatenate([ints] + [swap(ints, mask) for mask in (1, 2, 3)], axis=0)
    return jnp.concatenate([near, swap(near, 4)], axis=0)


def per_device(mask_tiles, slot_pos, src_shift, src_weight, pupil_phase, target):
    ints = all_sources(src_shift, src_weight)
    col = jnp.asarray(COL)
    row_table = lax.optimization_barrier(jnp.asarray(ROW_F32))
    tile = mask_tiles[0]
    got = lax.all_to_all(make_rims(slot_pos, tile, col), "tile", 0, 0, tiled=True)
    own = own_moments(tile, col, row_table)
    resist, back, sent = make_fields(slot_pos, ints, got, own, pupil_tables(pupil_phase), row_table, target[0])
    cores = [[2 * chip + core for chip in range(TILES // 2)] for core in range(2)]
    got = lax.all_to_all(sent, "tile", 0, 0, tiled=True, axis_index_groups=cores)
    other = lax.ppermute(got, "tile", [(i, i ^ 1) for i in range(TILES)])
    return (resist[None], make_steps(slot_pos, got, other, back, col)[None])


def solution(mesh):
    return jax.shard_map(
        per_device,
        mesh=mesh,
        in_specs=(P("tile", None, None), P(), P("src", None), P("src"), P(), P("tile", None, None)),
        out_specs=(P("tile", "src", None), P("tile", "src", None)),
        check_vma=False,
    )
```

time: 86.9 us -> 70.6 us (0.81)
  blocking collectives: 25.5 us -> 12.8 us
  between operations: 6.07 us -> 0.82 us
  waiting for transfers between devices: 3.95 us -> 8.96 us
  other arithmetic: 3.77 us -> 1.03 us
  starting transfers between devices: 18.8 us -> 21.4 us
  local copies, waits for them, and re-layouts: 7.44 us -> 5.06 us
  matrix products: 4.47 us -> 3.57 us
    all_to_all x1, blocking collectives: 25.5 us -> 12.8 us  [per_device(): lax.all_to_all(sent, 'tile', 0, 0, tiled=True, axis_index_groups=cores)]
    ppermute x3 -> x5, waiting for transfers between devices: 3.25 us -> 6.1 us  [the longest x4 4.93 us: all_sources(): lax.ppermute(value, 'src', [(i, i ^ mask) for i in range(SRC_DEVICES)])]
    reduce_sum x2 -> x0, other arithmetic: 2.59 us -> none  [the longest x1 1.3 us: places(): below = jnp.sum(jnp.where(slot_pos == my_position + 1, slot_ids, 0))]
    all_to_all x1, waiting for transfers between devices: 0.71 us -> 2.87 us  [per_device(): lax.all_to_all(make_rims(slot_pos, tile, col), 'tile', 0, 0, tiled=True)]
    ppermute x3 -> x5, starting transfers between devices: 9.31 us -> 11.3 us  [the longest x4 8.66 us: all_sources(): lax.ppermute(value, 'src', [(i, i ^ mask) for i in range(SRC_DEVICES)])]
    another operation x1 -> x0, local copies, waits for them, and re-layouts: 1.95 us -> none  [places(): jnp.stack([above, below, has_above.astype(jnp.int32), has_below.astype(jn...]
    dot_general x2, matrix products: 4.47 us -> 3.57 us  [the longest x1 2.57 us: own_moments(): half = jnp.dot(tile, col, preferred_element_type=jnp.float32)]
    unnamed x33 -> x27, local copies, waits for them, and re-layouts: 5.4 us -> 4.87 us
  transfers between devices with their start and end apart: 4 -> 6, of which waited for: 3 -> 3; matrix products, arithmetic and copies ran while one was open for 11% -> 6% of each run, Pallas kernels for 3% -> 4%
where the time goes in v3:
time: 70.6 us; the launch traced here: 70.2 us
  starting transfers between devices  21.4 us (30%)
  Pallas kernels  16.6 us (24%)
  blocking collectives  12.8 us (18%)
  waiting for transfers between devices  8.96 us (13%)
  local copies, waits for them, and re-layouts  5.06 us (7%)
  matrix products  3.57 us (5%)
  other arithmetic  1.03 us (1%)
  between operations  0.82 us (1%)
    all_to_all x1, blocking collectives, per_device(): lax.all_to_all(sent, 'tile', 0, 0, tiled=True, axis_index_groups=cores)  12.8 us
    pallas_call x1, Pallas kernels, make_fields(): pl.pallas_call(fields_kernel, out_shape=(jax.ShapeDtypeStruct((ROWS, TILE...  11.3 us
    all_to_all x1, starting transfers between devices, per_device(): lax.all_to_all(make_rims(slot_pos, tile, col), 'tile', 0, 0, tiled=True)  10 us
    ppermute x4, starting transfers between devices, all_sources(): lax.ppermute(value, 'src', [(i, i ^ mask) for i in range(SRC_DEVICES)])  8.66 us
    ppermute x4, waiting for transfers between devices, all_sources(): lax.ppermute(value, 'src', [(i, i ^ mask) for i in range(SRC_DEVICES)])  4.93 us
    unnamed x27, local copies, waits for them, and re-layouts  4.87 us
    pallas_call x1, Pallas kernels, make_rims(): pl.pallas_call(rims_kernel, out_shape=jax.ShapeDtypeStruct((TILES, HALO,...  3.02 us
    all_to_all x1, waiting for transfers between devices, per_device(): lax.all_to_all(make_rims(slot_pos, tile, col), 'tile', 0, 0, tiled=True)  2.87 us
  transfers between devices with their start and end apart: 6, of which 3 were waited for; matrix products, arithmetic and copies ran while one was open for 6% of the time, Pallas kernels for 4%

profile of v3, /device:TPU:1, one launch (start us, length us, event | category | flops | bytes accessed | tf_op | source)
XLA Modules:
  0.0 70.2 jit_solution(8733620349940024565)
XLA Ops:
  0.6 0.0 copy-start.11
  0.6 0.0 copy-start.10
  0.7 0.8 %copy.15 = s32[2,2]{0,1:T(2,128)S(1)} copy(s32[2,2]{1,0:T(2,128)} %param.14) | data formatting | bytes 32 | tf_op args[2]
  1.5 0.7 pad_add_fusion
  2.1 3.6 %collective-permute-start.2 = (s32[2,3]{0,1:T(4,128)S(1)}, s32[2,3]{0,1:T(4,128)S(1)}, u32[]{:S(2)}, u32[]{:S(2)}) collective-permute-start(s32[2,3]{0,1:T(4,128)S(1)} %pad_add_fusion), channel_id=1, source_target_pairs={{0,96},{32,64},{64,32},{96,0},{128,224},{160,192},{192,160},{224,1... | collective-permute-start | bytes 80 | tf_op jit(solution)/shard_map/ppermute | solution.py:346
  5.7 0.3 collective-permute-start.1
  6.0 0.3 collective-permute-start
  6.3 0.0 copy-start.7
  6.3 3.0 %rims.1 = bf16[32,64,128]{2,1,0:T(8,128)(2,1)} custom-call(s32[32]{0:T(128)} %slot_ref.5, bf16[1024,1024]{1,0:T(8,128)(2,1)} %bitcast.14, bf16[1024,128]{1,0:T(8,128)(2,1)} %constant.16.clone.col_ref), custom_call_target="tpu_custom_call" | custom-call | tf_op jit(solution)/shard_map/rims/pallas_call | solution.py:155
  9.4 0.0 copy-start
  9.4 10.0 %all-to-all-start = ((bf16[32,64,128]{2,1,0:T(8,128)(2,1)}), bf16[32,64,128]{2,1,0:T(8,128)(2,1)S(1)}, u32[]{:S(2)}, u32[]{:S(2)}) async-start(bf16[32,64,128]{2,1,0:T(8,128)(2,1)} %rims.1), calls=%async_computation | async-start | bytes 1048576 | tf_op jit(solution)/shard_map/all_to_all | solution.py:356
  19.4 0.0 copy-done.11
  19.4 0.0 copy-done.10
  19.4 0.2 select_multiply_fusion.1
  19.7 0.0 copy-start.12
  19.7 0.1 maximum_bitcast_fusion
  19.8 0.0 copy-done.7
  19.8 0.0 copy-start.1
  19.8 0.0 copy-start.6
  19.8 2.6 %fusion.2 = f32[128,1024]{1,0:T(8,128)S(1)} fusion(bf16[1024,128]{1,0:T(8,128)(2,1)S(1)} %copy-done.7, bf16[1,1024,1024]{2,1,0:T(8,128)(2,1)} %param.12), kind=kOutput, calls=%fused_computation.9 | convolution fusion | flops 268435456 | bytes 2883584 | tf_op jit(solution)/shard_map/dot_general | solution.py:337
  22.4 0.0 copy-done
  22.4 1.0 %fusion.own_ref = f32[128,128]{1,0:T(8,128)S(1)} fusion(f32[128,1024]{1,0:T(8,128)S(1)} %fusion.2, f32[1152,128]{1,0:T(8,128)S(1)} %copy-done), kind=kOutput, calls=%fused_computation | convolution fusion | flops 201326592 | bytes 1114112 | tf_op jit(solution)/shard_map/dot_general | solution.py:339
  23.4 0.0 collective-permute-done.2
  23.4 0.0 collective-permute-done.1
  23.4 0.0 collective-permute-done
  23.4 0.0 copy-done.12
  23.4 0.1 pad_add_fusion.1
  23.5 4.4 %collective-permute-start.3 = (s32[8,3]{0,1:T(4,128)S(1)}, s32[8,3]{0,1:T(4,128)S(1)}, u32[]{:S(2)}, u32[]{:S(2)}) collective-permute-start(s32[8,3]{0,1:T(4,128)S(1)} %pad_add_fusion.1), channel_id=1, source_target_pairs={{0,128},{32,160},{64,192},{96,224},{128,0},{160,32},{192,64},{224,... | collective-permute-start | bytes 296 | tf_op jit(solution)/shard_map/ppermute | solution.py:346
  27.9 4.9 %collective-permute-done.3 = s32[8,3]{0,1:T(4,128)S(1)} collective-permute-done((s32[8,3]{0,1:T(4,128)S(1)}, s32[8,3]{0,1:T(4,128)S(1)}, u32[]{:S(2)}, u32[]{:S(2)}) %collective-permute-start.3) | collective-permute-done | bytes 128 | tf_op jit(solution)/shard_map/ppermute | solution.py:346
  32.9 0.1 concatenate.18
  33.0 0.1 copy.16.ints_ref
  33.0 2.9 %all-to-all-done.got_ref = bf16[32,64,128]{2,1,0:T(8,128)(2,1)S(1)} async-done(((bf16[32,64,128]{2,1,0:T(8,128)(2,1)}), bf16[32,64,128]{2,1,0:T(8,128)(2,1)S(1)}, u32[]{:S(2)}, u32[]{:S(2)}) %all-to-all-start) | async-done | bytes 524320 | tf_op jit(solution)/shard_map/all_to_all | solution.py:356
  35.9 0.0 copy-done.1
  35.9 0.0 copy-done.6
  35.9 0.0 copy-start.2
  35.9 1.2 %copy-done.2 = bf16[1024,512]{1,0:T(8,128)(2,1)S(1)} copy-done((bf16[1024,512]{1,0:T(8,128)(2,1)S(1)}, bf16[1024,512]{1,0:T(8,128)(2,1)}, u32[]{:S(2)}) %copy-start.2) | copy-done | bytes 1048600
  37.2 0.0 copy-start.3
  37.2 1.1 %copy-done.3 = bf16[256,1152]{1,0:T(8,128)(2,1)S(1)} copy-done((bf16[256,1152]{1,0:T(8,128)(2,1)S(1)}, bf16[256,1152]{1,0:T(8,128)(2,1)}, u32[]{:S(2)}) %copy-start.3) | copy-done | bytes 589848
  38.2 0.0 copy-start.4
  38.2 1.0 %copy-done.4 = bf16[256,1024]{1,0:T(8,128)(2,1)S(1)} copy-done((bf16[256,1024]{1,0:T(8,128)(2,1)S(1)}, bf16[256,1024]{1,0:T(8,128)(2,1)}, u32[]{:S(2)}) %copy-start.4) | copy-done | bytes 524312
  39.3 11.3 %fields.1 = (f32[128,1024]{1,0:T(8,128)}, f32[128,128]{1,0:T(8,128)S(1)}, bf16[16,64,128]{2,1,0:T(8,128)(2,1)S(1)}) custom-call(s32[32]{0:T(128)S(1)} %copy-done.6, s32[16,3]{1,0:T(8,128)S(1)} %copy.16.ints_ref, bf16[32,64,128]{2,1,0:T(8,128)(2,1)S(1)} %all-to-all-done.got_ref, f32[128,128]{1,0:T(8,128)S(1)} %fusion.own_ref, ...), custom_call_target="tpu_custom_call" | custom-call | tf_op jit(solution)/shard_map/fields/pallas_call | solution.py:277
  50.6 0.0 copy-start.5
  50.6 12.8 %all_to_all.10.got_ref = bf16[16,64,128]{2,1,0:T(8,128)(2,1)S(1)} all-to-all(bf16[16,64,128]{2,1,0:T(8,128)(2,1)S(1)} %get-tuple-element.6), channel_id=1, replica_groups={{0,2,4,6,8,10,12,14,16,18,20,22,24,26,28,30},{1,3,5,7,9,11,13,15,17,19,..., dimensions={0} | all-to-all | bytes 524288 | tf_op jit(solution)/shard_map/all_to_all | solution.py:360
  63.4 0.0 copy-done.5
  63.4 0.0 copy-start.8
  63.4 2.7 %collective-permute-start.4 = (bf16[16,64,128]{2,1,0:T(8,128)(2,1)S(1)}, bf16[16,64,128]{2,1,0:T(8,128)(2,1)S(1)}, u32[]{:S(2)}, u32[]{:S(2)}) collective-permute-start(bf16[16,64,128]{2,1,0:T(8,128)(2,1)S(1)} %all_to_all.10.got_ref), channel_id=1, source_target_pairs={{0,1},{1,0},{2,3},{3,2},{4,5},{5,4},{6,7},{7,6},{8,9},{9,8},{10,11... | collective-permute-start | bytes 786440 | tf_op jit(solution)/shard_map/ppermute | solution.py:361
  66.1 1.2 %collective-permute-done.4.other_ref = bf16[16,64,128]{2,1,0:T(8,128)(2,1)S(1)} collective-permute-done((bf16[16,64,128]{2,1,0:T(8,128)(2,1)S(1)}, bf16[16,64,128]{2,1,0:T(8,128)(2,1)S(1)}, u32[]{:S(2)}, u32[]{:S(2)}) %collective-permute-start.4) | collective-permute-done | bytes 262176 | tf_op jit(solution)/shard_map/ppermute | solution.py:361
  67.2 0.0 copy-start.9
  67.2 0.0 copy-done.8
  67.2 0.7 copy-done.9
  67.9 2.3 %steps.1 = f32[128,1024]{1,0:T(8,128)} custom-call(s32[32]{0:T(128)} %slot_ref.5, bf16[16,64,128]{2,1,0:T(8,128)(2,1)} %copy-done.8, bf16[16,64,128]{2,1,0:T(8,128)(2,1)} %copy-done.9, f32[128,128]{1,0:T(8,128)} %copy-done.5, bf16[1024,128]{1,0:T(8,128)(2,1)} %constant.16.clone.col_ref), custom_call_target="tpu_custom_call" | custom-call | tf_op jit(solution)/shard_map/steps/pallas_call | solution.py:319
  (1 shorter events, 0.0 us)
Async XLA Ops:
  0.6 18.8 %copy-start.11 = (pred[64,64]{1,0:T(32,128)(4,1)S(1)}, pred[64,64]{1,0:T(32,128)(4,1)}, u32[]{:S(2)}) copy-start(pred[64,64]{1,0:T(32,128)(4,1)} %constant.18.clone) | copy-start | bytes 12292
  0.6 18.8 %copy-start.10 = (f32[128,128]{1,0:T(8,128)S(1)}, f32[128,128]{1,0:T(8,128)}, u32[]{:S(2)}) copy-start(f32[128,128]{1,0:T(8,128)} %param.16) | copy-start | bytes 196612
  2.1 21.3 %collective-permute-start.2 = (s32[2,3]{0,1:T(4,128)S(1)}, s32[2,3]{0,1:T(4,128)S(1)}, u32[]{:S(2)}, u32[]{:S(2)}) collective-permute-start(s32[2,3]{0,1:T(4,128)S(1)} %pad_add_fusion), channel_id=1, source_target_pairs={{0,96},{32,64},{64,32},{96,0},{128,224},{160,192},{192,160},{224,1... | collective-permute-start | bytes 80 | tf_op jit(solution)/shard_map/ppermute | solution.py:346
  5.7 17.7 %collective-permute-start.1 = (s32[2,3]{0,1:T(4,128)S(1)}, s32[2,3]{0,1:T(4,128)S(1)}, u32[]{:S(2)}, u32[]{:S(2)}) collective-permute-start(s32[2,3]{0,1:T(4,128)S(1)} %pad_add_fusion), channel_id=1, source_target_pairs={{0,64},{32,96},{64,0},{96,32},{128,192},{160,224},{192,128},{224,1... | collective-permute-start | bytes 80 | tf_op jit(solution)/shard_map/ppermute | solution.py:346
  6.0 17.4 %collective-permute-start = (s32[2,3]{0,1:T(4,128)S(1)}, s32[2,3]{0,1:T(4,128)S(1)}, u32[]{:S(2)}, u32[]{:S(2)}) collective-permute-start(s32[2,3]{0,1:T(4,128)S(1)} %pad_add_fusion), channel_id=1, source_target_pairs={{0,32},{32,0},{64,96},{96,64},{128,160},{160,128},{192,224},{224,1... | collective-permute-start | bytes 80 | tf_op jit(solution)/shard_map/ppermute | solution.py:346
  6.3 13.4 %copy-start.7 = (bf16[1024,128]{1,0:T(8,128)(2,1)S(1)}, bf16[1024,128]{1,0:T(8,128)(2,1)}, u32[]{:S(2)}) copy-start(bf16[1024,128]{1,0:T(8,128)(2,1)} %constant.16.clone.col_ref) | copy-start | bytes 786436
  9.4 13.0 %copy-start = (f32[1152,128]{1,0:T(8,128)S(1)}, f32[1152,128]{1,0:T(8,128)}, u32[]{:S(2)}) copy-start(f32[1152,128]{1,0:T(8,128)} %constant.17.clone.row_ref) | copy-start | bytes 1769476
  9.4 26.5 %all-to-all-start = ((bf16[32,64,128]{2,1,0:T(8,128)(2,1)}), bf16[32,64,128]{2,1,0:T(8,128)(2,1)S(1)}, u32[]{:S(2)}, u32[]{:S(2)}) async-start(bf16[32,64,128]{2,1,0:T(8,128)(2,1)} %rims.1), calls=%async_computation | async-start | bytes 1048576 | tf_op jit(solution)/shard_map/all_to_all | solution.py:356
  19.7 3.8 %copy-start.12 = (s32[2]{0:T(128)S(1)}, s32[2]{0:T(128)}, u32[]{:S(2)}) copy-start(s32[2]{0:T(128)} %param.15) | copy-start | bytes 28
  19.8 16.2 %copy-start.1 = (bf16[1,1024,1024]{2,1,0:T(8,128)(2,1)S(1)}, bf16[1,1024,1024]{2,1,0:T(8,128)(2,1)}, u32[]{:S(2)}) copy-start(bf16[1,1024,1024]{2,1,0:T(8,128)(2,1)} %param.17) | copy-start | bytes 6291460
  19.8 16.1 %copy-start.6 = (s32[32]{0:T(128)S(1)}, s32[32]{0:T(128)}, u32[]{:S(2)}) copy-start(s32[32]{0:T(128)} %slot_ref.5) | copy-start | bytes 388
  23.5 9.4 %collective-permute-start.3 = (s32[8,3]{0,1:T(4,128)S(1)}, s32[8,3]{0,1:T(4,128)S(1)}, u32[]{:S(2)}, u32[]{:S(2)}) collective-permute-start(s32[8,3]{0,1:T(4,128)S(1)} %pad_add_fusion.1), channel_id=1, source_target_pairs={{0,128},{32,160},{64,192},{96,224},{128,0},{160,32},{192,64},{224,... | collective-permute-start | bytes 296 | tf_op jit(solution)/shard_map/ppermute | solution.py:346
  35.9 1.2 %copy-start.2 = (bf16[1024,512]{1,0:T(8,128)(2,1)S(1)}, bf16[1024,512]{1,0:T(8,128)(2,1)}, u32[]{:S(2)}) copy-start(bf16[1024,512]{1,0:T(8,128)(2,1)} %constant.20.clone.grids_ref) | copy-start | bytes 3145732
  37.2 1.1 %copy-start.3 = (bf16[256,1152]{1,0:T(8,128)(2,1)S(1)}, bf16[256,1152]{1,0:T(8,128)(2,1)}, u32[]{:S(2)}) copy-start(bf16[256,1152]{1,0:T(8,128)(2,1)} %constant.19.clone.small_ref) | copy-start | bytes 1769476
  38.2 1.0 %copy-start.4 = (bf16[256,1024]{1,0:T(8,128)(2,1)S(1)}, bf16[256,1024]{1,0:T(8,128)(2,1)}, u32[]{:S(2)}) copy-start(bf16[256,1024]{1,0:T(8,128)(2,1)} %constant.21.clone.grid_yt_ref) | copy-start | bytes 1572868
  50.6 12.8 %copy-start.5 = (f32[128,128]{1,0:T(8,128)}, f32[128,128]{1,0:T(8,128)S(1)}, u32[]{:S(2)}) copy-start(f32[128,128]{1,0:T(8,128)S(1)} %get-tuple-element.7.back_ref) | copy-start | bytes 196612
  63.4 3.9 %copy-start.8 = (bf16[16,64,128]{2,1,0:T(8,128)(2,1)}, bf16[16,64,128]{2,1,0:T(8,128)(2,1)S(1)}, u32[]{:S(2)}) copy-start(bf16[16,64,128]{2,1,0:T(8,128)(2,1)S(1)} %all_to_all.10.got_ref) | copy-start | bytes 786436
  63.4 3.9 %collective-permute-start.4 = (bf16[16,64,128]{2,1,0:T(8,128)(2,1)S(1)}, bf16[16,64,128]{2,1,0:T(8,128)(2,1)S(1)}, u32[]{:S(2)}, u32[]{:S(2)}) collective-permute-start(bf16[16,64,128]{2,1,0:T(8,128)(2,1)S(1)} %all_to_all.10.got_ref), channel_id=1, source_target_pairs={{0,1},{1,0},{2,3},{3,2},{4,5},{5,4},{6,7},{7,6},{8,9},{9,8},{10,11... | collective-permute-start | bytes 786440 | tf_op jit(solution)/shard_map/ppermute | solution.py:361
  67.2 0.7 copy-start.9

commit v4 on v3

--- a/solution.py
+++ b/solution.py
@@ -91,7 +91,6 @@
 )
 ROWS_Y = (HALO + np.arange(TILE_PX)) / 9.0
 GRIDS = np.concatenate(split(interpolation(ROWS_Y)) + split(interpolation(np.arange(TILE_PX) / 8.0)), axis=1)
-GRID_YT = np.concatenate(split(interpolation(ROWS_Y).T), axis=0)
 DISC = (np.arange(64)[:, None] - 32) ** 2 + (np.arange(64)[None] - 32) ** 2 <= PUPIL_R * PUPIL_R
 
 
@@ -124,53 +123,136 @@
     return my_slot, lax.axis_index("src"), above, below
 
 
-def rims_kernel(slot_ref, tile_ref, col_ref, sent_ref, rows_ref, sems):
+def rims_kernel(slot_ref, tile_hbm, col_hbm, sent_hbm, rows_ref, col_ref, rims_ref, sems):
     copies = [
-        pltpu.make_async_copy(tile_ref.at[pl.ds(start, HALO)], rows_ref.at[pl.ds(place, HALO)], sems.at[number])
-        for number, (start, place) in enumerate(((0, 0), (TILE_PX - HALO, HALO)))
+        pltpu.make_async_copy(col_hbm, col_ref, sems.at[0]),
+        pltpu.make_async_copy(tile_hbm.at[pl.ds(0, HALO)], rows_ref.at[pl.ds(0, HALO)], sems.at[1]),
+        pltpu.make_async_copy(
+            tile_hbm.at[pl.ds(TILE_PX - HALO, HALO)], rows_ref.at[pl.ds(HALO, HALO)], sems.at[2]
+        ),
     ]
     for copy in copies:
         copy.start()
     my_slot, my_src, above, below = places(slot_ref)
-    sent_ref[...] = jnp.zeros(sent_ref.shape, jnp.bfloat16)
     for copy in copies:
         copy.wait()
-    rims = dot(rows_ref[...], col_ref[...]).astype(jnp.bfloat16)
-
-    @pl.when(above >= 0)
-    def _():
-        sent_ref[above] = rims[:HALO]
-
-    @pl.when(below >= 0)
-    def _():
-        sent_ref[below] = rims[HALO:]
+    rims_ref[...] = dot(rows_ref[...], col_ref[...]).astype(jnp.bfloat16).reshape(2, HALO, 128)
+
+    for number, slot in enumerate((above, below)):
+
+        @pl.when(slot >= 0)
+        def _():
+            pltpu.make_async_copy(rims_ref.at[number], sent_hbm.at[slot], sems.at[3 + number]).start()
+
+    for number, slot in enumerate((above, below)):
+
+        @pl.when(slot >= 0)
+        def _():
+            pltpu.make_async_copy(rims_ref.at[number], sent_hbm.at[slot], sems.at[3 + number]).wait()
 
 
 SCALARS = pl.BlockSpec(memory_space=pltpu.SMEM)
 WHOLE = pl.BlockSpec(memory_space=pltpu.VMEM)
-LEFT_THERE = pl.BlockSpec(memory_space=pl.ANY)
+LEFT_THERE = pl.BlockSpec(memory_space=pltpu.MemorySpace.HBM)
+MIB = 1024 * 1024
+ALL_VMEM = 63_000_000
 
 
 def make_rims(slot_pos, tile, col):
     return pl.pallas_call(
         rims_kernel,
         out_shape=jax.ShapeDtypeStruct((TILES, HALO, 128), jnp.bfloat16),
-        in_specs=[SCALARS, LEFT_THERE, WHOLE],
-        out_specs=WHOLE,
-        scratch_shapes=[pltpu.VMEM((2 * HALO, TILE_PX), jnp.bfloat16), pltpu.SemaphoreType.DMA((2,))],
+        in_specs=[SCALARS, LEFT_THERE, LEFT_THERE],
+        out_specs=LEFT_THERE,
+        scratch_shapes=[
+            pltpu.VMEM((2 * HALO, TILE_PX), jnp.bfloat16),
+            pltpu.VMEM((TILE_PX, 128), jnp.bfloat16),
+            pltpu.VMEM((2, HALO, 128), jnp.bfloat16),
+            pltpu.SemaphoreType.DMA((5,)),
+        ],
+        compiler_params=pltpu.CompilerParams(vmem_limit_bytes=ALL_VMEM),
         interpret=INTERPRET,
         name="rims",
     )(slot_pos, tile, col)
 
 
+def prep_kernel(small_hbm, grids_hbm, flipped_hbm, right_t_hbm, small_ref, grids_ref, flipped_ref, right_t_ref, sems):
+    fetches = [
+        pltpu.make_async_copy(grids_hbm, grids_ref, sems.at[0]),
+        pltpu.make_async_copy(small_hbm.at[:, pl.ds(384, 256)], small_ref, sems.at[1]),
+    ]
+    keeps = [
+        pltpu.make_async_copy(flipped_ref, flipped_hbm, sems.at[2]),
+        pltpu.make_async_copy(right_t_ref, right_t_hbm, sems.at[3]),
+    ]
+    for fetch in fetches:
+        fetch.start()
+    fetches[0].wait()
+    flipped_ref[...] = grids_ref[...].T
+    keeps[0].start()
+    fetches[1].wait()
+    right_t_ref[...] = small_ref[...].T
+    keeps[1].start()
+    for keep in keeps:
+        keep.wait()
+
+
+def flip_tables(small, grids):
+    return pl.pallas_call(
+        prep_kernel,
+        out_shape=(
+            jax.ShapeDtypeStruct(GRIDS.shape[::-1], jnp.bfloat16),
+            jax.ShapeDtypeStruct((256, 256), jnp.bfloat16),
+        ),
+        in_specs=[LEFT_THERE] * 2,
+        out_specs=[LEFT_THERE] * 2,
+        scratch_shapes=[
+            pltpu.VMEM((256, 256), jnp.bfloat16),
+            pltpu.VMEM(GRIDS.shape, jnp.bfloat16),
+            pltpu.VMEM(GRIDS.shape[::-1], jnp.bfloat16),
+            pltpu.VMEM((256, 256), jnp.bfloat16),
+            pltpu.SemaphoreType.DMA((4,)),
+        ],
+        compiler_params=pltpu.CompilerParams(vmem_limit_bytes=ALL_VMEM),
+        interpret=INTERPRET,
+        name="prep",
+    )(small, grids)
+
+
 def fields_kernel(
-    slot_ref, ints_ref, got_ref, own_ref, pupil_ref, small_ref, grids_ref, grid_yt_ref, row_ref, target_hbm,
-    resist_hbm, back_ref, sent_ref,
-    target_ref, resist_ref, spec_ref, field_ref, fold_ref, grad_ref, sems,
+    slot_ref, ints_ref, got_hbm, own_hbm, pupil_hbm, small_hbm, right_t_hbm, grids_hbm, flipped_hbm, row_hbm, target_hbm,
+    resist_hbm, back_hbm, sent_hbm,
+    got_ref, own_ref, pupil_ref, small_ref, right_t_ref, grids_ref, flipped_ref, row_ref, target_ref,
+    back_ref, edge_ref, resist_ref, spec_ref, field_ref, fold_ref, grad_ref, sems,
 ):
-    fetch = pltpu.make_async_copy(target_hbm, target_ref, sems.at[0])
-    fetch.start()
+    first_fetches = [
+        pltpu.make_async_copy(source, target, sems.at[number])
+        for number, (source, target) in enumerate(((small_hbm, small_ref), (own_hbm, own_ref), (pupil_hbm, pupil_ref)))
+    ]
+    for fetch in first_fetches:
+        fetch.start()
     my_slot, my_src, above, below = places(slot_ref)
+    for number, slot in enumerate((above, below)):
+        first_fetches.append(
+            pltpu.make_async_copy(got_hbm.at[jnp.maximum(slot, 0)], got_ref.at[number], sems.at[3 + number])
+        )
+        first_fetches[-1].start()
+    fetches = [
+        pltpu.make_async_copy(source, target, sems.at[5 + number])
+        for number, (source, target) in enumerate(
+            (
+                (grids_hbm, grids_ref),
+                (flipped_hbm, flipped_ref),
+                (target_hbm, target_ref),
+                (right_t_hbm, right_t_ref),
+                (row_hbm, row_ref),
+            )
+        )
+    ]
+    for fetch in fetches:
+        fetch.start()
+    for fetch in first_fetches:
+        fetch.wait()
     unfold = small_ref[:, 0:128]
     left = small_ref[:, 128:320]
     right = small_ref[:, 384:640]
@@ -181,8 +263,8 @@
     lanes2 = jnp.concatenate([lanes, lanes], axis=1)
     low = low_lanes((128, 128))
     low_w = low_lanes((64, 128))
-    up = jnp.where(above >= 0, got_ref[jnp.maximum(above, 0)].astype(jnp.float32), 0.0)
-    down = jnp.where(below >= 0, got_ref[jnp.maximum(below, 0)].astype(jnp.float32), 0.0)
+    up = jnp.where(above >= 0, got_ref[0].astype(jnp.float32), 0.0)
+    down = jnp.where(below >= 0, got_ref[1].astype(jnp.float32), 0.0)
     rims = jnp.concatenate([up, down], axis=0).astype(jnp.bfloat16)
     moments = own_ref[...] + dot(rim_table, jnp.concatenate([rims, rims], axis=0))
     half = dot(jnp.concatenate([unfold, unfold], axis=1), jnp.concatenate(halves(moments), axis=0))
@@ -212,14 +294,17 @@
         coarse = coarse + weight * (squared[:, :GRID] + squared[:, GRID:])
     coarse_h, coarse_l = halves(coarse)
     coarse_hh = jnp.concatenate([coarse_h, coarse_h], axis=0)
+    for fetch in fetches[:3]:
+        fetch.wait()
     grid_x = grids_ref[:, 256:512]
-    fetch.wait()
+    grid_xt = flipped_ref[256:512, :]
+    grid_yt = flipped_ref[0:256, :]
     chunk = 256
     for place in range(TILE_PX // chunk):
         rows = pl.ds(place * chunk, chunk)
         rows_y = dot(grids_ref[rows, 0:256], coarse_hh) + dot(grids_ref[rows, 0:128], coarse_l)
         rows_h, rows_l = halves(rows_y)
-        intensity = dot_t(jnp.concatenate([rows_h, rows_h], axis=1), grid_x) + dot_t(rows_l, grid_x[:, :GRID])
+        intensity = dot(jnp.concatenate([rows_h, rows_h], axis=1), grid_xt) + dot(rows_l, grid_xt[:GRID])
         resist = jax.nn.sigmoid(STEEPNESS * (intensity - THRESHOLD))
         resist_ref[rows, :] = resist
         wanted = target_ref[rows, :].astype(jnp.float32)
@@ -227,11 +312,13 @@
         folded = dot(adjoint, grid_x)
         fold_ref[rows, :] = jnp.concatenate(halves(folded[:, :GRID] + folded[:, GRID:]), axis=1)
     mine = pl.multiple_of(my_src * ROWS, ROWS)
-    keep = pltpu.make_async_copy(resist_ref.at[pl.ds(mine, ROWS)], resist_hbm, sems.at[1])
+    keep = pltpu.make_async_copy(resist_ref.at[pl.ds(mine, ROWS)], resist_hbm, sems.at[10])
     keep.start()
-    adjoint4 = dot(grid_yt_ref[...], fold_ref[...])
+    adjoint4 = dot(grid_yt, fold_ref[...])
     adjoint2 = adjoint4[:GRID] + adjoint4[GRID:]
     coarse_adjoint = 2.0 * (adjoint2[:, :GRID] + adjoint2[:, GRID:])
+    fetches[3].wait()
+    right_t = right_t_ref[...]
     grad_ref[...] = jnp.zeros(grad_ref.shape, jnp.float32)
     for source in range(SOURCES):
         shift_a = ints_ref[source, 0]
@@ -239,8 +326,8 @@
         weight = ints_ref[source, 2].astype(jnp.float32) * (1.0 / (4.0 * SOURCES))
         weighted = weight * coarse_adjoint
         dfield_h, dfield_l = halves(field_ref[source] * jnp.concatenate([weighted, weighted], axis=1))
-        dline2 = dot_t(dfield_h, right)
-        dline = dline2[:, :128] + dline2[:, 128:] + dot_t(dfield_l, right[:128])
+        dline2 = dot(dfield_h, right_t)
+        dline = dline2[:, :128] + dline2[:, 128:] + dot(dfield_l, right_t[:, :128])
         damp4 = dot(left_t, jnp.concatenate(halves(dline), axis=1))
         damp2 = damp4[:128] + damp4[128:]
         damp1 = damp2[:, :128] + damp2[:, 128:]
@@ -257,23 +344,29 @@
         [jnp.where(low, fold_re, -fold_im), jnp.where(low, -fold_im, -fold_re)], axis=0
     )
     packed = dot(jnp.concatenate([unfold_t, unfold_t], axis=1), jnp.concatenate(halves(packed), axis=0))
+    fetches[4].wait()
     first = my_src == 0
     edge_rows = row_ref[pl.ds(pl.multiple_of(jnp.where(first, EXT_PX - HALO, 0), HALO), HALO), :]
     mine_rows = row_ref[pl.ds(pl.multiple_of(HALO + my_src * ROWS, HALO), ROWS), :]
     tables = jnp.concatenate([edge_rows, mine_rows], axis=0)
     back = jnp.dot(tables, packed, precision=lax.Precision.HIGHEST, preferred_element_type=jnp.float32)
-    sent_ref[...] = jnp.zeros(sent_ref.shape, jnp.bfloat16)
     goes_to = jnp.where(first, below, above)
+    edge_ref[...] = back[:HALO].astype(jnp.bfloat16)
+    back_ref[...] = back[HALO:]
+    back_keep = pltpu.make_async_copy(back_ref, back_hbm, sems.at[11])
+    back_keep.start()
 
     @pl.when(goes_to >= 0)
     def _():
-        sent_ref[goes_to // 2] = back[:HALO].astype(jnp.bfloat16)
-
-    back_ref[...] = back[HALO:]
+        send = pltpu.make_async_copy(edge_ref, sent_hbm.at[goes_to // 2], sems.at[12])
+        send.start()
+        send.wait()
+
+    back_keep.wait()
     keep.wait()
 
 
-def make_fields(slot_pos, ints, got, own, pupil, row_table, target):
+def make_fields(slot_pos, ints, *arrays):
     return pl.pallas_call(
         fields_kernel,
         out_shape=(
@@ -281,49 +374,90 @@
             jax.ShapeDtypeStruct((ROWS, 128), jnp.float32),
             jax.ShapeDtypeStruct((TILES // 2, HALO, 128), jnp.bfloat16),
         ),
-        in_specs=[SCALARS, SCALARS] + [WHOLE] * 7 + [LEFT_THERE],
-        out_specs=[LEFT_THERE, WHOLE, WHOLE],
+        in_specs=[SCALARS, SCALARS] + [LEFT_THERE] * 9,
+        out_specs=[LEFT_THERE] * 3,
         scratch_shapes=[
+            pltpu.VMEM((2, HALO, 128), jnp.bfloat16),
+            pltpu.VMEM((128, 128), jnp.float32),
+            pltpu.VMEM((2, 64, 128), jnp.float32),
+            pltpu.VMEM(SMALL.shape, jnp.bfloat16),
+            pltpu.VMEM((256, 256), jnp.bfloat16),
+            pltpu.VMEM(GRIDS.shape, jnp.bfloat16),
+            pltpu.VMEM(GRIDS.shape[::-1], jnp.bfloat16),
+            pltpu.VMEM(ROW_F32.shape, jnp.float32),
             pltpu.VMEM((TILE_PX, TILE_PX), jnp.bfloat16),
+            pltpu.VMEM((ROWS, 128), jnp.float32),
+            pltpu.VMEM((HALO, 128), jnp.bfloat16),
             pltpu.VMEM((TILE_PX, TILE_PX), jnp.float32),
             pltpu.VMEM((2, FREQ, FREQ), jnp.float32),
             pltpu.VMEM((SOURCES, GRID, 2 * GRID), jnp.float32),
             pltpu.VMEM((TILE_PX, 2 * GRID), jnp.bfloat16),
             pltpu.VMEM((2, FREQ, FREQ), jnp.float32),
-            pltpu.SemaphoreType.DMA((2,)),
+            pltpu.SemaphoreType.DMA((13,)),
         ],
-        compiler_params=pltpu.CompilerParams(vmem_limit_bytes=48 * 1024 * 1024),
+        compiler_params=pltpu.CompilerParams(vmem_limit_bytes=ALL_VMEM),
         interpret=INTERPRET,
         name="fields",
-    )(
-        slot_pos, ints, got, own, pupil, jnp.asarray(SMALL), jnp.asarray(GRIDS), jnp.asarray(GRID_YT), row_table, target
-    )
-
-
-def steps_kernel(slot_ref, got_ref, other_ref, back_ref, col_ref, out_ref):
+    )(slot_pos, ints, *arrays)
+
+
+def steps_kernel(back_ref, col_ref, steps_hbm, edge_ref, steps_ref, sems):
+    my_src = lax.axis_index("src")
+    high, low = halves(-LEARN_RATE * back_ref[...])
+    steps_ref[...] = dot_t(high, col_ref[...]) + dot_t(low, col_ref[...])
+    keep = pltpu.make_async_copy(steps_ref, steps_hbm, sems.at[0])
+    keep.start()
+    at_end = my_src == SRC_DEVICES - 1
+    edge_ref[...] = jnp.where(at_end, steps_ref[ROWS - HALO :, :], steps_ref[:HALO, :])
+    keep.wait()
+
+
+def make_steps(back, col):
+    return pl.pallas_call(
+        steps_kernel,
+        out_shape=(
+            jax.ShapeDtypeStruct((ROWS, TILE_PX), jnp.float32),
+            jax.ShapeDtypeStruct((HALO, TILE_PX), jnp.float32),
+        ),
+        in_specs=[WHOLE, WHOLE],
+        out_specs=[LEFT_THERE, WHOLE],
+        scratch_shapes=[pltpu.VMEM((ROWS, TILE_PX), jnp.float32), pltpu.SemaphoreType.DMA((1,))],
+        compiler_params=pltpu.CompilerParams(vmem_limit_bytes=4 * MIB),
+        interpret=INTERPRET,
+        name="steps",
+    )(back, col)
+
+
+def edge_kernel(slot_ref, got_ref, other_ref, edge_ref, col_ref, steps_in, steps_hbm, sum_ref, sems):
     my_slot, my_src, above, below = places(slot_ref)
     first = my_src == 0
     last = my_src == SRC_DEVICES - 1
     comes_from = jnp.where(first, above, below)
-    place = jnp.maximum(comes_from, 0) // 2
-    same_core = lax.rem(jnp.maximum(comes_from, 0), 2) == lax.rem(my_slot, 2)
-    rim = jnp.where(same_core, got_ref[place].astype(jnp.float32), other_ref[place].astype(jnp.float32))
-    top = jnp.where(first & (above >= 0), rim, 0.0)
-    bottom = jnp.where(last & (below >= 0), rim, 0.0)
-    back = -LEARN_RATE * (back_ref[...] + jnp.concatenate([top, bottom], axis=0))
-    high, low = halves(back)
-    out_ref[...] = dot_t(high, col_ref[...]) + dot_t(low, col_ref[...])
-
-
-def make_steps(slot_pos, got, other, back, col):
+
+    @pl.when((first | last) & (comes_from >= 0))
+    def _():
+        place = comes_from // 2
+        same_core = lax.rem(comes_from, 2) == lax.rem(my_slot, 2)
+        rim = jnp.where(same_core, got_ref[place].astype(jnp.float32), other_ref[place].astype(jnp.float32))
+        sum_ref[...] = edge_ref[...] - LEARN_RATE * dot_t(rim.astype(jnp.bfloat16), col_ref[...])
+        start = pl.multiple_of(jnp.where(first, 0, ROWS - HALO), HALO)
+        keep = pltpu.make_async_copy(sum_ref, steps_hbm.at[pl.ds(start, HALO)], sems.at[0])
+        keep.start()
+        keep.wait()
+
+
+def add_edge(slot_pos, got, other, edge, col, steps):
     return pl.pallas_call(
-        steps_kernel,
+        edge_kernel,
         out_shape=jax.ShapeDtypeStruct((ROWS, TILE_PX), jnp.float32),
-        in_specs=[SCALARS] + [WHOLE] * 4,
-        out_specs=WHOLE,
+        in_specs=[SCALARS] + [WHOLE] * 4 + [LEFT_THERE],
+        out_specs=LEFT_THERE,
+        scratch_shapes=[pltpu.VMEM((HALO, TILE_PX), jnp.float32), pltpu.SemaphoreType.DMA((1,))],
+        input_output_aliases={5: 0},
+        compiler_params=pltpu.CompilerParams(vmem_limit_bytes=4 * MIB),
         interpret=INTERPRET,
-        name="steps",
-    )(slot_pos, got, other, back, col)
+        name="edge",
+    )(slot_pos, got, other, edge, col, steps)
 
 
 def pupil_tables(pupil_phase):
@@ -342,10 +476,11 @@
 
 
 def all_sources(src_shift, src_weight):
-    ints = jnp.concatenate([src_shift, src_weight[:, None]], axis=1)
     swap = lambda value, mask: lax.ppermute(value, "src", [(i, i ^ mask) for i in range(SRC_DEVICES)])
-    near = jnp.concatenate([ints] + [swap(ints, mask) for mask in (1, 2, 3)], axis=0)
-    return jnp.concatenate([near, swap(near, 4)], axis=0)
+    shifts = jnp.concatenate([src_shift, swap(src_shift, 4)], axis=0)
+    weights = jnp.concatenate([src_weight, swap(src_weight, 4)], axis=0)
+    ints = jnp.concatenate([shifts, weights[:, None]], axis=1)
+    return jnp.concatenate([ints] + [swap(ints, mask) for mask in (1, 2, 3)], axis=0)
 
 
 def per_device(mask_tiles, slot_pos, src_shift, src_weight, pupil_phase, target):
@@ -355,11 +490,18 @@
     tile = mask_tiles[0]
     got = lax.all_to_all(make_rims(slot_pos, tile, col), "tile", 0, 0, tiled=True)
     own = own_moments(tile, col, row_table)
-    resist, back, sent = make_fields(slot_pos, ints, got, own, pupil_tables(pupil_phase), row_table, target[0])
+    small = jnp.asarray(SMALL)
+    grids = jnp.asarray(GRIDS)
+    flipped, right_t = flip_tables(small, grids)
+    resist, back, sent = make_fields(
+        slot_pos, ints, got, own, pupil_tables(pupil_phase), small, right_t, grids, flipped, row_table, target[0]
+    )
     cores = [[2 * chip + core for chip in range(TILES // 2)] for core in range(2)]
     got = lax.all_to_all(sent, "tile", 0, 0, tiled=True, axis_index_groups=cores)
+    steps, edge = make_steps(back, col)
+    got, edge = lax.optimization_barrier((got, edge))
     other = lax.ppermute(got, "tile", [(i, i ^ 1) for i in range(TILES)])
-    return (resist[None], make_steps(slot_pos, got, other, back, col)[None])
+    return (resist[None], add_edge(slot_pos, got, other, edge, col, steps)[None])
 
 
 def solution(mesh):

time: 70.6 us -> 68.2 us (0.966)
  blocking collectives: 12.8 us -> 0 us
  starting transfers between devices: 21.4 us -> 27.3 us
  waiting for transfers between devices: 8.96 us -> 13.9 us
  Pallas kernels: 16.6 us -> 18.9 us
  local copies, waits for them, and re-layouts: 5.06 us -> 3.11 us
  matrix products: 3.57 us -> 2.45 us
    all_to_all x1 -> x0, blocking collectives: 12.8 us -> none  [per_device(): lax.all_to_all(sent, 'tile', 0, 0, tiled=True, axis_index_groups=cores)]
    all_to_all x0 -> x1, waiting for transfers between devices: none -> 6.89 us  [per_device(): lax.all_to_all(sent, 'tile', 0, 0, tiled=True, axis_index_groups=cores)]
    all_to_all x0 -> x1, starting transfers between devices: none -> 4.44 us  [per_device(): lax.all_to_all(sent, 'tile', 0, 0, tiled=True, axis_index_groups=cores)]
    pallas_call x1 -> x3, Pallas kernels: 2.27 us -> 5.34 us  [the longest x1 2.72 us: flip_tables(): pl.pallas_call(prep_kernel, out_shape=(jax.ShapeDtypeStruct(GRIDS.shape[:...]
    ppermute x4 -> x5, starting transfers between devices: 8.66 us -> 11.3 us  [all_sources(): lax.ppermute(value, 'src', [(i, i ^ mask) for i in range(SRC_DEVICES)])]
    unnamed x27 -> x19, local copies, waits for them, and re-layouts: 4.87 us -> 2.43 us
    dot_general x1, matrix products: 2.57 us -> 0.82 us  [own_moments(): half = jnp.dot(tile, col, preferred_element_type=jnp.float32)]
    all_to_all x1, starting transfers between devices: 10 us -> 8.34 us  [per_device(): lax.all_to_all(make_rims(slot_pos, tile, col), 'tile', 0, 0, tiled=True)]
  transfers between devices with their start and end apart: 6 -> 8, of which waited for: 3 -> 5; matrix products, arithmetic and copies ran while one was open for 6% -> 7% of each run, Pallas kernels for 4% -> 9%
where the time goes in v4:
time: 68.2 us; the launch traced here: 67.7 us
  starting transfers between devices  27.3 us (40%)
  Pallas kernels  18.9 us (28%)
  waiting for transfers between devices  13.9 us (20%)
  local copies, waits for them, and re-layouts  3.11 us (5%)
  matrix products  2.45 us (4%)
  other arithmetic  1.14 us (2%)
  between operations  0.95 us (1%)
    ppermute x5, starting transfers between devices, all_sources(): lax.ppermute(value, 'src', [(i, i ^ mask) for i in range(SRC_DEVICES)])  11.3 us
    pallas_call x1, Pallas kernels, make_fields(): pl.pallas_call(fields_kernel, out_shape=(jax.ShapeDtypeStruct((ROWS, TILE...  11 us
    all_to_all x1, starting transfers between devices, per_device(): lax.all_to_all(make_rims(slot_pos, tile, col), 'tile', 0, 0, tiled=True)  8.34 us
    all_to_all x1, waiting for transfers between devices, per_device(): lax.all_to_all(sent, 'tile', 0, 0, tiled=True, axis_index_groups=cores)  6.89 us
    all_to_all x1, starting transfers between devices, per_device(): lax.all_to_all(sent, 'tile', 0, 0, tiled=True, axis_index_groups=cores)  4.44 us
    ppermute x5, waiting for transfers between devices, all_sources(): lax.ppermute(value, 'src', [(i, i ^ mask) for i in range(SRC_DEVICES)])  3.56 us
    ppermute x1, starting transfers between devices, per_device(): other = lax.ppermute(got, 'tile', [(i, i ^ 1) for i in range(TILES)])  3.21 us
    pallas_call x1, Pallas kernels, flip_tables(): pl.pallas_call(prep_kernel, out_shape=(jax.ShapeDtypeStruct(GRIDS.shape[:...  2.72 us
  transfers between devices with their start and end apart: 8, of which 5 were waited for; matrix products, arithmetic and copies ran while one was open for 7% of the time, Pallas kernels for 9%

profile of v4, /device:TPU:1, one launch (start us, length us, event | category | flops | bytes accessed | tf_op | source)
XLA Modules:
  0.0 67.7 jit_solution(8368672883596934555)
XLA Ops:
  0.6 0.0 copy-start.7
  0.6 0.0 copy-start.6
  0.7 7.8 %collective-permute-start.1 = (s32[2]{0:T(128)}, s32[2]{0:T(128)S(1)}, u32[]{:S(2)}, u32[]{:S(2)}) collective-permute-start(s32[2]{0:T(128)} %param.14), channel_id=1, source_target_pairs={{0,128},{32,160},{64,192},{96,224},{128,0},{160,32},{192,64},{224,... | collective-permute-start | bytes 32 | tf_op jit(solution)/shard_map/ppermute | solution.py:479
  8.5 0.8 %copy.16 = s32[2,2]{0,1:T(2,128)S(1)} copy(s32[2,2]{1,0:T(2,128)} %param.13) | data formatting | bytes 32 | tf_op args[2]
  9.2 0.0 collective-permute-start
  9.3 2.6 %rims.1 = bf16[32,64,128]{2,1,0:T(8,128)(2,1)} custom-call(s32[32]{0:T(128)} %slot_ref.5, bf16[1024,1024]{1,0:T(8,128)(2,1)} %bitcast.14, bf16[1024,128]{1,0:T(8,128)(2,1)} %constant.14.clone.col_hbm.col_ref), custom_call_target="tpu_custom_call" | custom-call | tf_op jit(solution)/shard_map/rims/pallas_call | solution.py:162
  11.8 0.0 copy-start
  11.9 0.0 copy-start.3
  11.9 8.3 %all-to-all-start = ((bf16[32,64,128]{2,1,0:T(8,128)(2,1)}), bf16[32,64,128]{2,1,0:T(8,128)(2,1)S(1)}, u32[]{:S(2)}, u32[]{:S(2)}) async-start(bf16[32,64,128]{2,1,0:T(8,128)(2,1)} %rims.1), calls=%async_computation | async-start | bytes 1048576 | tf_op jit(solution)/shard_map/all_to_all | solution.py:491
  20.2 0.0 copy-done.7
  20.2 0.0 copy-done.6
  20.2 0.2 select_multiply_fusion.1
  20.4 0.1 maximum_bitcast_fusion
  20.5 0.0 copy-start.4
  20.6 2.7 %prep.1 = (bf16[512,1024]{1,0:T(8,128)(2,1)}, bf16[256,256]{1,0:T(8,128)(2,1)}) custom-call(bf16[256,1152]{1,0:T(8,128)(2,1)} %constant.16.clone.small_hbm, bf16[1024,512]{1,0:T(8,128)(2,1)} %constant.17.clone.grids_hbm), custom_call_target="tpu_custom_call" | custom-call | tf_op jit(solution)/shard_map/prep/pallas_call | solution.py:201
  23.3 0.0 copy-start.8
  23.3 0.6 pad_maximum_fusion.pupil_hbm
  23.9 0.0 copy-done
  23.9 0.0 copy-done.3
  23.9 0.8 %fusion.2 = f32[128,1024]{1,0:T(8,128)S(1)} fusion(bf16[1024,128]{1,0:T(8,128)(2,1)S(1)} %copy-done, bf16[1,1024,1024]{2,1,0:T(8,128)(2,1)S(1)} %copy-done.3), kind=kOutput, calls=%fused_computation.10 | convolution fusion | flops 268435456 | bytes 2883584 | tf_op jit(solution)/shard_map/dot_general | solution.py:471
  24.8 0.0 copy-done.4
  24.8 1.6 %fusion.own_hbm = f32[128,128]{1,0:T(8,128)} fusion(f32[128,1024]{1,0:T(8,128)S(1)} %fusion.2, f32[1152,128]{1,0:T(8,128)S(1)} %copy-done.4), kind=kOutput, calls=%fused_computation | convolution fusion | flops 201326592 | bytes 1114112 | tf_op jit(solution)/shard_map/dot_general | solution.py:473
  26.4 0.0 collective-permute-done.1
  26.4 0.0 copy-done.8
  26.4 0.1 add_bitcast_fusion
  26.5 0.0 collective-permute-done
  26.5 0.1 pad_add_fusion
  26.5 2.8 %collective-permute-start.4 = (s32[4,3]{0,1:T(4,128)S(1)}, s32[4,3]{0,1:T(4,128)S(1)}, u32[]{:S(2)}, u32[]{:S(2)}) collective-permute-start(s32[4,3]{0,1:T(4,128)S(1)} %pad_add_fusion), channel_id=1, source_target_pairs={{0,96},{32,64},{64,32},{96,0},{128,224},{160,192},{192,160},{224,1... | collective-permute-start | bytes 152 | tf_op jit(solution)/shard_map/ppermute | solution.py:479
  29.3 0.4 collective-permute-start.3
  29.7 0.3 collective-permute-start.2
  30.0 0.6 collective-permute-done.4
  30.6 3.0 %collective-permute-done.3 = s32[4,3]{0,1:T(4,128)S(1)} collective-permute-done((s32[4,3]{0,1:T(4,128)S(1)}, s32[4,3]{0,1:T(4,128)S(1)}, u32[]{:S(2)}, u32[]{:S(2)}) %collective-permute-start.3) | collective-permute-done | bytes 80 | tf_op jit(solution)/shard_map/ppermute | solution.py:479
  33.5 0.0 collective-permute-done.2
  33.5 0.1 pad_add_fusion.1
  33.6 0.7 copy.17.ints_ref
  34.3 2.3 %all-to-all-done.got_hbm = bf16[32,64,128]{2,1,0:T(8,128)(2,1)S(1)} async-done(((bf16[32,64,128]{2,1,0:T(8,128)(2,1)}), bf16[32,64,128]{2,1,0:T(8,128)(2,1)S(1)}, u32[]{:S(2)}, u32[]{:S(2)}) %all-to-all-start) | async-done | bytes 524320 | tf_op jit(solution)/shard_map/all_to_all | solution.py:491
  36.6 0.0 copy-start.5
  36.6 0.8 %copy-done.5 = bf16[32,64,128]{2,1,0:T(8,128)(2,1)} copy-done((bf16[32,64,128]{2,1,0:T(8,128)(2,1)}, bf16[32,64,128]{2,1,0:T(8,128)(2,1)S(1)}, u32[]{:S(2)}) %copy-start.5) | copy-done | bytes 524312
  37.4 0.0 copy-start.2
  37.4 11.0 %fields.1 = (f32[128,1024]{1,0:T(8,128)}, f32[128,128]{1,0:T(8,128)}, bf16[16,64,128]{2,1,0:T(8,128)(2,1)}) custom-call(s32[32]{0:T(128)} %slot_ref.5, s32[16,3]{1,0:T(8,128)} %copy.17.ints_ref, bf16[32,64,128]{2,1,0:T(8,128)(2,1)} %copy-done.5, f32[128,128]{1,0:T(8,128)} %fusion.own_hbm, f32[2,64,128]{2,1,0:T(8,128)} %pad_maximum_fusion.pupil_hbm, ...), custom_call_target="tpu_custom_call" | custom-call | tf_op jit(solution)/shard_map/fields/pallas_call | solution.py:370
  48.4 4.4 %all-to-all-start.1 = ((bf16[16,64,128]{2,1,0:T(8,128)(2,1)}), bf16[16,64,128]{2,1,0:T(8,128)(2,1)S(1)}, u32[]{:S(2)}, u32[]{:S(2)}) async-start(bf16[16,64,128]{2,1,0:T(8,128)(2,1)} %get-tuple-element.14), calls=%async_computation.1 | async-start | bytes 524288 | tf_op jit(solution)/shard_map/all_to_all | solution.py:500
  52.9 0.0 copy-start.1
  52.9 0.8 %copy-done.1 = f32[128,128]{1,0:T(8,128)S(1)} copy-done((f32[128,128]{1,0:T(8,128)S(1)}, f32[128,128]{1,0:T(8,128)}, u32[]{:S(2)}) %copy-start.1) | copy-done | bytes 65560
  53.7 1.1 %steps.1 = (f32[128,1024]{1,0:T(8,128)}, f32[64,1024]{1,0:T(8,128)S(1)}) custom-call(f32[128,128]{1,0:T(8,128)S(1)} %copy-done.1, bf16[1024,128]{1,0:T(8,128)(2,1)S(1)} %copy-done), custom_call_target="tpu_custom_call" | custom-call | tf_op jit(solution)/shard_map/steps/pallas_call | solution.py:416
  54.8 6.9 %all-to-all-done.1.got_ref = bf16[16,64,128]{2,1,0:T(8,128)(2,1)S(1)} async-done(((bf16[16,64,128]{2,1,0:T(8,128)(2,1)}), bf16[16,64,128]{2,1,0:T(8,128)(2,1)S(1)}, u32[]{:S(2)}, u32[]{:S(2)}) %all-to-all-start.1) | async-done | bytes 262176 | tf_op jit(solution)/shard_map/all_to_all | solution.py:500
  61.7 3.2 %collective-permute-start.5 = (bf16[16,64,128]{2,1,0:T(8,128)(2,1)S(1)}, bf16[16,64,128]{2,1,0:T(8,128)(2,1)S(1)}, u32[]{:S(2)}, u32[]{:S(2)}) collective-permute-start(bf16[16,64,128]{2,1,0:T(8,128)(2,1)S(1)} %all-to-all-done.1.got_ref), channel_id=1, source_target_pairs={{0,1},{1,0},{2,3},{3,2},{4,5},{5,4},{6,7},{7,6},{8,9},{9,8},{10,11... | collective-permute-start | bytes 786440 | tf_op jit(solution)/shard_map/ppermute | solution.py:503
  64.9 1.2 %collective-permute-done.5.other_ref = bf16[16,64,128]{2,1,0:T(8,128)(2,1)S(1)} collective-permute-done((bf16[16,64,128]{2,1,0:T(8,128)(2,1)S(1)}, bf16[16,64,128]{2,1,0:T(8,128)(2,1)S(1)}, u32[]{:S(2)}, u32[]{:S(2)}) %collective-permute-start.5) | collective-permute-done | bytes 262176 | tf_op jit(solution)/shard_map/ppermute | solution.py:503
  66.1 0.0 copy-done.2
  66.1 1.5 %edge.1 = f32[128,1024]{1,0:T(8,128)} custom-call(s32[32]{0:T(128)S(1)} %copy-done.2, bf16[16,64,128]{2,1,0:T(8,128)(2,1)S(1)} %all-to-all-done.1.got_ref, bf16[16,64,128]{2,1,0:T(8,128)(2,1)S(1)} %collective-permute-done.5.other_ref, f32[64,1024]{1,0:T(8,128)S(1)} %get-tuple-element.18.edge_ref, ...), custom_call_target="tpu_custom_call", output_to_operand_aliasing={{}: (5, {})} | custom-call | tf_op jit(solution)/shard_map/edge/pallas_call | solution.py:450
Async XLA Ops:
  0.6 19.6 %copy-start.7 = (pred[64,64]{1,0:T(32,128)(4,1)S(1)}, pred[64,64]{1,0:T(32,128)(4,1)}, u32[]{:S(2)}) copy-start(pred[64,64]{1,0:T(32,128)(4,1)} %constant.18.clone) | copy-start | bytes 12292
  0.6 19.6 %copy-start.6 = (f32[128,128]{1,0:T(8,128)S(1)}, f32[128,128]{1,0:T(8,128)}, u32[]{:S(2)}) copy-start(f32[128,128]{1,0:T(8,128)} %param.15) | copy-start | bytes 196612
  0.7 25.7 %collective-permute-start.1 = (s32[2]{0:T(128)}, s32[2]{0:T(128)S(1)}, u32[]{:S(2)}, u32[]{:S(2)}) collective-permute-start(s32[2]{0:T(128)} %param.14), channel_id=1, source_target_pairs={{0,128},{32,160},{64,192},{96,224},{128,0},{160,32},{192,64},{224,... | collective-permute-start | bytes 32 | tf_op jit(solution)/shard_map/ppermute | solution.py:479
  9.2 17.2 %collective-permute-start = (s32[2,2]{0,1:T(2,128)S(1)}, s32[2,2]{0,1:T(2,128)S(1)}, u32[]{:S(2)}, u32[]{:S(2)}) collective-permute-start(s32[2,2]{0,1:T(2,128)S(1)} %copy.16), channel_id=1, source_target_pairs={{0,128},{32,160},{64,192},{96,224},{128,0},{160,32},{192,64},{224,... | collective-permute-start | bytes 56 | tf_op jit(solution)/shard_map/ppermute | solution.py:479
  11.8 12.1 %copy-start = (bf16[1024,128]{1,0:T(8,128)(2,1)S(1)}, bf16[1024,128]{1,0:T(8,128)(2,1)}, u32[]{:S(2)}) copy-start(bf16[1024,128]{1,0:T(8,128)(2,1)} %constant.14.clone.col_hbm.col_ref) | copy-start | bytes 786436
  11.9 12.1 %copy-start.3 = (bf16[1,1024,1024]{2,1,0:T(8,128)(2,1)S(1)}, bf16[1,1024,1024]{2,1,0:T(8,128)(2,1)}, u32[]{:S(2)}) copy-start(bf16[1,1024,1024]{2,1,0:T(8,128)(2,1)} %param.11) | copy-start | bytes 6291460
  11.9 24.7 %all-to-all-start = ((bf16[32,64,128]{2,1,0:T(8,128)(2,1)}), bf16[32,64,128]{2,1,0:T(8,128)(2,1)S(1)}, u32[]{:S(2)}, u32[]{:S(2)}) async-start(bf16[32,64,128]{2,1,0:T(8,128)(2,1)} %rims.1), calls=%async_computation | async-start | bytes 1048576 | tf_op jit(solution)/shard_map/all_to_all | solution.py:491
  20.5 4.2 %copy-start.4 = (f32[1152,128]{1,0:T(8,128)S(1)}, f32[1152,128]{1,0:T(8,128)}, u32[]{:S(2)}) copy-start(f32[1152,128]{1,0:T(8,128)} %constant.15.clone.row_hbm) | copy-start | bytes 1769476
  23.3 3.1 %copy-start.8 = (s32[2]{0:T(128)S(1)}, s32[2]{0:T(128)}, u32[]{:S(2)}) copy-start(s32[2]{0:T(128)} %param.14) | copy-start | bytes 28
  26.5 4.0 %collective-permute-start.4 = (s32[4,3]{0,1:T(4,128)S(1)}, s32[4,3]{0,1:T(4,128)S(1)}, u32[]{:S(2)}, u32[]{:S(2)}) collective-permute-start(s32[4,3]{0,1:T(4,128)S(1)} %pad_add_fusion), channel_id=1, source_target_pairs={{0,96},{32,64},{64,32},{96,0},{128,224},{160,192},{192,160},{224,1... | collective-permute-start | bytes 152 | tf_op jit(solution)/shard_map/ppermute | solution.py:479
  29.3 4.2 %collective-permute-start.3 = (s32[4,3]{0,1:T(4,128)S(1)}, s32[4,3]{0,1:T(4,128)S(1)}, u32[]{:S(2)}, u32[]{:S(2)}) collective-permute-start(s32[4,3]{0,1:T(4,128)S(1)} %pad_add_fusion), channel_id=1, source_target_pairs={{0,64},{32,96},{64,0},{96,32},{128,192},{160,224},{192,128},{224,1... | collective-permute-start | bytes 152 | tf_op jit(solution)/shard_map/ppermute | solution.py:479
  29.7 3.9 %collective-permute-start.2 = (s32[4,3]{0,1:T(4,128)S(1)}, s32[4,3]{0,1:T(4,128)S(1)}, u32[]{:S(2)}, u32[]{:S(2)}) collective-permute-start(s32[4,3]{0,1:T(4,128)S(1)} %pad_add_fusion), channel_id=1, source_target_pairs={{0,32},{32,0},{64,96},{96,64},{128,160},{160,128},{192,224},{224,1... | collective-permute-start | bytes 152 | tf_op jit(solution)/shard_map/ppermute | solution.py:479
  36.6 0.8 %copy-start.5 = (bf16[32,64,128]{2,1,0:T(8,128)(2,1)}, bf16[32,64,128]{2,1,0:T(8,128)(2,1)S(1)}, u32[]{:S(2)}) copy-start(bf16[32,64,128]{2,1,0:T(8,128)(2,1)S(1)} %all-to-all-done.got_hbm) | copy-start | bytes 1572868
  37.4 28.7 %copy-start.2 = (s32[32]{0:T(128)S(1)}, s32[32]{0:T(128)}, u32[]{:S(2)}) copy-start(s32[32]{0:T(128)} %slot_ref.5) | copy-start | bytes 388
  48.4 13.3 %all-to-all-start.1 = ((bf16[16,64,128]{2,1,0:T(8,128)(2,1)}), bf16[16,64,128]{2,1,0:T(8,128)(2,1)S(1)}, u32[]{:S(2)}, u32[]{:S(2)}) async-start(bf16[16,64,128]{2,1,0:T(8,128)(2,1)} %get-tuple-element.14), calls=%async_computation.1 | async-start | bytes 524288 | tf_op jit(solution)/shard_map/all_to_all | solution.py:500
  52.9 0.8 %copy-start.1 = (f32[128,128]{1,0:T(8,128)S(1)}, f32[128,128]{1,0:T(8,128)}, u32[]{:S(2)}) copy-start(f32[128,128]{1,0:T(8,128)} %get-tuple-element.15.back_ref) | copy-start | bytes 196612
  61.7 4.4 %collective-permute-start.5 = (bf16[16,64,128]{2,1,0:T(8,128)(2,1)S(1)}, bf16[16,64,128]{2,1,0:T(8,128)(2,1)S(1)}, u32[]{:S(2)}, u32[]{:S(2)}) collective-permute-start(bf16[16,64,128]{2,1,0:T(8,128)(2,1)S(1)} %all-to-all-done.1.got_ref), channel_id=1, source_target_pairs={{0,1},{1,0},{2,3},{3,2},{4,5},{5,4},{6,7},{7,6},{8,9},{9,8},{10,11... | collective-permute-start | bytes 786440 | tf_op jit(solution)/shard_map/ppermute | solution.py:503

commit v5 on v4

--- a/solution.py
+++ b/solution.py
@@ -156,6 +156,7 @@
 LEFT_THERE = pl.BlockSpec(memory_space=pltpu.MemorySpace.HBM)
 MIB = 1024 * 1024
 ALL_VMEM = 63_000_000
+FIELDS_VMEM = 54_000_000
 
 
 def make_rims(slot_pos, tile, col):
@@ -220,39 +221,19 @@
 
 
 def fields_kernel(
-    slot_ref, ints_ref, got_hbm, own_hbm, pupil_hbm, small_hbm, right_t_hbm, grids_hbm, flipped_hbm, row_hbm, target_hbm,
-    resist_hbm, back_hbm, sent_hbm,
-    got_ref, own_ref, pupil_ref, small_ref, right_t_ref, grids_ref, flipped_ref, row_ref, target_ref,
-    back_ref, edge_ref, resist_ref, spec_ref, field_ref, fold_ref, grad_ref, sems,
+    slot_ref, ints_ref, got_ref, own_ref, pupil_ref, small_ref, right_t_ref, row_ref, grids_hbm, flipped_hbm, target_hbm,
+    resist_hbm, back_ref, sent_hbm,
+    edge_ref, grids_ref, flipped_ref, target_ref, resist_ref, spec_ref, field_ref, fold_ref, grad_ref, sems,
 ):
-    first_fetches = [
+    fetches = [
         pltpu.make_async_copy(source, target, sems.at[number])
-        for number, (source, target) in enumerate(((small_hbm, small_ref), (own_hbm, own_ref), (pupil_hbm, pupil_ref)))
-    ]
-    for fetch in first_fetches:
-        fetch.start()
-    my_slot, my_src, above, below = places(slot_ref)
-    for number, slot in enumerate((above, below)):
-        first_fetches.append(
-            pltpu.make_async_copy(got_hbm.at[jnp.maximum(slot, 0)], got_ref.at[number], sems.at[3 + number])
-        )
-        first_fetches[-1].start()
-    fetches = [
-        pltpu.make_async_copy(source, target, sems.at[5 + number])
         for number, (source, target) in enumerate(
-            (
-                (grids_hbm, grids_ref),
-                (flipped_hbm, flipped_ref),
-                (target_hbm, target_ref),
-                (right_t_hbm, right_t_ref),
-                (row_hbm, row_ref),
-            )
+            ((grids_hbm, grids_ref), (flipped_hbm, flipped_ref), (target_hbm, target_ref))
         )
     ]
     for fetch in fetches:
         fetch.start()
-    for fetch in first_fetches:
-        fetch.wait()
+    my_slot, my_src, above, below = places(slot_ref)
     unfold = small_ref[:, 0:128]
     left = small_ref[:, 128:320]
     right = small_ref[:, 384:640]
@@ -263,8 +244,8 @@
     lanes2 = jnp.concatenate([lanes, lanes], axis=1)
     low = low_lanes((128, 128))
     low_w = low_lanes((64, 128))
-    up = jnp.where(above >= 0, got_ref[0].astype(jnp.float32), 0.0)
-    down = jnp.where(below >= 0, got_ref[1].astype(jnp.float32), 0.0)
+    up = jnp.where(above >= 0, got_ref[jnp.maximum(above, 0)].astype(jnp.float32), 0.0)
+    down = jnp.where(below >= 0, got_ref[jnp.maximum(below, 0)].astype(jnp.float32), 0.0)
     rims = jnp.concatenate([up, down], axis=0).astype(jnp.bfloat16)
     moments = own_ref[...] + dot(rim_table, jnp.concatenate([rims, rims], axis=0))
     half = dot(jnp.concatenate([unfold, unfold], axis=1), jnp.concatenate(halves(moments), axis=0))
@@ -294,17 +275,17 @@
         coarse = coarse + weight * (squared[:, :GRID] + squared[:, GRID:])
     coarse_h, coarse_l = halves(coarse)
     coarse_hh = jnp.concatenate([coarse_h, coarse_h], axis=0)
-    for fetch in fetches[:3]:
+    for fetch in fetches:
         fetch.wait()
     grid_x = grids_ref[:, 256:512]
-    grid_xt = flipped_ref[256:512, :]
+    grid_xhh = jnp.concatenate([flipped_ref[256:384, :], flipped_ref[256:384, :]], axis=0)
     grid_yt = flipped_ref[0:256, :]
     chunk = 256
     for place in range(TILE_PX // chunk):
         rows = pl.ds(place * chunk, chunk)
         rows_y = dot(grids_ref[rows, 0:256], coarse_hh) + dot(grids_ref[rows, 0:128], coarse_l)
         rows_h, rows_l = halves(rows_y)
-        intensity = dot(jnp.concatenate([rows_h, rows_h], axis=1), grid_xt) + dot(rows_l, grid_xt[:GRID])
+        intensity = dot(jnp.concatenate([rows_h, rows_l], axis=1), grid_xhh)
         resist = jax.nn.sigmoid(STEEPNESS * (intensity - THRESHOLD))
         resist_ref[rows, :] = resist
         wanted = target_ref[rows, :].astype(jnp.float32)
@@ -312,12 +293,11 @@
         folded = dot(adjoint, grid_x)
         fold_ref[rows, :] = jnp.concatenate(halves(folded[:, :GRID] + folded[:, GRID:]), axis=1)
     mine = pl.multiple_of(my_src * ROWS, ROWS)
-    keep = pltpu.make_async_copy(resist_ref.at[pl.ds(mine, ROWS)], resist_hbm, sems.at[10])
+    keep = pltpu.make_async_copy(resist_ref.at[pl.ds(mine, ROWS)], resist_hbm, sems.at[3])
     keep.start()
     adjoint4 = dot(grid_yt, fold_ref[...])
     adjoint2 = adjoint4[:GRID] + adjoint4[GRID:]
     coarse_adjoint = 2.0 * (adjoint2[:, :GRID] + adjoint2[:, GRID:])
-    fetches[3].wait()
     right_t = right_t_ref[...]
     grad_ref[...] = jnp.zeros(grad_ref.shape, jnp.float32)
     for source in range(SOURCES):
@@ -344,25 +324,21 @@
         [jnp.where(low, fold_re, -fold_im), jnp.where(low, -fold_im, -fold_re)], axis=0
     )
     packed = dot(jnp.concatenate([unfold_t, unfold_t], axis=1), jnp.concatenate(halves(packed), axis=0))
-    fetches[4].wait()
     first = my_src == 0
     edge_rows = row_ref[pl.ds(pl.multiple_of(jnp.where(first, EXT_PX - HALO, 0), HALO), HALO), :]
     mine_rows = row_ref[pl.ds(pl.multiple_of(HALO + my_src * ROWS, HALO), ROWS), :]
     tables = jnp.concatenate([edge_rows, mine_rows], axis=0)
     back = jnp.dot(tables, packed, precision=lax.Precision.HIGHEST, preferred_element_type=jnp.float32)
     goes_to = jnp.where(first, below, above)
-    edge_ref[...] = back[:HALO].astype(jnp.bfloat16)
-    back_ref[...] = back[HALO:]
-    back_keep = pltpu.make_async_copy(back_ref, back_hbm, sems.at[11])
-    back_keep.start()
 
     @pl.when(goes_to >= 0)
     def _():
-        send = pltpu.make_async_copy(edge_ref, sent_hbm.at[goes_to // 2], sems.at[12])
+        edge_ref[...] = back[:HALO].astype(jnp.bfloat16)
+        send = pltpu.make_async_copy(edge_ref, sent_hbm.at[goes_to // 2], sems.at[4])
         send.start()
         send.wait()
 
-    back_keep.wait()
+    back_ref[...] = back[HALO:]
     keep.wait()
 
 
@@ -374,28 +350,21 @@
             jax.ShapeDtypeStruct((ROWS, 128), jnp.float32),
             jax.ShapeDtypeStruct((TILES // 2, HALO, 128), jnp.bfloat16),
         ),
-        in_specs=[SCALARS, SCALARS] + [LEFT_THERE] * 9,
-        out_specs=[LEFT_THERE] * 3,
+        in_specs=[SCALARS, SCALARS] + [WHOLE] * 6 + [LEFT_THERE] * 3,
+        out_specs=[LEFT_THERE, WHOLE, LEFT_THERE],
         scratch_shapes=[
-            pltpu.VMEM((2, HALO, 128), jnp.bfloat16),
-            pltpu.VMEM((128, 128), jnp.float32),
-            pltpu.VMEM((2, 64, 128), jnp.float32),
-            pltpu.VMEM(SMALL.shape, jnp.bfloat16),
-            pltpu.VMEM((256, 256), jnp.bfloat16),
+            pltpu.VMEM((HALO, 128), jnp.bfloat16),
             pltpu.VMEM(GRIDS.shape, jnp.bfloat16),
             pltpu.VMEM(GRIDS.shape[::-1], jnp.bfloat16),
-            pltpu.VMEM(ROW_F32.shape, jnp.float32),
             pltpu.VMEM((TILE_PX, TILE_PX), jnp.bfloat16),
-            pltpu.VMEM((ROWS, 128), jnp.float32),
-            pltpu.VMEM((HALO, 128), jnp.bfloat16),
             pltpu.VMEM((TILE_PX, TILE_PX), jnp.float32),
             pltpu.VMEM((2, FREQ, FREQ), jnp.float32),
             pltpu.VMEM((SOURCES, GRID, 2 * GRID), jnp.float32),
             pltpu.VMEM((TILE_PX, 2 * GRID), jnp.bfloat16),
             pltpu.VMEM((2, FREQ, FREQ), jnp.float32),
-            pltpu.SemaphoreType.DMA((13,)),
+            pltpu.SemaphoreType.DMA((5,)),
         ],
-        compiler_params=pltpu.CompilerParams(vmem_limit_bytes=ALL_VMEM),
+        compiler_params=pltpu.CompilerParams(vmem_limit_bytes=FIELDS_VMEM),
         interpret=INTERPRET,
         name="fields",
     )(slot_pos, ints, *arrays)
@@ -494,7 +463,7 @@
     grids = jnp.asarray(GRIDS)
     flipped, right_t = flip_tables(small, grids)
     resist, back, sent = make_fields(
-        slot_pos, ints, got, own, pupil_tables(pupil_phase), small, right_t, grids, flipped, row_table, target[0]
+        slot_pos, ints, got, own, pupil_tables(pupil_phase), small, right_t, row_table, grids, flipped, target[0]
     )
     cores = [[2 * chip + core for chip in range(TILES // 2)] for core in range(2)]
     got = lax.all_to_all(sent, "tile", 0, 0, tiled=True, axis_index_groups=cores)

time: 68.2 us -> 66.5 us (0.975)
  local copies, waits for them, and re-layouts: 3.11 us -> 0.9 us
  matrix products: 2.45 us -> 3.5 us
  waiting for transfers between devices: 13.9 us -> 14.9 us
    dot_general x1, matrix products: 0.82 us -> 2.48 us  [own_moments(): half = jnp.dot(tile, col, preferred_element_type=jnp.float32)]
    unnamed x19 -> x17, local copies, waits for them, and re-layouts: 2.43 us -> 0.81 us
    all_to_all x1, waiting for transfers between devices: 6.89 us -> 7.72 us  [per_device(): lax.all_to_all(sent, 'tile', 0, 0, tiled=True, axis_index_groups=cores)]
  transfers between devices with their start and end apart: 8 -> 8, of which waited for: 5 -> 5; matrix products, arithmetic and copies ran while one was open for 7% -> 7% of each run, Pallas kernels for 9% -> 10%
where the time goes in v5:
time: 66.5 us; the launch traced here: 66.1 us
  starting transfers between devices  27.1 us (41%)
  Pallas kernels  18.3 us (28%)
  waiting for transfers between devices  14.9 us (22%)
  matrix products  3.5 us (5%)
  local copies, waits for them, and re-layouts  0.9 us (1%)
  between operations  0.84 us (1%)
    ppermute x5, starting transfers between devices, all_sources(): lax.ppermute(value, 'src', [(i, i ^ mask) for i in range(SRC_DEVICES)])  11.3 us
    pallas_call x1, Pallas kernels, make_fields(): pl.pallas_call(fields_kernel, out_shape=(jax.ShapeDtypeStruct((ROWS, TILE...  10.4 us
    all_to_all x1, starting transfers between devices, per_device(): lax.all_to_all(make_rims(slot_pos, tile, col), 'tile', 0, 0, tiled=True)  8.34 us
    all_to_all x1, waiting for transfers between devices, per_device(): lax.all_to_all(sent, 'tile', 0, 0, tiled=True, axis_index_groups=cores)  7.72 us
    all_to_all x1, starting transfers between devices, per_device(): lax.all_to_all(sent, 'tile', 0, 0, tiled=True, axis_index_groups=cores)  4.31 us
    ppermute x5, waiting for transfers between devices, all_sources(): lax.ppermute(value, 'src', [(i, i ^ mask) for i in range(SRC_DEVICES)])  3.56 us
    ppermute x1, starting transfers between devices, per_device(): other = lax.ppermute(got, 'tile', [(i, i ^ 1) for i in range(TILES)])  3.22 us
    pallas_call x1, Pallas kernels, flip_tables(): pl.pallas_call(prep_kernel, out_shape=(jax.ShapeDtypeStruct(GRIDS.shape[:...  2.67 us
  transfers between devices with their start and end apart: 8, of which 5 were waited for; matrix products, arithmetic and copies ran while one was open for 7% of the time, Pallas kernels for 10%

profile of v5, /device:TPU:1, one launch (start us, length us, event | category | flops | bytes accessed | tf_op | source)
XLA Modules:
  0.0 66.1 jit_solution(9746182813327532745)
XLA Ops:
  0.6 0.0 copy-start.6
  0.6 0.0 copy-start.5
  0.7 7.8 %collective-permute-start.1 = (s32[2]{0:T(128)}, s32[2]{0:T(128)S(1)}, u32[]{:S(2)}, u32[]{:S(2)}) collective-permute-start(s32[2]{0:T(128)} %param.14), channel_id=1, source_target_pairs={{0,128},{32,160},{64,192},{96,224},{128,0},{160,32},{192,64},{224,... | collective-permute-start | bytes 32 | tf_op jit(solution)/shard_map/ppermute | solution.py:448
  8.5 0.8 %copy.16 = s32[2,2]{0,1:T(2,128)S(1)} copy(s32[2,2]{1,0:T(2,128)} %param.13) | data formatting | bytes 32 | tf_op args[2]
  9.2 0.0 collective-permute-start
  9.3 2.6 %rims.1 = bf16[32,64,128]{2,1,0:T(8,128)(2,1)} custom-call(s32[32]{0:T(128)} %slot_ref.5, bf16[1024,1024]{1,0:T(8,128)(2,1)} %bitcast.14, bf16[1024,128]{1,0:T(8,128)(2,1)} %constant.14.clone.col_hbm.col_ref), custom_call_target="tpu_custom_call" | custom-call | tf_op jit(solution)/shard_map/rims/pallas_call | solution.py:163
  11.8 0.0 copy-start
  11.9 8.3 %all-to-all-start = ((bf16[32,64,128]{2,1,0:T(8,128)(2,1)}), bf16[32,64,128]{2,1,0:T(8,128)(2,1)S(1)}, u32[]{:S(2)}, u32[]{:S(2)}) async-start(bf16[32,64,128]{2,1,0:T(8,128)(2,1)} %rims.1), calls=%async_computation | async-start | bytes 1048576 | tf_op jit(solution)/shard_map/all_to_all | solution.py:460
  20.2 0.0 copy-done.6
  20.2 0.0 copy-done.5
  20.2 0.2 select_multiply_fusion.1
  20.4 0.1 maximum_bitcast_fusion
  20.5 0.0 copy-start.2
  20.5 2.7 %prep.1 = (bf16[512,1024]{1,0:T(8,128)(2,1)}, bf16[256,256]{1,0:T(8,128)(2,1)}) custom-call(bf16[256,1152]{1,0:T(8,128)(2,1)} %constant.16.clone.small_hbm.small_ref, bf16[1024,512]{1,0:T(8,128)(2,1)} %constant.17.clone.grids_hbm), custom_call_target="tpu_custom_call" | custom-call | tf_op jit(solution)/shard_map/prep/pallas_call | solution.py:202
  23.2 0.0 copy-start.7
  23.2 0.0 copy-start.1
  23.2 0.0 copy-start.3
  23.3 0.0 copy-start.4
  23.3 0.0 copy-done
  23.3 2.5 %fusion.2 = f32[128,1024]{1,0:T(8,128)S(1)} fusion(bf16[1024,128]{1,0:T(8,128)(2,1)S(1)} %copy-done, bf16[1,1024,1024]{2,1,0:T(8,128)(2,1)} %param.11), kind=kOutput, calls=%fused_computation.10 | convolution fusion | flops 268435456 | bytes 2883584 | tf_op jit(solution)/shard_map/dot_general | solution.py:440
  25.8 0.0 copy-done.2
  25.8 1.0 %fusion.own_ref = f32[128,128]{1,0:T(8,128)S(1)} fusion(f32[128,1024]{1,0:T(8,128)S(1)} %fusion.2, f32[1152,128]{1,0:T(8,128)S(1)} %copy-done.2), kind=kOutput, calls=%fused_computation | convolution fusion | flops 201326592 | bytes 1114112 | tf_op jit(solution)/shard_map/dot_general | solution.py:442
  26.8 0.0 collective-permute-done.1
  26.8 0.0 copy-done.7
  26.8 0.1 add_bitcast_fusion
  26.9 0.0 collective-permute-done
  26.9 0.1 pad_add_fusion
  27.0 2.8 %collective-permute-start.4 = (s32[4,3]{0,1:T(4,128)S(1)}, s32[4,3]{0,1:T(4,128)S(1)}, u32[]{:S(2)}, u32[]{:S(2)}) collective-permute-start(s32[4,3]{0,1:T(4,128)S(1)} %pad_add_fusion), channel_id=1, source_target_pairs={{0,96},{32,64},{64,32},{96,0},{128,224},{160,192},{192,160},{224,1... | collective-permute-start | bytes 152 | tf_op jit(solution)/shard_map/ppermute | solution.py:448
  29.7 0.3 collective-permute-start.3
  30.1 0.3 collective-permute-start.2
  30.4 0.6 collective-permute-done.4
  31.0 3.0 %collective-permute-done.3 = s32[4,3]{0,1:T(4,128)S(1)} collective-permute-done((s32[4,3]{0,1:T(4,128)S(1)}, s32[4,3]{0,1:T(4,128)S(1)}, u32[]{:S(2)}, u32[]{:S(2)}) %collective-permute-start.3) | collective-permute-done | bytes 80 | tf_op jit(solution)/shard_map/ppermute | solution.py:448
  34.0 0.0 collective-permute-done.2
  34.0 0.1 pad_add_fusion.1
  34.1 0.1 copy.17.ints_ref
  34.2 2.5 %all-to-all-done.got_ref = bf16[32,64,128]{2,1,0:T(8,128)(2,1)S(1)} async-done(((bf16[32,64,128]{2,1,0:T(8,128)(2,1)}), bf16[32,64,128]{2,1,0:T(8,128)(2,1)S(1)}, u32[]{:S(2)}, u32[]{:S(2)}) %all-to-all-start) | async-done | bytes 524320 | tf_op jit(solution)/shard_map/all_to_all | solution.py:460
  36.6 0.0 copy-done.1
  36.6 0.0 copy-done.3
  36.6 0.0 copy-done.4
  36.6 10.4 %fields.1 = (f32[128,1024]{1,0:T(8,128)}, f32[128,128]{1,0:T(8,128)S(1)}, bf16[16,64,128]{2,1,0:T(8,128)(2,1)}) custom-call(s32[32]{0:T(128)S(1)} %copy-done.4, s32[16,3]{1,0:T(8,128)S(1)} %copy.17.ints_ref, bf16[32,64,128]{2,1,0:T(8,128)(2,1)S(1)} %all-to-all-done.got_ref, f32[128,128]{1,0:T(8,128)S(1)} %fusion.own_ref, ...), custom_call_target="tpu_custom_call" | custom-call | tf_op jit(solution)/shard_map/fields/pallas_call | solution.py:346
  47.1 4.3 %all-to-all-start.1 = ((bf16[16,64,128]{2,1,0:T(8,128)(2,1)}), bf16[16,64,128]{2,1,0:T(8,128)(2,1)S(1)}, u32[]{:S(2)}, u32[]{:S(2)}) async-start(bf16[16,64,128]{2,1,0:T(8,128)(2,1)} %get-tuple-element.14), calls=%async_computation.1 | async-start | bytes 524288 | tf_op jit(solution)/shard_map/all_to_all | solution.py:469
  51.4 1.1 %steps.1 = (f32[128,1024]{1,0:T(8,128)}, f32[64,1024]{1,0:T(8,128)S(1)}) custom-call(f32[128,128]{1,0:T(8,128)S(1)} %get-tuple-element.15.back_ref, bf16[1024,128]{1,0:T(8,128)(2,1)S(1)} %copy-done), custom_call_target="tpu_custom_call" | custom-call | tf_op jit(solution)/shard_map/steps/pallas_call | solution.py:385
  52.5 7.7 %all-to-all-done.1.got_ref = bf16[16,64,128]{2,1,0:T(8,128)(2,1)S(1)} async-done(((bf16[16,64,128]{2,1,0:T(8,128)(2,1)}), bf16[16,64,128]{2,1,0:T(8,128)(2,1)S(1)}, u32[]{:S(2)}, u32[]{:S(2)}) %all-to-all-start.1) | async-done | bytes 262176 | tf_op jit(solution)/shard_map/all_to_all | solution.py:469
  60.2 3.2 %collective-permute-start.5 = (bf16[16,64,128]{2,1,0:T(8,128)(2,1)S(1)}, bf16[16,64,128]{2,1,0:T(8,128)(2,1)S(1)}, u32[]{:S(2)}, u32[]{:S(2)}) collective-permute-start(bf16[16,64,128]{2,1,0:T(8,128)(2,1)S(1)} %all-to-all-done.1.got_ref), channel_id=1, source_target_pairs={{0,1},{1,0},{2,3},{3,2},{4,5},{5,4},{6,7},{7,6},{8,9},{9,8},{10,11... | collective-permute-start | bytes 786440 | tf_op jit(solution)/shard_map/ppermute | solution.py:472
  63.4 1.2 %collective-permute-done.5.other_ref = bf16[16,64,128]{2,1,0:T(8,128)(2,1)S(1)} collective-permute-done((bf16[16,64,128]{2,1,0:T(8,128)(2,1)S(1)}, bf16[16,64,128]{2,1,0:T(8,128)(2,1)S(1)}, u32[]{:S(2)}, u32[]{:S(2)}) %collective-permute-start.5) | collective-permute-done | bytes 262176 | tf_op jit(solution)/shard_map/ppermute | solution.py:472
  64.6 1.5 %edge.1 = f32[128,1024]{1,0:T(8,128)} custom-call(s32[32]{0:T(128)S(1)} %copy-done.4, bf16[16,64,128]{2,1,0:T(8,128)(2,1)S(1)} %all-to-all-done.1.got_ref, bf16[16,64,128]{2,1,0:T(8,128)(2,1)S(1)} %collective-permute-done.5.other_ref, f32[64,1024]{1,0:T(8,128)S(1)} %get-tuple-element.18.edge_ref, ...), custom_call_target="tpu_custom_call", output_to_operand_aliasing={{}: (5, {})} | custom-call | tf_op jit(solution)/shard_map/edge/pallas_call | solution.py:419
  (1 shorter events, 0.0 us)
Async XLA Ops:
  0.6 19.6 %copy-start.6 = (pred[64,64]{1,0:T(32,128)(4,1)S(1)}, pred[64,64]{1,0:T(32,128)(4,1)}, u32[]{:S(2)}) copy-start(pred[64,64]{1,0:T(32,128)(4,1)} %constant.18.clone) | copy-start | bytes 12292
  0.6 19.6 %copy-start.5 = (f32[128,128]{1,0:T(8,128)S(1)}, f32[128,128]{1,0:T(8,128)}, u32[]{:S(2)}) copy-start(f32[128,128]{1,0:T(8,128)} %param.15) | copy-start | bytes 196612
  0.7 26.2 %collective-permute-start.1 = (s32[2]{0:T(128)}, s32[2]{0:T(128)S(1)}, u32[]{:S(2)}, u32[]{:S(2)}) collective-permute-start(s32[2]{0:T(128)} %param.14), channel_id=1, source_target_pairs={{0,128},{32,160},{64,192},{96,224},{128,0},{160,32},{192,64},{224,... | collective-permute-start | bytes 32 | tf_op jit(solution)/shard_map/ppermute | solution.py:448
  9.2 17.7 %collective-permute-start = (s32[2,2]{0,1:T(2,128)S(1)}, s32[2,2]{0,1:T(2,128)S(1)}, u32[]{:S(2)}, u32[]{:S(2)}) collective-permute-start(s32[2,2]{0,1:T(2,128)S(1)} %copy.16), channel_id=1, source_target_pairs={{0,128},{32,160},{64,192},{96,224},{128,0},{160,32},{192,64},{224,... | collective-permute-start | bytes 56 | tf_op jit(solution)/shard_map/ppermute | solution.py:448
  11.8 11.4 %copy-start = (bf16[1024,128]{1,0:T(8,128)(2,1)S(1)}, bf16[1024,128]{1,0:T(8,128)(2,1)}, u32[]{:S(2)}) copy-start(bf16[1024,128]{1,0:T(8,128)(2,1)} %constant.14.clone.col_hbm.col_ref) | copy-start | bytes 786436
  11.9 24.8 %all-to-all-start = ((bf16[32,64,128]{2,1,0:T(8,128)(2,1)}), bf16[32,64,128]{2,1,0:T(8,128)(2,1)S(1)}, u32[]{:S(2)}, u32[]{:S(2)}) async-start(bf16[32,64,128]{2,1,0:T(8,128)(2,1)} %rims.1), calls=%async_computation | async-start | bytes 1048576 | tf_op jit(solution)/shard_map/all_to_all | solution.py:460
  20.5 5.3 %copy-start.2 = (f32[1152,128]{1,0:T(8,128)S(1)}, f32[1152,128]{1,0:T(8,128)}, u32[]{:S(2)}) copy-start(f32[1152,128]{1,0:T(8,128)} %constant.15.clone.row_ref) | copy-start | bytes 1769476
  23.2 3.6 %copy-start.7 = (s32[2]{0:T(128)S(1)}, s32[2]{0:T(128)}, u32[]{:S(2)}) copy-start(s32[2]{0:T(128)} %param.14) | copy-start | bytes 28
  23.2 13.4 %copy-start.1 = (bf16[256,1152]{1,0:T(8,128)(2,1)S(1)}, bf16[256,1152]{1,0:T(8,128)(2,1)}, u32[]{:S(2)}) copy-start(bf16[256,1152]{1,0:T(8,128)(2,1)} %constant.16.clone.small_hbm.small_ref) | copy-start | bytes 1769476
  23.2 13.4 %copy-start.3 = (bf16[256,256]{1,0:T(8,128)(2,1)S(1)}, bf16[256,256]{1,0:T(8,128)(2,1)}, u32[]{:S(2)}) copy-start(bf16[256,256]{1,0:T(8,128)(2,1)} %get-tuple-element.11.right_t_ref) | copy-start | bytes 393220
  23.3 13.4 %copy-start.4 = (s32[32]{0:T(128)S(1)}, s32[32]{0:T(128)}, u32[]{:S(2)}) copy-start(s32[32]{0:T(128)} %slot_ref.5) | copy-start | bytes 388
  27.0 4.0 %collective-permute-start.4 = (s32[4,3]{0,1:T(4,128)S(1)}, s32[4,3]{0,1:T(4,128)S(1)}, u32[]{:S(2)}, u32[]{:S(2)}) collective-permute-start(s32[4,3]{0,1:T(4,128)S(1)} %pad_add_fusion), channel_id=1, source_target_pairs={{0,96},{32,64},{64,32},{96,0},{128,224},{160,192},{192,160},{224,1... | collective-permute-start | bytes 152 | tf_op jit(solution)/shard_map/ppermute | solution.py:448
  29.7 4.2 %collective-permute-start.3 = (s32[4,3]{0,1:T(4,128)S(1)}, s32[4,3]{0,1:T(4,128)S(1)}, u32[]{:S(2)}, u32[]{:S(2)}) collective-permute-start(s32[4,3]{0,1:T(4,128)S(1)} %pad_add_fusion), channel_id=1, source_target_pairs={{0,64},{32,96},{64,0},{96,32},{128,192},{160,224},{192,128},{224,1... | collective-permute-start | bytes 152 | tf_op jit(solution)/shard_map/ppermute | solution.py:448
  30.1 3.9 %collective-permute-start.2 = (s32[4,3]{0,1:T(4,128)S(1)}, s32[4,3]{0,1:T(4,128)S(1)}, u32[]{:S(2)}, u32[]{:S(2)}) collective-permute-start(s32[4,3]{0,1:T(4,128)S(1)} %pad_add_fusion), channel_id=1, source_target_pairs={{0,32},{32,0},{64,96},{96,64},{128,160},{160,128},{192,224},{224,1... | collective-permute-start | bytes 152 | tf_op jit(solution)/shard_map/ppermute | solution.py:448
  47.1 13.2 %all-to-all-start.1 = ((bf16[16,64,128]{2,1,0:T(8,128)(2,1)}), bf16[16,64,128]{2,1,0:T(8,128)(2,1)S(1)}, u32[]{:S(2)}, u32[]{:S(2)}) async-start(bf16[16,64,128]{2,1,0:T(8,128)(2,1)} %get-tuple-element.14), calls=%async_computation.1 | async-start | bytes 524288 | tf_op jit(solution)/shard_map/all_to_all | solution.py:469
  60.2 4.4 %collective-permute-start.5 = (bf16[16,64,128]{2,1,0:T(8,128)(2,1)S(1)}, bf16[16,64,128]{2,1,0:T(8,128)(2,1)S(1)}, u32[]{:S(2)}, u32[]{:S(2)}) collective-permute-start(bf16[16,64,128]{2,1,0:T(8,128)(2,1)S(1)} %all-to-all-done.1.got_ref), channel_id=1, source_target_pairs={{0,1},{1,0},{2,3},{3,2},{4,5},{5,4},{6,7},{7,6},{8,9},{9,8},{10,11... | collective-permute-start | bytes 786440 | tf_op jit(solution)/shard_map/ppermute | solution.py:472

commit v6 on v5

--- a/solution.py
+++ b/solution.py
@@ -228,9 +228,12 @@
     fetches = [
         pltpu.make_async_copy(source, target, sems.at[number])
         for number, (source, target) in enumerate(
-            ((grids_hbm, grids_ref), (flipped_hbm, flipped_ref), (target_hbm, target_ref))
+            [(grids_hbm.at[:, pl.ds(0, 256)], grids_ref.at[:, pl.ds(0, 256)]), (flipped_hbm.at[pl.ds(256, 128)], flipped_ref.at[pl.ds(256, 128)])]
+            + [(target_hbm.at[pl.ds(256 * part, 256)], target_ref.at[pl.ds(256 * part, 256)]) for part in range(4)]
+            + [(grids_hbm.at[:, pl.ds(256, 256)], grids_ref.at[:, pl.ds(256, 256)]), (flipped_hbm.at[pl.ds(0, 256)], flipped_ref.at[pl.ds(0, 256)])]
         )
     ]
+    fetches = [fetches[number] for number in (0, 1, 6, 2, 3, 4, 5, 7)]
     for fetch in fetches:
         fetch.start()
     my_slot, my_src, above, below = places(slot_ref)
@@ -275,11 +278,10 @@
         coarse = coarse + weight * (squared[:, :GRID] + squared[:, GRID:])
     coarse_h, coarse_l = halves(coarse)
     coarse_hh = jnp.concatenate([coarse_h, coarse_h], axis=0)
-    for fetch in fetches:
+    for fetch in fetches[:3]:
         fetch.wait()
     grid_x = grids_ref[:, 256:512]
     grid_xhh = jnp.concatenate([flipped_ref[256:384, :], flipped_ref[256:384, :]], axis=0)
-    grid_yt = flipped_ref[0:256, :]
     chunk = 256
     for place in range(TILE_PX // chunk):
         rows = pl.ds(place * chunk, chunk)
@@ -288,14 +290,16 @@
         intensity = dot(jnp.concatenate([rows_h, rows_l], axis=1), grid_xhh)
         resist = jax.nn.sigmoid(STEEPNESS * (intensity - THRESHOLD))
         resist_ref[rows, :] = resist
+        fetches[3 + place].wait()
         wanted = target_ref[rows, :].astype(jnp.float32)
         adjoint = ((2.0 * STEEPNESS) * (resist - wanted) * resist * (1.0 - resist)).astype(jnp.bfloat16)
         folded = dot(adjoint, grid_x)
         fold_ref[rows, :] = jnp.concatenate(halves(folded[:, :GRID] + folded[:, GRID:]), axis=1)
     mine = pl.multiple_of(my_src * ROWS, ROWS)
-    keep = pltpu.make_async_copy(resist_ref.at[pl.ds(mine, ROWS)], resist_hbm, sems.at[3])
+    keep = pltpu.make_async_copy(resist_ref.at[pl.ds(mine, ROWS)], resist_hbm, sems.at[8])
     keep.start()
-    adjoint4 = dot(grid_yt, fold_ref[...])
+    fetches[7].wait()
+    adjoint4 = dot(flipped_ref[0:256, :], fold_ref[...])
     adjoint2 = adjoint4[:GRID] + adjoint4[GRID:]
     coarse_adjoint = 2.0 * (adjoint2[:, :GRID] + adjoint2[:, GRID:])
     right_t = right_t_ref[...]
@@ -334,7 +338,7 @@
     @pl.when(goes_to >= 0)
     def _():
         edge_ref[...] = back[:HALO].astype(jnp.bfloat16)
-        send = pltpu.make_async_copy(edge_ref, sent_hbm.at[goes_to // 2], sems.at[4])
+        send = pltpu.make_async_copy(edge_ref, sent_hbm.at[goes_to // 2], sems.at[9])
         send.start()
         send.wait()
 
@@ -362,7 +366,7 @@
             pltpu.VMEM((SOURCES, GRID, 2 * GRID), jnp.float32),
             pltpu.VMEM((TILE_PX, 2 * GRID), jnp.bfloat16),
             pltpu.VMEM((2, FREQ, FREQ), jnp.float32),
-            pltpu.SemaphoreType.DMA((5,)),
+            pltpu.SemaphoreType.DMA((10,)),
         ],
         compiler_params=pltpu.CompilerParams(vmem_limit_bytes=FIELDS_VMEM),
         interpret=INTERPRET,
@@ -444,23 +448,29 @@
     )
 
 
-def all_sources(src_shift, src_weight):
-    swap = lambda value, mask: lax.ppermute(value, "src", [(i, i ^ mask) for i in range(SRC_DEVICES)])
-    shifts = jnp.concatenate([src_shift, swap(src_shift, 4)], axis=0)
-    weights = jnp.concatenate([src_weight, swap(src_weight, 4)], axis=0)
-    ints = jnp.concatenate([shifts, weights[:, None]], axis=1)
-    return jnp.concatenate([ints] + [swap(ints, mask) for mask in (1, 2, 3)], axis=0)
+def swap_src(value, mask):
+    return lax.ppermute(value, "src", [(i, i ^ mask) for i in range(SRC_DEVICES)])
+
+
+def pair_sources(src_shift, src_weight):
+    shifts = jnp.concatenate([src_shift, swap_src(src_shift, 4)], axis=0)
+    weights = jnp.concatenate([src_weight, swap_src(src_weight, 4)], axis=0)
+    return jnp.concatenate([shifts, weights[:, None]], axis=1)
+
+
+def all_sources(pair):
+    return jnp.concatenate([pair] + [swap_src(pair, mask) for mask in (1, 2, 3)], axis=0)
 
 
 def per_device(mask_tiles, slot_pos, src_shift, src_weight, pupil_phase, target):
-    ints = all_sources(src_shift, src_weight)
+    pair = pair_sources(src_shift, src_weight)
     col = jnp.asarray(COL)
     row_table = lax.optimization_barrier(jnp.asarray(ROW_F32))
     tile = mask_tiles[0]
     got = lax.all_to_all(make_rims(slot_pos, tile, col), "tile", 0, 0, tiled=True)
-    own = own_moments(tile, col, row_table)
-    small = jnp.asarray(SMALL)
-    grids = jnp.asarray(GRIDS)
+    pair, col_after, small, grids = lax.optimization_barrier((pair, col, jnp.asarray(SMALL), jnp.asarray(GRIDS)))
+    ints = all_sources(pair)
+    own = own_moments(tile, col_after, row_table)
     flipped, right_t = flip_tables(small, grids)
     resist, back, sent = make_fields(
         slot_pos, ints, got, own, pupil_tables(pupil_phase), small, right_t, row_table, grids, flipped, target[0]

time: 66.5 us -> 65.5 us (0.985)
  starting transfers between devices: 27.1 us -> 24.8 us
  waiting for transfers between devices: 14.9 us -> 16.2 us
    all_to_all x1, waiting for transfers between devices: 2.46 us -> 6.07 us  [per_device(): lax.all_to_all(make_rims(slot_pos, tile, col), 'tile', 0, 0, tiled=True)]
    ppermute x5, waiting for transfers between devices: 3.56 us -> 0.01 us  [swap_src(): lax.ppermute(value, 'src', [(i, i ^ mask) for i in range(SRC_DEVICES)])]
    ppermute x1, starting transfers between devices: 3.22 us -> 1.59 us  [per_device(): other = lax.ppermute(got, 'tile', [(i, i ^ 1) for i in range(TILES)])]
    all_to_all x1, waiting for transfers between devices: 7.72 us -> 8.92 us  [per_device(): lax.all_to_all(sent, 'tile', 0, 0, tiled=True, axis_index_groups=cores)]
    all_to_all x1, starting transfers between devices: 4.31 us -> 3.57 us  [per_device(): lax.all_to_all(sent, 'tile', 0, 0, tiled=True, axis_index_groups=cores)]
  transfers between devices with their start and end apart: 8 -> 8, of which waited for: 5 -> 3; matrix products, arithmetic and copies ran while one was open for 7% -> 7% of each run, Pallas kernels for 10% -> 10%
where the time goes in v6:
time: 65.5 us; the launch traced here: 65.1 us
  starting transfers between devices  24.8 us (38%)
  Pallas kernels  18.2 us (28%)
  waiting for transfers between devices  16.2 us (25%)
  matrix products  3.49 us (5%)
  between operations  1.01 us (2%)
  local copies, waits for them, and re-layouts  0.9 us (1%)
    ppermute x5, starting transfers between devices, swap_src(): lax.ppermute(value, 'src', [(i, i ^ mask) for i in range(SRC_DEVICES)])  11.3 us
    pallas_call x1, Pallas kernels, make_fields(): pl.pallas_call(fields_kernel, out_shape=(jax.ShapeDtypeStruct((ROWS, TILE...  10.2 us
    all_to_all x1, waiting for transfers between devices, per_device(): lax.all_to_all(sent, 'tile', 0, 0, tiled=True, axis_index_groups=cores)  8.92 us
    all_to_all x1, starting transfers between devices, per_device(): lax.all_to_all(make_rims(slot_pos, tile, col), 'tile', 0, 0, tiled=True)  8.34 us
    all_to_all x1, waiting for transfers between devices, per_device(): lax.all_to_all(make_rims(slot_pos, tile, col), 'tile', 0, 0, tiled=True)  6.07 us
    all_to_all x1, starting transfers between devices, per_device(): lax.all_to_all(sent, 'tile', 0, 0, tiled=True, axis_index_groups=cores)  3.57 us
    pallas_call x1, Pallas kernels, make_rims(): pl.pallas_call(rims_kernel, out_shape=jax.ShapeDtypeStruct((TILES, HALO,...  2.71 us
    pallas_call x1, Pallas kernels, flip_tables(): pl.pallas_call(prep_kernel, out_shape=(jax.ShapeDtypeStruct(GRIDS.shape[:...  2.6 us
  transfers between devices with their start and end apart: 8, of which 3 were waited for; matrix products, arithmetic and copies ran while one was open for 7% of the time, Pallas kernels for 10%

profile of v6, /device:TPU:1, one launch (start us, length us, event | category | flops | bytes accessed | tf_op | source)
XLA Modules:
  0.0 65.1 jit_solution(8986476873150202922)
XLA Ops:
  0.6 0.0 copy-start.6
  0.6 0.0 copy-start.5
  0.7 7.8 %collective-permute-start.1 = (s32[2]{0:T(128)}, s32[2]{0:T(128)S(1)}, u32[]{:S(2)}, u32[]{:S(2)}) collective-permute-start(s32[2]{0:T(128)} %param.14), channel_id=1, source_target_pairs={{0,128},{32,160},{64,192},{96,224},{128,0},{160,32},{192,64},{224,... | collective-permute-start | bytes 32 | tf_op jit(solution)/shard_map/ppermute | solution.py:452
  8.5 0.8 %copy.16 = s32[2,2]{0,1:T(2,128)S(1)} copy(s32[2,2]{1,0:T(2,128)} %param.13) | data formatting | bytes 32 | tf_op args[2]
  9.2 0.0 collective-permute-start
  9.3 0.0 copy-start.7
  9.3 2.7 %rims.1 = bf16[32,64,128]{2,1,0:T(8,128)(2,1)} custom-call(s32[32]{0:T(128)} %slot_ref.5, bf16[1024,1024]{1,0:T(8,128)(2,1)} %bitcast.14, bf16[1024,128]{1,0:T(8,128)(2,1)} %constant.14.clone.col_hbm.col_ref), custom_call_target="tpu_custom_call" | custom-call | tf_op jit(solution)/shard_map/rims/pallas_call | solution.py:163
  12.0 0.0 copy-start
  12.0 8.3 %all-to-all-start = ((bf16[32,64,128]{2,1,0:T(8,128)(2,1)}), bf16[32,64,128]{2,1,0:T(8,128)(2,1)S(1)}, u32[]{:S(2)}, u32[]{:S(2)}) async-start(bf16[32,64,128]{2,1,0:T(8,128)(2,1)} %rims.1), calls=%async_computation | async-start | bytes 1048576 | tf_op jit(solution)/shard_map/all_to_all | solution.py:470
  20.3 0.0 copy-done.6
  20.3 0.0 copy-done.5
  20.4 0.2 select_multiply_fusion.1
  20.6 0.1 maximum_bitcast_fusion
  20.7 0.0 collective-permute-done.1
  20.7 0.0 copy-done.7
  20.7 0.1 add_bitcast_fusion
  20.8 0.0 collective-permute-done
  20.8 0.1 pad_add_fusion
  20.9 0.0 copy-start.2
  20.9 2.8 %collective-permute-start.4 = (s32[4,3]{0,1:T(4,128)S(1)}, s32[4,3]{0,1:T(4,128)S(1)}, u32[]{:S(2)}, u32[]{:S(2)}) collective-permute-start(s32[4,3]{0,1:T(4,128)S(1)} %pad_add_fusion), channel_id=1, source_target_pairs={{0,96},{32,64},{64,32},{96,0},{128,224},{160,192},{192,160},{224,1... | collective-permute-start | bytes 152 | tf_op jit(solution)/shard_map/ppermute | solution.py:452
  23.6 0.3 collective-permute-start.3
  24.0 0.3 collective-permute-start.2
  24.3 2.6 %prep.1 = (bf16[512,1024]{1,0:T(8,128)(2,1)}, bf16[256,256]{1,0:T(8,128)(2,1)}) custom-call(bf16[256,1152]{1,0:T(8,128)(2,1)} %constant.16.clone.small_hbm.small_ref, bf16[1024,512]{1,0:T(8,128)(2,1)} %constant.17.clone.grids_hbm), custom_call_target="tpu_custom_call" | custom-call | tf_op jit(solution)/shard_map/prep/pallas_call | solution.py:202
  26.9 0.0 copy-done
  26.9 0.0 copy-start.1
  26.9 0.0 copy-start.3
  26.9 0.0 copy-start.4
  27.0 2.5 %fusion.2 = f32[128,1024]{1,0:T(8,128)S(1)} fusion(bf16[1024,128]{1,0:T(8,128)(2,1)S(1)} %copy-done, bf16[1,1024,1024]{2,1,0:T(8,128)(2,1)} %param.11), kind=kOutput, calls=%fused_computation.10 | convolution fusion | flops 268435456 | bytes 2883584 | tf_op jit(solution)/shard_map/dot_general | solution.py:444
  29.4 0.0 copy-done.2
  29.5 1.0 %fusion.own_ref = f32[128,128]{1,0:T(8,128)S(1)} fusion(f32[128,1024]{1,0:T(8,128)S(1)} %fusion.2, f32[1152,128]{1,0:T(8,128)S(1)} %copy-done.2), kind=kOutput, calls=%fused_computation | convolution fusion | flops 201326592 | bytes 1114112 | tf_op jit(solution)/shard_map/dot_general | solution.py:446
  30.5 0.0 collective-permute-done.4
  30.5 0.0 collective-permute-done.3
  30.5 0.0 collective-permute-done.2
  30.5 0.1 pad_add_fusion.1
  30.6 0.1 copy.17.ints_ref
  30.7 6.1 %all-to-all-done.got_ref = bf16[32,64,128]{2,1,0:T(8,128)(2,1)S(1)} async-done(((bf16[32,64,128]{2,1,0:T(8,128)(2,1)}), bf16[32,64,128]{2,1,0:T(8,128)(2,1)S(1)}, u32[]{:S(2)}, u32[]{:S(2)}) %all-to-all-start) | async-done | bytes 524320 | tf_op jit(solution)/shard_map/all_to_all | solution.py:470
  36.7 0.0 copy-done.1
  36.7 0.0 copy-done.3
  36.7 0.0 copy-done.4
  36.8 10.2 %fields.1 = (f32[128,1024]{1,0:T(8,128)}, f32[128,128]{1,0:T(8,128)S(1)}, bf16[16,64,128]{2,1,0:T(8,128)(2,1)}) custom-call(s32[32]{0:T(128)S(1)} %copy-done.4, s32[16,3]{1,0:T(8,128)S(1)} %copy.17.ints_ref, bf16[32,64,128]{2,1,0:T(8,128)(2,1)S(1)} %all-to-all-done.got_ref, f32[128,128]{1,0:T(8,128)S(1)} %fusion.own_ref, ...), custom_call_target="tpu_custom_call" | custom-call | tf_op jit(solution)/shard_map/fields/pallas_call | solution.py:350
  47.0 3.6 %all-to-all-start.1 = ((bf16[16,64,128]{2,1,0:T(8,128)(2,1)}), bf16[16,64,128]{2,1,0:T(8,128)(2,1)S(1)}, u32[]{:S(2)}, u32[]{:S(2)}) async-start(bf16[16,64,128]{2,1,0:T(8,128)(2,1)} %get-tuple-element.22), calls=%async_computation.1 | async-start | bytes 524288 | tf_op jit(solution)/shard_map/all_to_all | solution.py:479
  50.6 1.1 %steps.1 = (f32[128,1024]{1,0:T(8,128)}, f32[64,1024]{1,0:T(8,128)S(1)}) custom-call(f32[128,128]{1,0:T(8,128)S(1)} %get-tuple-element.23.back_ref, bf16[1024,128]{1,0:T(8,128)(2,1)S(1)} %copy-done), custom_call_target="tpu_custom_call" | custom-call | tf_op jit(solution)/shard_map/steps/pallas_call | solution.py:389
  51.7 8.9 %all-to-all-done.1.got_ref = bf16[16,64,128]{2,1,0:T(8,128)(2,1)S(1)} async-done(((bf16[16,64,128]{2,1,0:T(8,128)(2,1)}), bf16[16,64,128]{2,1,0:T(8,128)(2,1)S(1)}, u32[]{:S(2)}, u32[]{:S(2)}) %all-to-all-start.1) | async-done | bytes 262176 | tf_op jit(solution)/shard_map/all_to_all | solution.py:479
  60.6 1.6 %collective-permute-start.5 = (bf16[16,64,128]{2,1,0:T(8,128)(2,1)S(1)}, bf16[16,64,128]{2,1,0:T(8,128)(2,1)S(1)}, u32[]{:S(2)}, u32[]{:S(2)}) collective-permute-start(bf16[16,64,128]{2,1,0:T(8,128)(2,1)S(1)} %all-to-all-done.1.got_ref), channel_id=1, source_target_pairs={{0,1},{1,0},{2,3},{3,2},{4,5},{5,4},{6,7},{7,6},{8,9},{9,8},{10,11... | collective-permute-start | bytes 786440 | tf_op jit(solution)/shard_map/ppermute | solution.py:482
  62.2 1.2 %collective-permute-done.5.other_ref = bf16[16,64,128]{2,1,0:T(8,128)(2,1)S(1)} collective-permute-done((bf16[16,64,128]{2,1,0:T(8,128)(2,1)S(1)}, bf16[16,64,128]{2,1,0:T(8,128)(2,1)S(1)}, u32[]{:S(2)}, u32[]{:S(2)}) %collective-permute-start.5) | collective-permute-done | bytes 262176 | tf_op jit(solution)/shard_map/ppermute | solution.py:482
  63.4 1.5 %edge.1 = f32[128,1024]{1,0:T(8,128)} custom-call(s32[32]{0:T(128)S(1)} %copy-done.4, bf16[16,64,128]{2,1,0:T(8,128)(2,1)S(1)} %all-to-all-done.1.got_ref, bf16[16,64,128]{2,1,0:T(8,128)(2,1)S(1)} %collective-permute-done.5.other_ref, f32[64,1024]{1,0:T(8,128)S(1)} %get-tuple-element.26.edge_ref, ...), custom_call_target="tpu_custom_call", output_to_operand_aliasing={{}: (5, {})} | custom-call | tf_op jit(solution)/shard_map/edge/pallas_call | solution.py:423
  (1 shorter events, 0.0 us)
Async XLA Ops:
  0.6 19.7 %copy-start.6 = (pred[64,64]{1,0:T(32,128)(4,1)S(1)}, pred[64,64]{1,0:T(32,128)(4,1)}, u32[]{:S(2)}) copy-start(pred[64,64]{1,0:T(32,128)(4,1)} %constant.18.clone) | copy-start | bytes 12292
  0.6 19.7 %copy-start.5 = (f32[128,128]{1,0:T(8,128)S(1)}, f32[128,128]{1,0:T(8,128)}, u32[]{:S(2)}) copy-start(f32[128,128]{1,0:T(8,128)} %param.15) | copy-start | bytes 196612
  0.7 20.0 %collective-permute-start.1 = (s32[2]{0:T(128)}, s32[2]{0:T(128)S(1)}, u32[]{:S(2)}, u32[]{:S(2)}) collective-permute-start(s32[2]{0:T(128)} %param.14), channel_id=1, source_target_pairs={{0,128},{32,160},{64,192},{96,224},{128,0},{160,32},{192,64},{224,... | collective-permute-start | bytes 32 | tf_op jit(solution)/shard_map/ppermute | solution.py:452
  9.2 11.5 %collective-permute-start = (s32[2,2]{0,1:T(2,128)S(1)}, s32[2,2]{0,1:T(2,128)S(1)}, u32[]{:S(2)}, u32[]{:S(2)}) collective-permute-start(s32[2,2]{0,1:T(2,128)S(1)} %copy.16), channel_id=1, source_target_pairs={{0,128},{32,160},{64,192},{96,224},{128,0},{160,32},{192,64},{224,... | collective-permute-start | bytes 56 | tf_op jit(solution)/shard_map/ppermute | solution.py:452
  9.3 11.4 %copy-start.7 = (s32[2]{0:T(128)S(1)}, s32[2]{0:T(128)}, u32[]{:S(2)}) copy-start(s32[2]{0:T(128)} %param.14) | copy-start | bytes 28
  12.0 14.9 %copy-start = (bf16[1024,128]{1,0:T(8,128)(2,1)S(1)}, bf16[1024,128]{1,0:T(8,128)(2,1)}, u32[]{:S(2)}) copy-start(bf16[1024,128]{1,0:T(8,128)(2,1)} %constant.14.clone.col_hbm.col_ref) | copy-start | bytes 786436
  12.0 24.7 %all-to-all-start = ((bf16[32,64,128]{2,1,0:T(8,128)(2,1)}), bf16[32,64,128]{2,1,0:T(8,128)(2,1)S(1)}, u32[]{:S(2)}, u32[]{:S(2)}) async-start(bf16[32,64,128]{2,1,0:T(8,128)(2,1)} %rims.1), calls=%async_computation | async-start | bytes 1048576 | tf_op jit(solution)/shard_map/all_to_all | solution.py:470
  20.9 8.6 %copy-start.2 = (f32[1152,128]{1,0:T(8,128)S(1)}, f32[1152,128]{1,0:T(8,128)}, u32[]{:S(2)}) copy-start(f32[1152,128]{1,0:T(8,128)} %constant.15.clone.row_ref) | copy-start | bytes 1769476
  20.9 9.6 %collective-permute-start.4 = (s32[4,3]{0,1:T(4,128)S(1)}, s32[4,3]{0,1:T(4,128)S(1)}, u32[]{:S(2)}, u32[]{:S(2)}) collective-permute-start(s32[4,3]{0,1:T(4,128)S(1)} %pad_add_fusion), channel_id=1, source_target_pairs={{0,96},{32,64},{64,32},{96,0},{128,224},{160,192},{192,160},{224,1... | collective-permute-start | bytes 152 | tf_op jit(solution)/shard_map/ppermute | solution.py:452
  23.6 6.9 %collective-permute-start.3 = (s32[4,3]{0,1:T(4,128)S(1)}, s32[4,3]{0,1:T(4,128)S(1)}, u32[]{:S(2)}, u32[]{:S(2)}) collective-permute-start(s32[4,3]{0,1:T(4,128)S(1)} %pad_add_fusion), channel_id=1, source_target_pairs={{0,64},{32,96},{64,0},{96,32},{128,192},{160,224},{192,128},{224,1... | collective-permute-start | bytes 152 | tf_op jit(solution)/shard_map/ppermute | solution.py:452
  24.0 6.5 %collective-permute-start.2 = (s32[4,3]{0,1:T(4,128)S(1)}, s32[4,3]{0,1:T(4,128)S(1)}, u32[]{:S(2)}, u32[]{:S(2)}) collective-permute-start(s32[4,3]{0,1:T(4,128)S(1)} %pad_add_fusion), channel_id=1, source_target_pairs={{0,32},{32,0},{64,96},{96,64},{128,160},{160,128},{192,224},{224,1... | collective-permute-start | bytes 152 | tf_op jit(solution)/shard_map/ppermute | solution.py:452
  26.9 9.8 %copy-start.1 = (bf16[256,1152]{1,0:T(8,128)(2,1)S(1)}, bf16[256,1152]{1,0:T(8,128)(2,1)}, u32[]{:S(2)}) copy-start(bf16[256,1152]{1,0:T(8,128)(2,1)} %constant.16.clone.small_hbm.small_ref) | copy-start | bytes 1769476
  26.9 9.8 %copy-start.3 = (bf16[256,256]{1,0:T(8,128)(2,1)S(1)}, bf16[256,256]{1,0:T(8,128)(2,1)}, u32[]{:S(2)}) copy-start(bf16[256,256]{1,0:T(8,128)(2,1)} %get-tuple-element.19.right_t_ref) | copy-start | bytes 393220
  26.9 9.8 %copy-start.4 = (s32[32]{0:T(128)S(1)}, s32[32]{0:T(128)}, u32[]{:S(2)}) copy-start(s32[32]{0:T(128)} %slot_ref.5) | copy-start | bytes 388
  47.0 13.6 %all-to-all-start.1 = ((bf16[16,64,128]{2,1,0:T(8,128)(2,1)}), bf16[16,64,128]{2,1,0:T(8,128)(2,1)S(1)}, u32[]{:S(2)}, u32[]{:S(2)}) async-start(bf16[16,64,128]{2,1,0:T(8,128)(2,1)} %get-tuple-element.22), calls=%async_computation.1 | async-start | bytes 524288 | tf_op jit(solution)/shard_map/all_to_all | solution.py:479
  60.6 2.8 %collective-permute-start.5 = (bf16[16,64,128]{2,1,0:T(8,128)(2,1)S(1)}, bf16[16,64,128]{2,1,0:T(8,128)(2,1)S(1)}, u32[]{:S(2)}, u32[]{:S(2)}) collective-permute-start(bf16[16,64,128]{2,1,0:T(8,128)(2,1)S(1)} %all-to-all-done.1.got_ref), channel_id=1, source_target_pairs={{0,1},{1,0},{2,3},{3,2},{4,5},{5,4},{6,7},{7,6},{8,9},{9,8},{10,11... | collective-permute-start | bytes 786440 | tf_op jit(solution)/shard_map/ppermute | solution.py:482

commit v7 on v6

--- a/solution.py
+++ b/solution.py
@@ -77,7 +77,6 @@
 )
 LEFT_T = np.concatenate(split(np.concatenate([COS_W.T, SIN_W.T], axis=0)), axis=0)
 RIM = np.concatenate(split(np.concatenate([ROW[:HALO], ROW[EXT_PX - HALO :]], axis=0).T), axis=1)
-LANES = np.concatenate([EVEN, ODD], axis=1)
 SMALL = np.concatenate(
     [
         UNFOLD.astype(BF16),
@@ -85,7 +84,7 @@
         RIGHT,
         LEFT_T,
         np.concatenate([RIM, UNFOLD.T.astype(BF16)], axis=0),
-        np.concatenate([LANES, np.zeros_like(LANES)], axis=0).astype(BF16),
+        RIGHT.T,
     ],
     axis=1,
 )
@@ -123,7 +122,9 @@
     return my_slot, lax.axis_index("src"), above, below
 
 
-def rims_kernel(slot_ref, tile_hbm, col_hbm, sent_hbm, rows_ref, col_ref, rims_ref, sems):
+def rims_kernel(
+    slot_ref, shift_ref, weight_ref, tile_hbm, col_hbm, sent_hbm, ints_hbm, rows_ref, col_ref, rims_ref, ints_ref, sems
+):
     copies = [
         pltpu.make_async_copy(col_hbm, col_ref, sems.at[0]),
         pltpu.make_async_copy(tile_hbm.at[pl.ds(0, HALO)], rows_ref.at[pl.ds(0, HALO)], sems.at[1]),
@@ -134,6 +135,15 @@
     for copy in copies:
         copy.start()
     my_slot, my_src, above, below = places(slot_ref)
+    row = lax.broadcasted_iota(jnp.int32, ints_ref.shape, 0) - 2 * my_src
+    lane = lax.broadcasted_iota(jnp.int32, ints_ref.shape, 1)
+    table = jnp.zeros(ints_ref.shape, jnp.int32)
+    for source in range(2):
+        for place, value in enumerate((shift_ref[source, 0], shift_ref[source, 1], weight_ref[source])):
+            table = jnp.where((row == source) & (lane == place), value, table)
+    ints_ref[...] = table
+    ints_keep = pltpu.make_async_copy(ints_ref, ints_hbm, sems.at[5])
+    ints_keep.start()
     for copy in copies:
         copy.wait()
     rims_ref[...] = dot(rows_ref[...], col_ref[...]).astype(jnp.bfloat16).reshape(2, HALO, 128)
@@ -149,6 +159,8 @@
         @pl.when(slot >= 0)
         def _():
             pltpu.make_async_copy(rims_ref.at[number], sent_hbm.at[slot], sems.at[3 + number]).wait()
+
+    ints_keep.wait()
 
 
 SCALARS = pl.BlockSpec(memory_space=pltpu.SMEM)
@@ -159,69 +171,57 @@
 FIELDS_VMEM = 54_000_000
 
 
-def make_rims(slot_pos, tile, col):
+def make_rims(slot_pos, src_shift, src_weight, tile, col):
     return pl.pallas_call(
         rims_kernel,
-        out_shape=jax.ShapeDtypeStruct((TILES, HALO, 128), jnp.bfloat16),
-        in_specs=[SCALARS, LEFT_THERE, LEFT_THERE],
-        out_specs=LEFT_THERE,
+        out_shape=(
+            jax.ShapeDtypeStruct((TILES, HALO, 128), jnp.bfloat16),
+            jax.ShapeDtypeStruct((SOURCES, 128), jnp.int32),
+        ),
+        in_specs=[SCALARS, SCALARS, SCALARS, LEFT_THERE, LEFT_THERE],
+        out_specs=[LEFT_THERE, LEFT_THERE],
         scratch_shapes=[
             pltpu.VMEM((2 * HALO, TILE_PX), jnp.bfloat16),
             pltpu.VMEM((TILE_PX, 128), jnp.bfloat16),
             pltpu.VMEM((2, HALO, 128), jnp.bfloat16),
-            pltpu.SemaphoreType.DMA((5,)),
+            pltpu.VMEM((SOURCES, 128), jnp.int32),
+            pltpu.SemaphoreType.DMA((6,)),
         ],
         compiler_params=pltpu.CompilerParams(vmem_limit_bytes=ALL_VMEM),
         interpret=INTERPRET,
         name="rims",
-    )(slot_pos, tile, col)
-
-
-def prep_kernel(small_hbm, grids_hbm, flipped_hbm, right_t_hbm, small_ref, grids_ref, flipped_ref, right_t_ref, sems):
-    fetches = [
-        pltpu.make_async_copy(grids_hbm, grids_ref, sems.at[0]),
-        pltpu.make_async_copy(small_hbm.at[:, pl.ds(384, 256)], small_ref, sems.at[1]),
-    ]
-    keeps = [
-        pltpu.make_async_copy(flipped_ref, flipped_hbm, sems.at[2]),
-        pltpu.make_async_copy(right_t_ref, right_t_hbm, sems.at[3]),
-    ]
-    for fetch in fetches:
-        fetch.start()
-    fetches[0].wait()
+    )(slot_pos, src_shift, src_weight, tile, col)
+
+
+def prep_kernel(grids_hbm, flipped_hbm, grids_ref, flipped_ref, sems):
+    fetch = pltpu.make_async_copy(grids_hbm, grids_ref, sems.at[0])
+    fetch.start()
+    fetch.wait()
     flipped_ref[...] = grids_ref[...].T
-    keeps[0].start()
-    fetches[1].wait()
-    right_t_ref[...] = small_ref[...].T
-    keeps[1].start()
-    for keep in keeps:
-        keep.wait()
-
-
-def flip_tables(small, grids):
+    keep = pltpu.make_async_copy(flipped_ref, flipped_hbm, sems.at[1])
+    keep.start()
+    keep.wait()
+
+
+def flip_tables(grids):
     return pl.pallas_call(
         prep_kernel,
-        out_shape=(
-            jax.ShapeDtypeStruct(GRIDS.shape[::-1], jnp.bfloat16),
-            jax.ShapeDtypeStruct((256, 256), jnp.bfloat16),
-        ),
-        in_specs=[LEFT_THERE] * 2,
-        out_specs=[LEFT_THERE] * 2,
+        out_shape=jax.ShapeDtypeStruct(GRIDS.shape[::-1], jnp.bfloat16),
+        in_specs=[LEFT_THERE],
+        out_specs=LEFT_THERE,
         scratch_shapes=[
-            pltpu.VMEM((256, 256), jnp.bfloat16),
             pltpu.VMEM(GRIDS.shape, jnp.bfloat16),
             pltpu.VMEM(GRIDS.shape[::-1], jnp.bfloat16),
-            pltpu.VMEM((256, 256), jnp.bfloat16),
-            pltpu.SemaphoreType.DMA((4,)),
+            pltpu.SemaphoreType.DMA((2,)),
         ],
         compiler_params=pltpu.CompilerParams(vmem_limit_bytes=ALL_VMEM),
         interpret=INTERPRET,
         name="prep",
-    )(small, grids)
+    )(grids)
 
 
 def fields_kernel(
-    slot_ref, ints_ref, got_ref, own_ref, pupil_ref, small_ref, right_t_ref, row_ref, grids_hbm, flipped_hbm, target_hbm,
+    slot_ref, ints_ref, got_ref, own_ref, pupil_ref, small_ref, row_ref, grids_hbm, flipped_hbm, target_hbm,
     resist_hbm, back_ref, sent_hbm,
     edge_ref, grids_ref, flipped_ref, target_ref, resist_ref, spec_ref, field_ref, fold_ref, grad_ref, sems,
 ):
@@ -243,7 +243,7 @@
     left_t = small_ref[:, 640:768]
     rim_table = small_ref[:128, 768:1024]
     unfold_t = small_ref[128:, 768:1024]
-    lanes = small_ref[:128, 1024:1152]
+    lanes = unfold[:128] + unfold[128:]
     lanes2 = jnp.concatenate([lanes, lanes], axis=1)
     low = low_lanes((128, 128))
     low_w = low_lanes((64, 128))
@@ -302,7 +302,7 @@
     adjoint4 = dot(flipped_ref[0:256, :], fold_ref[...])
     adjoint2 = adjoint4[:GRID] + adjoint4[GRID:]
     coarse_adjoint = 2.0 * (adjoint2[:, :GRID] + adjoint2[:, GRID:])
-    right_t = right_t_ref[...]
+    right_t = small_ref[:, 1024:1280]
     grad_ref[...] = jnp.zeros(grad_ref.shape, jnp.float32)
     for source in range(SOURCES):
         shift_a = ints_ref[source, 0]
@@ -354,7 +354,7 @@
             jax.ShapeDtypeStruct((ROWS, 128), jnp.float32),
             jax.ShapeDtypeStruct((TILES // 2, HALO, 128), jnp.bfloat16),
         ),
-        in_specs=[SCALARS, SCALARS] + [WHOLE] * 6 + [LEFT_THERE] * 3,
+        in_specs=[SCALARS, SCALARS] + [WHOLE] * 5 + [LEFT_THERE] * 3,
         out_specs=[LEFT_THERE, WHOLE, LEFT_THERE],
         scratch_shapes=[
             pltpu.VMEM((HALO, 128), jnp.bfloat16),
@@ -452,28 +452,20 @@
     return lax.ppermute(value, "src", [(i, i ^ mask) for i in range(SRC_DEVICES)])
 
 
-def pair_sources(src_shift, src_weight):
-    shifts = jnp.concatenate([src_shift, swap_src(src_shift, 4)], axis=0)
-    weights = jnp.concatenate([src_weight, swap_src(src_weight, 4)], axis=0)
-    return jnp.concatenate([shifts, weights[:, None]], axis=1)
-
-
-def all_sources(pair):
-    return jnp.concatenate([pair] + [swap_src(pair, mask) for mask in (1, 2, 3)], axis=0)
-
-
 def per_device(mask_tiles, slot_pos, src_shift, src_weight, pupil_phase, target):
-    pair = pair_sources(src_shift, src_weight)
     col = jnp.asarray(COL)
     row_table = lax.optimization_barrier(jnp.asarray(ROW_F32))
     tile = mask_tiles[0]
-    got = lax.all_to_all(make_rims(slot_pos, tile, col), "tile", 0, 0, tiled=True)
-    pair, col_after, small, grids = lax.optimization_barrier((pair, col, jnp.asarray(SMALL), jnp.asarray(GRIDS)))
-    ints = all_sources(pair)
-    own = own_moments(tile, col_after, row_table)
-    flipped, right_t = flip_tables(small, grids)
+    sent, ints = make_rims(slot_pos, src_shift, src_weight, tile, col)
+    ints = ints + swap_src(ints, 4)
+    got = lax.all_to_all(sent, "tile", 0, 0, tiled=True)
+    ints = ints + swap_src(ints, 1) + swap_src(ints, 2) + swap_src(ints, 3)
+    small = jnp.asarray(SMALL)
+    grids = jnp.asarray(GRIDS)
+    own = own_moments(tile, col, row_table)
+    flipped = flip_tables(grids)
     resist, back, sent = make_fields(
-        slot_pos, ints, got, own, pupil_tables(pupil_phase), small, right_t, row_table, grids, flipped, target[0]
+        slot_pos, ints, got, own, pupil_tables(pupil_phase), small, row_table, grids, flipped, target[0]
     )
     cores = [[2 * chip + core for chip in range(TILES // 2)] for core in range(2)]
     got = lax.all_to_all(sent, "tile", 0, 0, tiled=True, axis_index_groups=cores)

time: 65.5 us -> 67.5 us (1.031)
  starting transfers between devices: 24.8 us -> 28.7 us
  matrix products: 3.49 us -> 1.85 us
  local copies, waits for them, and re-layouts: 0.9 us -> 0.05 us
  waiting for transfers between devices: 16.2 us -> 16.9 us
    ppermute x5 -> x4, waiting for transfers between devices: 0.01 us -> 7.95 us  [swap_src(): lax.ppermute(value, 'src', [(i, i ^ mask) for i in range(SRC_DEVICES)])]
    all_to_all x1, waiting for transfers between devices: 6.07 us -> 0.01 us  [per_device(): got = lax.all_to_all(sent, 'tile', 0, 0, tiled=True)]
    ppermute x5 -> x4, starting transfers between devices: 11.3 us -> 7.71 us  [swap_src(): lax.ppermute(value, 'src', [(i, i ^ mask) for i in range(SRC_DEVICES)])]
    all_to_all x1, starting transfers between devices: 3.57 us -> 6.86 us  [per_device(): lax.all_to_all(sent, 'tile', 0, 0, tiled=True, axis_index_groups=cores)]
    ppermute x1, starting transfers between devices: 1.59 us -> 3.93 us  [per_device(): other = lax.ppermute(got, 'tile', [(i, i ^ 1) for i in range(TILES)])]
    all_to_all x1, starting transfers between devices: 8.34 us -> 10.2 us  [per_device(): got = lax.all_to_all(sent, 'tile', 0, 0, tiled=True)]
    dot_general x1, matrix products: 2.48 us -> 0.83 us  [own_moments(): half = jnp.dot(tile, col, preferred_element_type=jnp.float32)]
    all_to_all x1, waiting for transfers between devices: 8.92 us -> 7.82 us  [per_device(): lax.all_to_all(sent, 'tile', 0, 0, tiled=True, axis_index_groups=cores)]
  transfers between devices with their start and end apart: 8 -> 7, of which waited for: 3 -> 4; matrix products, arithmetic and copies ran while one was open for 7% -> 3% of each run, Pallas kernels for 10% -> 5%
where the time goes in v7:
time: 67.5 us; the launch traced here: 67.1 us
  starting transfers between devices  28.7 us (43%)
  Pallas kernels  18.5 us (27%)
  waiting for transfers between devices  16.9 us (25%)
  matrix products  1.85 us (3%)
  between operations  0.83 us (1%)
    pallas_call x1, Pallas kernels, make_fields(): pl.pallas_call(fields_kernel, out_shape=(jax.ShapeDtypeStruct((ROWS, TILE...  10.6 us
    all_to_all x1, starting transfers between devices, per_device(): got = lax.all_to_all(sent, 'tile', 0, 0, tiled=True)  10.2 us
    ppermute x4, waiting for transfers between devices, swap_src(): lax.ppermute(value, 'src', [(i, i ^ mask) for i in range(SRC_DEVICES)])  7.95 us
    all_to_all x1, waiting for transfers between devices, per_device(): lax.all_to_all(sent, 'tile', 0, 0, tiled=True, axis_index_groups=cores)  7.82 us
    ppermute x4, starting transfers between devices, swap_src(): lax.ppermute(value, 'src', [(i, i ^ mask) for i in range(SRC_DEVICES)])  7.71 us
    all_to_all x1, starting transfers between devices, per_device(): lax.all_to_all(sent, 'tile', 0, 0, tiled=True, axis_index_groups=cores)  6.86 us
    ppermute x1, starting transfers between devices, per_device(): other = lax.ppermute(got, 'tile', [(i, i ^ 1) for i in range(TILES)])  3.93 us
    pallas_call x1, Pallas kernels, make_rims(): pl.pallas_call(rims_kernel, out_shape=(jax.ShapeDtypeStruct((TILES, HALO,...  2.76 us
  transfers between devices with their start and end apart: 7, of which 4 were waited for; matrix products, arithmetic and copies ran while one was open for 3% of the time, Pallas kernels for 5%

profile of v7, /device:TPU:1, one launch (start us, length us, event | category | flops | bytes accessed | tf_op | source)
XLA Modules:
  0.0 67.1 jit_solution(6762270102118024752)
XLA Ops:
  0.6 0.0 copy-start
  0.6 0.0 copy-start.7
  0.7 0.0 copy-start.4
  0.7 0.0 copy-start.5
  0.7 2.8 %rims.1 = (bf16[32,64,128]{2,1,0:T(8,128)(2,1)}, s32[16,128]{1,0:T(8,128)}) custom-call(s32[32]{0:T(128)} %slot_ref.5, s32[2,2]{1,0:T(2,128)} %shift_ref.1, s32[2]{0:T(128)} %weight_ref.1, bf16[1024,1024]{1,0:T(8,128)(2,1)} %bitcast.12, bf16[1024,128]{1,0:T(8,128)(2,1)} %constant.14.clone.col_hbm.col_ref), custom_call_target="tpu_custom_call" | custom-call | tf_op jit(solution)/shard_map/rims/pallas_call | solution.py:175
  3.4 0.0 copy-start.1
  3.5 10.2 %all-to-all-start = ((bf16[32,64,128]{2,1,0:T(8,128)(2,1)}), bf16[32,64,128]{2,1,0:T(8,128)(2,1)S(1)}, u32[]{:S(2)}, u32[]{:S(2)}) async-start(bf16[32,64,128]{2,1,0:T(8,128)(2,1)} %get-tuple-element.12), calls=%async_computation | async-start | bytes 1048576 | tf_op jit(solution)/shard_map/all_to_all | solution.py:461
  13.6 4.3 %collective-permute-start = (s32[16,128]{1,0:T(8,128)}, s32[16,128]{1,0:T(8,128)S(1)}, u32[]{:S(2)}, u32[]{:S(2)}) collective-permute-start(s32[16,128]{1,0:T(8,128)} %get-tuple-element.11), channel_id=1, source_target_pairs={{0,128},{32,160},{64,192},{96,224},{128,0},{160,32},{192,64},{224,... | collective-permute-start | bytes 24584 | tf_op jit(solution)/shard_map/ppermute | solution.py:452
  17.9 0.0 copy-done.7
  17.9 0.0 copy-done.5
  17.9 0.2 select_multiply_fusion.1
  18.1 0.0 copy-done
  18.1 0.0 copy-done.4
  18.2 0.0 copy-start.6
  18.2 0.8 %fusion.2 = f32[128,1024]{1,0:T(8,128)S(1)} fusion(bf16[1024,128]{1,0:T(8,128)(2,1)S(1)} %copy-done, bf16[1,1024,1024]{2,1,0:T(8,128)(2,1)S(1)} %copy-done.4), kind=kOutput, calls=%fused_computation.8 | convolution fusion | flops 268435456 | bytes 2883584 | tf_op jit(solution)/shard_map/dot_general | solution.py:444
  19.0 0.0 copy-done.1
  19.0 0.0 copy-start.2
  19.0 0.0 copy-start.3
  19.0 1.0 %fusion.own_ref = f32[128,128]{1,0:T(8,128)S(1)} fusion(f32[128,1024]{1,0:T(8,128)S(1)} %fusion.2, f32[1152,128]{1,0:T(8,128)S(1)} %copy-done.1), kind=kOutput, calls=%fused_computation | convolution fusion | flops 201326592 | bytes 1114112 | tf_op jit(solution)/shard_map/dot_general | solution.py:446
  20.1 0.1 maximum_bitcast_fusion
  20.2 7.2 %collective-permute-done = s32[16,128]{1,0:T(8,128)S(1)} collective-permute-done((s32[16,128]{1,0:T(8,128)}, s32[16,128]{1,0:T(8,128)S(1)}, u32[]{:S(2)}, u32[]{:S(2)}) %collective-permute-start) | collective-permute-done | bytes 8224 | tf_op jit(solution)/shard_map/ppermute | solution.py:452
  27.4 0.0 copy-done.6
  27.4 2.7 %collective-permute-start.3 = (s32[16,128]{1,0:T(8,128)S(1)}, s32[16,128]{1,0:T(8,128)S(1)}, u32[]{:S(2)}, u32[]{:S(2)}) collective-permute-start(s32[16,128]{1,0:T(8,128)S(1)} %add.12), channel_id=1, source_target_pairs={{0,96},{32,64},{64,32},{96,0},{128,224},{160,192},{192,160},{224,1... | collective-permute-start | bytes 24584 | tf_op jit(solution)/shard_map/ppermute | solution.py:452
  30.1 0.3 collective-permute-start.2
  30.5 0.3 collective-permute-start.1
  30.8 2.6 %prep.1.flipped_hbm = bf16[512,1024]{1,0:T(8,128)(2,1)} custom-call(bf16[1024,512]{1,0:T(8,128)(2,1)} %constant.17.clone.grids_hbm), custom_call_target="tpu_custom_call" | custom-call | tf_op jit(solution)/shard_map/prep/pallas_call | solution.py:207
  33.4 0.0 collective-permute-done.3
  33.4 0.7 %collective-permute-done.2 = s32[16,128]{1,0:T(8,128)S(1)} collective-permute-done((s32[16,128]{1,0:T(8,128)S(1)}, s32[16,128]{1,0:T(8,128)S(1)}, u32[]{:S(2)}, u32[]{:S(2)}) %collective-permute-start.2) | collective-permute-done | bytes 8224 | tf_op jit(solution)/shard_map/ppermute | solution.py:452
  34.1 0.0 collective-permute-done.1
  34.1 0.0 all-to-all-done.got_ref
  34.1 0.0 copy-done.2
  34.1 0.0 copy-done.3
  34.2 10.6 %fields.1 = (f32[128,1024]{1,0:T(8,128)}, f32[128,128]{1,0:T(8,128)S(1)}, bf16[16,64,128]{2,1,0:T(8,128)(2,1)}) custom-call(s32[32]{0:T(128)S(1)} %copy-done.3, s32[16,128]{1,0:T(8,128)S(1)} %add_add_fusion.ints_ref, bf16[32,64,128]{2,1,0:T(8,128)(2,1)S(1)} %all-to-all-done.got_ref, f32[128,128]{1,0:T(8,128)S(1)} %fusion.own_ref, ...), custom_call_target="tpu_custom_call" | custom-call | tf_op jit(solution)/shard_map/fields/pallas_call | solution.py:350
  44.7 6.9 %all-to-all-start.1 = ((bf16[16,64,128]{2,1,0:T(8,128)(2,1)}), bf16[16,64,128]{2,1,0:T(8,128)(2,1)S(1)}, u32[]{:S(2)}, u32[]{:S(2)}) async-start(bf16[16,64,128]{2,1,0:T(8,128)(2,1)} %get-tuple-element.14), calls=%async_computation.1 | async-start | bytes 524288 | tf_op jit(solution)/shard_map/all_to_all | solution.py:471
  51.6 1.1 %steps.1 = (f32[128,1024]{1,0:T(8,128)}, f32[64,1024]{1,0:T(8,128)S(1)}) custom-call(f32[128,128]{1,0:T(8,128)S(1)} %get-tuple-element.15.back_ref, bf16[1024,128]{1,0:T(8,128)(2,1)S(1)} %copy-done), custom_call_target="tpu_custom_call" | custom-call | tf_op jit(solution)/shard_map/steps/pallas_call | solution.py:389
  52.7 7.8 %all-to-all-done.1.got_ref = bf16[16,64,128]{2,1,0:T(8,128)(2,1)S(1)} async-done(((bf16[16,64,128]{2,1,0:T(8,128)(2,1)}), bf16[16,64,128]{2,1,0:T(8,128)(2,1)S(1)}, u32[]{:S(2)}, u32[]{:S(2)}) %all-to-all-start.1) | async-done | bytes 262176 | tf_op jit(solution)/shard_map/all_to_all | solution.py:471
  60.5 3.9 %collective-permute-start.4 = (bf16[16,64,128]{2,1,0:T(8,128)(2,1)S(1)}, bf16[16,64,128]{2,1,0:T(8,128)(2,1)S(1)}, u32[]{:S(2)}, u32[]{:S(2)}) collective-permute-start(bf16[16,64,128]{2,1,0:T(8,128)(2,1)S(1)} %all-to-all-done.1.got_ref), channel_id=1, source_target_pairs={{0,1},{1,0},{2,3},{3,2},{4,5},{5,4},{6,7},{7,6},{8,9},{9,8},{10,11... | collective-permute-start | bytes 786440 | tf_op jit(solution)/shard_map/ppermute | solution.py:474
  64.5 1.2 %collective-permute-done.4.other_ref = bf16[16,64,128]{2,1,0:T(8,128)(2,1)S(1)} collective-permute-done((bf16[16,64,128]{2,1,0:T(8,128)(2,1)S(1)}, bf16[16,64,128]{2,1,0:T(8,128)(2,1)S(1)}, u32[]{:S(2)}, u32[]{:S(2)}) %collective-permute-start.4) | collective-permute-done | bytes 262176 | tf_op jit(solution)/shard_map/ppermute | solution.py:474
  65.6 1.5 %edge.1 = f32[128,1024]{1,0:T(8,128)} custom-call(s32[32]{0:T(128)S(1)} %copy-done.3, bf16[16,64,128]{2,1,0:T(8,128)(2,1)S(1)} %all-to-all-done.1.got_ref, bf16[16,64,128]{2,1,0:T(8,128)(2,1)S(1)} %collective-permute-done.4.other_ref, f32[64,1024]{1,0:T(8,128)S(1)} %get-tuple-element.18.edge_ref, ...), custom_call_target="tpu_custom_call", output_to_operand_aliasing={{}: (5, {})} | custom-call | tf_op jit(solution)/shard_map/edge/pallas_call | solution.py:423
  (3 shorter events, 0.0 us)
Async XLA Ops:
  0.6 17.5 %copy-start = (bf16[1024,128]{1,0:T(8,128)(2,1)S(1)}, bf16[1024,128]{1,0:T(8,128)(2,1)}, u32[]{:S(2)}) copy-start(bf16[1024,128]{1,0:T(8,128)(2,1)} %constant.14.clone.col_hbm.col_ref) | copy-start | bytes 786436
  0.6 17.3 %copy-start.7 = (pred[64,64]{1,0:T(32,128)(4,1)S(1)}, pred[64,64]{1,0:T(32,128)(4,1)}, u32[]{:S(2)}) copy-start(pred[64,64]{1,0:T(32,128)(4,1)} %constant.18.clone) | copy-start | bytes 12292
  0.7 17.5 %copy-start.4 = (bf16[1,1024,1024]{2,1,0:T(8,128)(2,1)S(1)}, bf16[1,1024,1024]{2,1,0:T(8,128)(2,1)}, u32[]{:S(2)}) copy-start(bf16[1,1024,1024]{2,1,0:T(8,128)(2,1)} %param.11) | copy-start | bytes 6291460
  0.7 17.3 %copy-start.5 = (f32[128,128]{1,0:T(8,128)S(1)}, f32[128,128]{1,0:T(8,128)}, u32[]{:S(2)}) copy-start(f32[128,128]{1,0:T(8,128)} %param.15) | copy-start | bytes 196612
  3.4 15.6 %copy-start.1 = (f32[1152,128]{1,0:T(8,128)S(1)}, f32[1152,128]{1,0:T(8,128)}, u32[]{:S(2)}) copy-start(f32[1152,128]{1,0:T(8,128)} %constant.15.clone.row_ref) | copy-start | bytes 1769476
  3.5 30.7 %all-to-all-start = ((bf16[32,64,128]{2,1,0:T(8,128)(2,1)}), bf16[32,64,128]{2,1,0:T(8,128)(2,1)S(1)}, u32[]{:S(2)}, u32[]{:S(2)}) async-start(bf16[32,64,128]{2,1,0:T(8,128)(2,1)} %get-tuple-element.12), calls=%async_computation | async-start | bytes 1048576 | tf_op jit(solution)/shard_map/all_to_all | solution.py:461
  13.6 13.7 %collective-permute-start = (s32[16,128]{1,0:T(8,128)}, s32[16,128]{1,0:T(8,128)S(1)}, u32[]{:S(2)}, u32[]{:S(2)}) collective-permute-start(s32[16,128]{1,0:T(8,128)} %get-tuple-element.11), channel_id=1, source_target_pairs={{0,128},{32,160},{64,192},{96,224},{128,0},{160,32},{192,64},{224,... | collective-permute-start | bytes 24584 | tf_op jit(solution)/shard_map/ppermute | solution.py:452
  18.2 9.2 %copy-start.6 = (s32[16,128]{1,0:T(8,128)S(1)}, s32[16,128]{1,0:T(8,128)}, u32[]{:S(2)}) copy-start(s32[16,128]{1,0:T(8,128)} %get-tuple-element.11) | copy-start | bytes 24580
  19.0 15.1 %copy-start.2 = (bf16[256,1280]{1,0:T(8,128)(2,1)S(1)}, bf16[256,1280]{1,0:T(8,128)(2,1)}, u32[]{:S(2)}) copy-start(bf16[256,1280]{1,0:T(8,128)(2,1)} %constant.16.clone.small_ref) | copy-start | bytes 1966084
  19.0 15.1 %copy-start.3 = (s32[32]{0:T(128)S(1)}, s32[32]{0:T(128)}, u32[]{:S(2)}) copy-start(s32[32]{0:T(128)} %slot_ref.5) | copy-start | bytes 388
  27.4 6.0 %collective-permute-start.3 = (s32[16,128]{1,0:T(8,128)S(1)}, s32[16,128]{1,0:T(8,128)S(1)}, u32[]{:S(2)}, u32[]{:S(2)}) collective-permute-start(s32[16,128]{1,0:T(8,128)S(1)} %add.12), channel_id=1, source_target_pairs={{0,96},{32,64},{64,32},{96,0},{128,224},{160,192},{192,160},{224,1... | collective-permute-start | bytes 24584 | tf_op jit(solution)/shard_map/ppermute | solution.py:452
  30.1 4.0 %collective-permute-start.2 = (s32[16,128]{1,0:T(8,128)S(1)}, s32[16,128]{1,0:T(8,128)S(1)}, u32[]{:S(2)}, u32[]{:S(2)}) collective-permute-start(s32[16,128]{1,0:T(8,128)S(1)} %add.12), channel_id=1, source_target_pairs={{0,64},{32,96},{64,0},{96,32},{128,192},{160,224},{192,128},{224,1... | collective-permute-start | bytes 24584 | tf_op jit(solution)/shard_map/ppermute | solution.py:452
  30.5 3.7 %collective-permute-start.1 = (s32[16,128]{1,0:T(8,128)S(1)}, s32[16,128]{1,0:T(8,128)S(1)}, u32[]{:S(2)}, u32[]{:S(2)}) collective-permute-start(s32[16,128]{1,0:T(8,128)S(1)} %add.12), channel_id=1, source_target_pairs={{0,32},{32,0},{64,96},{96,64},{128,160},{160,128},{192,224},{224,1... | collective-permute-start | bytes 24584 | tf_op jit(solution)/shard_map/ppermute | solution.py:452
  44.7 15.8 %all-to-all-start.1 = ((bf16[16,64,128]{2,1,0:T(8,128)(2,1)}), bf16[16,64,128]{2,1,0:T(8,128)(2,1)S(1)}, u32[]{:S(2)}, u32[]{:S(2)}) async-start(bf16[16,64,128]{2,1,0:T(8,128)(2,1)} %get-tuple-element.14), calls=%async_computation.1 | async-start | bytes 524288 | tf_op jit(solution)/shard_map/all_to_all | solution.py:471
  60.5 5.1 %collective-permute-start.4 = (bf16[16,64,128]{2,1,0:T(8,128)(2,1)S(1)}, bf16[16,64,128]{2,1,0:T(8,128)(2,1)S(1)}, u32[]{:S(2)}, u32[]{:S(2)}) collective-permute-start(bf16[16,64,128]{2,1,0:T(8,128)(2,1)S(1)} %all-to-all-done.1.got_ref), channel_id=1, source_target_pairs={{0,1},{1,0},{2,3},{3,2},{4,5},{5,4},{6,7},{7,6},{8,9},{9,8},{10,11... | collective-permute-start | bytes 786440 | tf_op jit(solution)/shard_map/ppermute | solution.py:474

commit v8 on v6

--- a/solution.py
+++ b/solution.py
@@ -123,6 +123,16 @@
     return my_slot, lax.axis_index("src"), above, below
 
 
+def pack_kernel(shift_ref, weight_ref, ints_ref):
+    row = lax.broadcasted_iota(jnp.int32, ints_ref.shape, 0) - 2 * lax.axis_index("src")
+    lane = lax.broadcasted_iota(jnp.int32, ints_ref.shape, 1)
+    table = jnp.zeros(ints_ref.shape, jnp.int32)
+    for source in range(2):
+        for place, value in enumerate((shift_ref[source, 0], shift_ref[source, 1], weight_ref[source])):
+            table = jnp.where((row == source) & (lane == place), value, table)
+    ints_ref[...] = table
+
+
 def rims_kernel(slot_ref, tile_hbm, col_hbm, sent_hbm, rows_ref, col_ref, rims_ref, sems):
     copies = [
         pltpu.make_async_copy(col_hbm, col_ref, sems.at[0]),
@@ -157,6 +167,18 @@
 MIB = 1024 * 1024
 ALL_VMEM = 63_000_000
 FIELDS_VMEM = 54_000_000
+
+
+def pack_sources(src_shift, src_weight):
+    return pl.pallas_call(
+        pack_kernel,
+        out_shape=jax.ShapeDtypeStruct((SOURCES, 128), jnp.int32),
+        in_specs=[SCALARS, SCALARS],
+        out_specs=WHOLE,
+        compiler_params=pltpu.CompilerParams(vmem_limit_bytes=4 * MIB),
+        interpret=INTERPRET,
+        name="pack",
+    )(src_shift, src_weight)
 
 
 def make_rims(slot_pos, tile, col):
@@ -452,24 +474,15 @@
     return lax.ppermute(value, "src", [(i, i ^ mask) for i in range(SRC_DEVICES)])
 
 
-def pair_sources(src_shift, src_weight):
-    shifts = jnp.concatenate([src_shift, swap_src(src_shift, 4)], axis=0)
-    weights = jnp.concatenate([src_weight, swap_src(src_weight, 4)], axis=0)
-    return jnp.concatenate([shifts, weights[:, None]], axis=1)
-
-
-def all_sources(pair):
-    return jnp.concatenate([pair] + [swap_src(pair, mask) for mask in (1, 2, 3)], axis=0)
-
-
 def per_device(mask_tiles, slot_pos, src_shift, src_weight, pupil_phase, target):
-    pair = pair_sources(src_shift, src_weight)
+    ints = pack_sources(src_shift, src_weight)
+    ints = ints + swap_src(ints, 4)
     col = jnp.asarray(COL)
     row_table = lax.optimization_barrier(jnp.asarray(ROW_F32))
     tile = mask_tiles[0]
     got = lax.all_to_all(make_rims(slot_pos, tile, col), "tile", 0, 0, tiled=True)
-    pair, col_after, small, grids = lax.optimization_barrier((pair, col, jnp.asarray(SMALL), jnp.asarray(GRIDS)))
-    ints = all_sources(pair)
+    ints, col_after, small, grids = lax.optimization_barrier((ints, col, jnp.asarray(SMALL), jnp.asarray(GRIDS)))
+    ints = ints + swap_src(ints, 1) + swap_src(ints, 2) + swap_src(ints, 3)
     own = own_moments(tile, col_after, row_table)
     flipped, right_t = flip_tables(small, grids)
     resist, back, sent = make_fields(

time: 65.5 us -> 65.9 us (level)
  matrix products: 3.49 us -> 1.82 us
  starting transfers between devices: 24.8 us -> 23.4 us
  local copies, waits for them, and re-layouts: 0.9 us -> 2.26 us
  waiting for transfers between devices: 16.2 us -> 17.3 us
    dot_general x1, matrix products: 2.48 us -> 0.82 us  [own_moments(): half = jnp.dot(tile, col, preferred_element_type=jnp.float32)]
    unnamed x17 -> x16, local copies, waits for them, and re-layouts: 0.81 us -> 2.26 us
    all_to_all x1, starting transfers between devices: 8.34 us -> 6.92 us  [per_device(): lax.all_to_all(make_rims(slot_pos, tile, col), 'tile', 0, 0, tiled=True)]
    all_to_all x1, waiting for transfers between devices: 6.07 us -> 7.23 us  [per_device(): lax.all_to_all(make_rims(slot_pos, tile, col), 'tile', 0, 0, tiled=True)]
    mul x1, other arithmetic: 0.2 us -> 1 us  [pupil_tables(): real = jnp.where(DISC, jnp.cos(window), 0.0) * SCALE]
    ppermute x5 -> x4, starting transfers between devices: 11.3 us -> 11.3 us  [swap_src(): lax.ppermute(value, 'src', [(i, i ^ mask) for i in range(SRC_DEVICES)])]
  transfers between devices with their start and end apart: 8 -> 7, of which waited for: 3 -> 3; matrix products, arithmetic and copies ran while one was open for 7% -> 4% of each run, Pallas kernels for 10% -> 10%
where the time goes in v8:
time: 65.9 us; the launch traced here: 65.4 us
  starting transfers between devices  23.4 us (36%)
  Pallas kernels  18.7 us (28%)
  waiting for transfers between devices  17.3 us (26%)
  local copies, waits for them, and re-layouts  2.26 us (3%)
  matrix products  1.82 us (3%)
  other arithmetic  1.1 us (2%)
  between operations  0.82 us (1%)
    ppermute x4, starting transfers between devices, swap_src(): lax.ppermute(value, 'src', [(i, i ^ mask) for i in range(SRC_DEVICES)])  11.3 us
    pallas_call x1, Pallas kernels, make_fields(): pl.pallas_call(fields_kernel, out_shape=(jax.ShapeDtypeStruct((ROWS, TILE...  10.2 us
    all_to_all x1, waiting for transfers between devices, per_device(): lax.all_to_all(sent, 'tile', 0, 0, tiled=True, axis_index_groups=cores)  8.92 us
    all_to_all x1, waiting for transfers between devices, per_device(): lax.all_to_all(make_rims(slot_pos, tile, col), 'tile', 0, 0, tiled=True)  7.23 us
    all_to_all x1, starting transfers between devices, per_device(): lax.all_to_all(make_rims(slot_pos, tile, col), 'tile', 0, 0, tiled=True)  6.92 us
    all_to_all x1, starting transfers between devices, per_device(): lax.all_to_all(sent, 'tile', 0, 0, tiled=True, axis_index_groups=cores)  3.57 us
    pallas_call x1, Pallas kernels, make_rims(): pl.pallas_call(rims_kernel, out_shape=jax.ShapeDtypeStruct((TILES, HALO,...  2.71 us
    pallas_call x1, Pallas kernels, flip_tables(): pl.pallas_call(prep_kernel, out_shape=(jax.ShapeDtypeStruct(GRIDS.shape[:...  2.61 us
  transfers between devices with their start and end apart: 7, of which 3 were waited for; matrix products, arithmetic and copies ran while one was open for 4% of the time, Pallas kernels for 10%

profile of v8, /device:TPU:1, one launch (start us, length us, event | category | flops | bytes accessed | tf_op | source)
XLA Modules:
  0.0 65.4 jit_solution(3131286976795424972)
XLA Ops:
  0.6 0.0 copy-start.5
  0.6 0.7 %copy-done.5 = s32[2,2]{1,0:T(2,128)S(1)} copy-done((s32[2,2]{1,0:T(2,128)S(1)}, s32[2,2]{1,0:T(2,128)}, u32[]{:S(2)}) %copy-start.5) | copy-done | bytes 40
  1.3 0.0 copy-start.6
  1.3 0.7 copy-done.6
  2.0 0.6 pack.1
  2.5 7.8 %collective-permute-start = (s32[16,128]{1,0:T(8,128)S(1)}, s32[16,128]{1,0:T(8,128)S(1)}, u32[]{:S(2)}, u32[]{:S(2)}) collective-permute-start(s32[16,128]{1,0:T(8,128)S(1)} %pack.1), channel_id=1, source_target_pairs={{0,128},{32,160},{64,192},{96,224},{128,0},{160,32},{192,64},{224,... | collective-permute-start | bytes 24584 | tf_op jit(solution)/shard_map/ppermute | solution.py:474
  10.4 0.0 copy-start
  10.4 0.0 copy-start.7
  10.4 2.7 %rims.1 = bf16[32,64,128]{2,1,0:T(8,128)(2,1)} custom-call(s32[32]{0:T(128)} %slot_ref.5, bf16[1024,1024]{1,0:T(8,128)(2,1)} %bitcast.12, bf16[1024,128]{1,0:T(8,128)(2,1)} %constant.14.clone.col_hbm.col_ref), custom_call_target="tpu_custom_call" | custom-call | tf_op jit(solution)/shard_map/rims/pallas_call | solution.py:185
  13.1 0.0 copy-start.2
  13.1 6.9 %all-to-all-start = ((bf16[32,64,128]{2,1,0:T(8,128)(2,1)}), bf16[32,64,128]{2,1,0:T(8,128)(2,1)S(1)}, u32[]{:S(2)}, u32[]{:S(2)}) async-start(bf16[32,64,128]{2,1,0:T(8,128)(2,1)} %rims.1), calls=%async_computation | async-start | bytes 1048576 | tf_op jit(solution)/shard_map/all_to_all | solution.py:483
  20.0 1.0 %select_multiply_fusion.1 = (f32[64,64]{1,0:T(8,128)S(1)}, f32[64,64]{1,0:T(8,128)S(1)}, f32[64,64]{1,0:T(8,128)S(1)}) fusion(pred[64,64]{1,0:T(32,128)(4,1)} %constant.18.clone, f32[128,128]{1,0:T(8,128)} %param.15), kind=kLoop, calls=%fused_computation.6 | loop fusion | flops 20480 | bytes 69632 | tf_op jit(solution)/shard_map/mul | solution.py:460
  21.0 0.1 maximum_bitcast_fusion
  21.1 0.0 collective-permute-done
  21.2 2.8 %collective-permute-start.3 = (s32[16,128]{1,0:T(8,128)S(1)}, s32[16,128]{1,0:T(8,128)S(1)}, u32[]{:S(2)}, u32[]{:S(2)}) collective-permute-start(s32[16,128]{1,0:T(8,128)S(1)} %add.12), channel_id=1, source_target_pairs={{0,96},{32,64},{64,32},{96,0},{128,224},{160,192},{192,160},{224,1... | collective-permute-start | bytes 24584 | tf_op jit(solution)/shard_map/ppermute | solution.py:474
  24.0 0.4 collective-permute-start.2
  24.3 0.3 collective-permute-start.1
  24.7 0.0 copy-done
  24.7 0.0 copy-done.7
  24.7 0.8 %fusion.2 = f32[128,1024]{1,0:T(8,128)S(1)} fusion(bf16[1024,128]{1,0:T(8,128)(2,1)S(1)} %copy-done, bf16[1,1024,1024]{2,1,0:T(8,128)(2,1)S(1)} %copy-done.7), kind=kOutput, calls=%fused_computation.8 | convolution fusion | flops 268435456 | bytes 2883584 | tf_op jit(solution)/shard_map/dot_general | solution.py:466
  25.5 0.0 copy-done.2
  25.5 0.0 copy-start.1
  25.5 0.0 copy-start.4
  25.5 1.0 %fusion.own_ref = f32[128,128]{1,0:T(8,128)S(1)} fusion(f32[128,1024]{1,0:T(8,128)S(1)} %fusion.2, f32[1152,128]{1,0:T(8,128)S(1)} %copy-done.2), kind=kOutput, calls=%fused_computation | convolution fusion | flops 201326592 | bytes 1114112 | tf_op jit(solution)/shard_map/dot_general | solution.py:468
  26.5 2.6 %prep.1 = (bf16[512,1024]{1,0:T(8,128)(2,1)}, bf16[256,256]{1,0:T(8,128)(2,1)}) custom-call(bf16[256,1152]{1,0:T(8,128)(2,1)} %constant.16.clone.small_hbm.small_ref, bf16[1024,512]{1,0:T(8,128)(2,1)} %constant.17.clone.grids_hbm), custom_call_target="tpu_custom_call" | custom-call | tf_op jit(solution)/shard_map/prep/pallas_call | solution.py:224
  29.2 0.0 collective-permute-done.3
  29.2 0.0 collective-permute-done.2
  29.2 0.0 collective-permute-done.1
  29.2 7.2 %all-to-all-done.got_ref = bf16[32,64,128]{2,1,0:T(8,128)(2,1)S(1)} async-done(((bf16[32,64,128]{2,1,0:T(8,128)(2,1)}), bf16[32,64,128]{2,1,0:T(8,128)(2,1)S(1)}, u32[]{:S(2)}, u32[]{:S(2)}) %all-to-all-start) | async-done | bytes 524320 | tf_op jit(solution)/shard_map/all_to_all | solution.py:483
  36.4 0.0 copy-done.1
  36.4 0.0 copy-done.4
  36.4 0.0 copy-start.3
  36.4 0.9 %copy-done.3 = bf16[256,256]{1,0:T(8,128)(2,1)S(1)} copy-done((bf16[256,256]{1,0:T(8,128)(2,1)S(1)}, bf16[256,256]{1,0:T(8,128)(2,1)}, u32[]{:S(2)}) %copy-start.3) | copy-done | bytes 131096
  37.3 10.2 %fields.1 = (f32[128,1024]{1,0:T(8,128)}, f32[128,128]{1,0:T(8,128)S(1)}, bf16[16,64,128]{2,1,0:T(8,128)(2,1)}) custom-call(s32[32]{0:T(128)S(1)} %copy-done.4, s32[16,128]{1,0:T(8,128)S(1)} %add_add_fusion.ints_ref, bf16[32,64,128]{2,1,0:T(8,128)(2,1)S(1)} %all-to-all-done.got_ref, f32[128,128]{1,0:T(8,128)S(1)} %fusion.own_ref, ...), custom_call_target="tpu_custom_call" | custom-call | tf_op jit(solution)/shard_map/fields/pallas_call | solution.py:372
  47.6 3.6 %all-to-all-start.1 = ((bf16[16,64,128]{2,1,0:T(8,128)(2,1)}), bf16[16,64,128]{2,1,0:T(8,128)(2,1)S(1)}, u32[]{:S(2)}, u32[]{:S(2)}) async-start(bf16[16,64,128]{2,1,0:T(8,128)(2,1)} %get-tuple-element.22), calls=%async_computation.1 | async-start | bytes 524288 | tf_op jit(solution)/shard_map/all_to_all | solution.py:492
  51.1 1.1 %steps.1 = (f32[128,1024]{1,0:T(8,128)}, f32[64,1024]{1,0:T(8,128)S(1)}) custom-call(f32[128,128]{1,0:T(8,128)S(1)} %get-tuple-element.23.back_ref, bf16[1024,128]{1,0:T(8,128)(2,1)S(1)} %copy-done), custom_call_target="tpu_custom_call" | custom-call | tf_op jit(solution)/shard_map/steps/pallas_call | solution.py:411
  52.2 8.9 %all-to-all-done.1.got_ref = bf16[16,64,128]{2,1,0:T(8,128)(2,1)S(1)} async-done(((bf16[16,64,128]{2,1,0:T(8,128)(2,1)}), bf16[16,64,128]{2,1,0:T(8,128)(2,1)S(1)}, u32[]{:S(2)}, u32[]{:S(2)}) %all-to-all-start.1) | async-done | bytes 262176 | tf_op jit(solution)/shard_map/all_to_all | solution.py:492
  61.2 1.6 %collective-permute-start.4 = (bf16[16,64,128]{2,1,0:T(8,128)(2,1)S(1)}, bf16[16,64,128]{2,1,0:T(8,128)(2,1)S(1)}, u32[]{:S(2)}, u32[]{:S(2)}) collective-permute-start(bf16[16,64,128]{2,1,0:T(8,128)(2,1)S(1)} %all-to-all-done.1.got_ref), channel_id=1, source_target_pairs={{0,1},{1,0},{2,3},{3,2},{4,5},{5,4},{6,7},{7,6},{8,9},{9,8},{10,11... | collective-permute-start | bytes 786440 | tf_op jit(solution)/shard_map/ppermute | solution.py:495
  62.8 1.2 %collective-permute-done.4.other_ref = bf16[16,64,128]{2,1,0:T(8,128)(2,1)S(1)} collective-permute-done((bf16[16,64,128]{2,1,0:T(8,128)(2,1)S(1)}, bf16[16,64,128]{2,1,0:T(8,128)(2,1)S(1)}, u32[]{:S(2)}, u32[]{:S(2)}) %collective-permute-start.4) | collective-permute-done | bytes 262176 | tf_op jit(solution)/shard_map/ppermute | solution.py:495
  63.9 1.5 %edge.1 = f32[128,1024]{1,0:T(8,128)} custom-call(s32[32]{0:T(128)S(1)} %copy-done.4, bf16[16,64,128]{2,1,0:T(8,128)(2,1)S(1)} %all-to-all-done.1.got_ref, bf16[16,64,128]{2,1,0:T(8,128)(2,1)S(1)} %collective-permute-done.4.other_ref, f32[64,1024]{1,0:T(8,128)S(1)} %get-tuple-element.26.edge_ref, ...), custom_call_target="tpu_custom_call", output_to_operand_aliasing={{}: (5, {})} | custom-call | tf_op jit(solution)/shard_map/edge/pallas_call | solution.py:445
  (3 shorter events, 0.0 us)
Async XLA Ops:
  0.6 0.7 %copy-start.5 = (s32[2,2]{1,0:T(2,128)S(1)}, s32[2,2]{1,0:T(2,128)}, u32[]{:S(2)}) copy-start(s32[2,2]{1,0:T(2,128)} %shift_ref.1) | copy-start | bytes 52
  1.3 0.7 %copy-start.6 = (s32[2]{0:T(128)S(1)}, s32[2]{0:T(128)}, u32[]{:S(2)}) copy-start(s32[2]{0:T(128)} %weight_ref.1) | copy-start | bytes 28
  2.5 18.6 %collective-permute-start = (s32[16,128]{1,0:T(8,128)S(1)}, s32[16,128]{1,0:T(8,128)S(1)}, u32[]{:S(2)}, u32[]{:S(2)}) collective-permute-start(s32[16,128]{1,0:T(8,128)S(1)} %pack.1), channel_id=1, source_target_pairs={{0,128},{32,160},{64,192},{96,224},{128,0},{160,32},{192,64},{224,... | collective-permute-start | bytes 24584 | tf_op jit(solution)/shard_map/ppermute | solution.py:474
  10.4 14.3 %copy-start = (bf16[1024,128]{1,0:T(8,128)(2,1)S(1)}, bf16[1024,128]{1,0:T(8,128)(2,1)}, u32[]{:S(2)}) copy-start(bf16[1024,128]{1,0:T(8,128)(2,1)} %constant.14.clone.col_hbm.col_ref) | copy-start | bytes 786436
  10.4 14.3 %copy-start.7 = (bf16[1,1024,1024]{2,1,0:T(8,128)(2,1)S(1)}, bf16[1,1024,1024]{2,1,0:T(8,128)(2,1)}, u32[]{:S(2)}) copy-start(bf16[1,1024,1024]{2,1,0:T(8,128)(2,1)} %param.11) | copy-start | bytes 6291460
  13.1 12.4 %copy-start.2 = (f32[1152,128]{1,0:T(8,128)S(1)}, f32[1152,128]{1,0:T(8,128)}, u32[]{:S(2)}) copy-start(f32[1152,128]{1,0:T(8,128)} %constant.15.clone.row_ref) | copy-start | bytes 1769476
  13.1 23.3 %all-to-all-start = ((bf16[32,64,128]{2,1,0:T(8,128)(2,1)}), bf16[32,64,128]{2,1,0:T(8,128)(2,1)S(1)}, u32[]{:S(2)}, u32[]{:S(2)}) async-start(bf16[32,64,128]{2,1,0:T(8,128)(2,1)} %rims.1), calls=%async_computation | async-start | bytes 1048576 | tf_op jit(solution)/shard_map/all_to_all | solution.py:483
  21.2 8.0 %collective-permute-start.3 = (s32[16,128]{1,0:T(8,128)S(1)}, s32[16,128]{1,0:T(8,128)S(1)}, u32[]{:S(2)}, u32[]{:S(2)}) collective-permute-start(s32[16,128]{1,0:T(8,128)S(1)} %add.12), channel_id=1, source_target_pairs={{0,96},{32,64},{64,32},{96,0},{128,224},{160,192},{192,160},{224,1... | collective-permute-start | bytes 24584 | tf_op jit(solution)/shard_map/ppermute | solution.py:474
  24.0 5.2 %collective-permute-start.2 = (s32[16,128]{1,0:T(8,128)S(1)}, s32[16,128]{1,0:T(8,128)S(1)}, u32[]{:S(2)}, u32[]{:S(2)}) collective-permute-start(s32[16,128]{1,0:T(8,128)S(1)} %add.12), channel_id=1, source_target_pairs={{0,64},{32,96},{64,0},{96,32},{128,192},{160,224},{192,128},{224,1... | collective-permute-start | bytes 24584 | tf_op jit(solution)/shard_map/ppermute | solution.py:474
  24.3 4.8 %collective-permute-start.1 = (s32[16,128]{1,0:T(8,128)S(1)}, s32[16,128]{1,0:T(8,128)S(1)}, u32[]{:S(2)}, u32[]{:S(2)}) collective-permute-start(s32[16,128]{1,0:T(8,128)S(1)} %add.12), channel_id=1, source_target_pairs={{0,32},{32,0},{64,96},{96,64},{128,160},{160,128},{192,224},{224,1... | collective-permute-start | bytes 24584 | tf_op jit(solution)/shard_map/ppermute | solution.py:474
  25.5 10.9 %copy-start.1 = (bf16[256,1152]{1,0:T(8,128)(2,1)S(1)}, bf16[256,1152]{1,0:T(8,128)(2,1)}, u32[]{:S(2)}) copy-start(bf16[256,1152]{1,0:T(8,128)(2,1)} %constant.16.clone.small_hbm.small_ref) | copy-start | bytes 1769476
  25.5 10.9 %copy-start.4 = (s32[32]{0:T(128)S(1)}, s32[32]{0:T(128)}, u32[]{:S(2)}) copy-start(s32[32]{0:T(128)} %slot_ref.5) | copy-start | bytes 388
  36.4 0.9 %copy-start.3 = (bf16[256,256]{1,0:T(8,128)(2,1)S(1)}, bf16[256,256]{1,0:T(8,128)(2,1)}, u32[]{:S(2)}) copy-start(bf16[256,256]{1,0:T(8,128)(2,1)} %get-tuple-element.19.right_t_ref) | copy-start | bytes 393220
  47.6 13.6 %all-to-all-start.1 = ((bf16[16,64,128]{2,1,0:T(8,128)(2,1)}), bf16[16,64,128]{2,1,0:T(8,128)(2,1)S(1)}, u32[]{:S(2)}, u32[]{:S(2)}) async-start(bf16[16,64,128]{2,1,0:T(8,128)(2,1)} %get-tuple-element.22), calls=%async_computation.1 | async-start | bytes 524288 | tf_op jit(solution)/shard_map/all_to_all | solution.py:492
  61.2 2.8 %collective-permute-start.4 = (bf16[16,64,128]{2,1,0:T(8,128)(2,1)S(1)}, bf16[16,64,128]{2,1,0:T(8,128)(2,1)S(1)}, u32[]{:S(2)}, u32[]{:S(2)}) collective-permute-start(bf16[16,64,128]{2,1,0:T(8,128)(2,1)S(1)} %all-to-all-done.1.got_ref), channel_id=1, source_target_pairs={{0,1},{1,0},{2,3},{3,2},{4,5},{5,4},{6,7},{7,6},{8,9},{9,8},{10,11... | collective-permute-start | bytes 786440 | tf_op jit(solution)/shard_map/ppermute | solution.py:495
